TPU v7x, 512 devices: a whole 4x8x8 slice. The times are simulated.
512 devices in a mesh: sec: 2 (over x_hi), ax: 16 (over y, core), az: 16 (over x_lo, z).
Axes of the slice: x: 4 (x_hi: 2, x_lo: 2; x = x_hi * 2 + x_lo), y: 8, z: 8, core: 2. Of those that a mesh axis runs over, the one named last changes fastest.
Arguments:
- fields: float32 [2, 4, 256, 256, 256], P('sec', None, 'ax', 'az'), may hold values from -6 to 6
- coefficients: float32 [2, 3, 256, 256, 256], P('sec', None, 'ax', 'az'), may hold values from -0.8 to 0.8, as said below
- old_source: float32 [4, 256, 256, 256], P(None, 'ax', 'az'), may hold values from -6 to 6
- weight_blocks: bfloat16 [16, 16, 8, 128, 128], P('ax', 'az'), may hold values from -0.5 to 0.5
- send_ids: int32 [16, 16, 16, 8], P('ax', 'az'), may hold values from -1 to 511, as said below
- target_ids: int32 [16, 16, 16, 8], P('ax', 'az'), may hold values from 0 to 511
- weight_ids: int32 [16, 16, 16, 8], P('ax', 'az'), may hold values from 0 to 7
Outputs:
- advanced: float32 [2, 4, 256, 256, 256], P('sec', None, 'ax', 'az')
Inputs may be any that keep to these rules, and one draw needn't show every extreme that they name: `send_ids`: entries are -1 (an empty slot) or a block index of the sending device; empty slots follow the live ones in a list. In each sector one cycle, drawn from the seed, receives full lists of 8 live slots from every device of that sector; lists to the other cycles hold fewer than 8 live slots, at most a number that shrinks the farther the cycle lies from that one. A block index appears at most once among one device's lists. `coefficients`: section 0 holds positive viscosities, section 1 the mean flow.
All inputs are finite; a program needn't handle non-finite values.
Results may differ from a plain program's by a relative error of at most 0.0004.
Values may be sent and summed in bfloat16 or wider, within the bound.
No kernel may reach another device: no remote copies, remote signals or barrier semaphores. Data moves between devices by JAX's collectives and lax.ppermute only.
A program may use at most 64 MiB of HBM per device.

v0:
```python
import jax
import jax.numpy as jnp
from jax import lax
from jax.sharding import PartitionSpec as P

LINE = 128


STEP = 0.25


def with_halo(block, sides, width, periodic):
    for axis, dim in sides:
        count = lax.axis_size(axis)
        forward = [(i, i + 1) for i in range(count - 1)]
        if periodic:
            forward.append((count - 1, 0))
        backward = [(target, source) for source, target in forward]
        low = lax.ppermute(
            lax.slice_in_dim(block, block.shape[dim] - width, None, axis=dim), axis, forward
        )
        high = lax.ppermute(lax.slice_in_dim(block, 0, width, axis=dim), axis, backward)
        block = jnp.concatenate([low, block, high], axis=dim)
    return block


def shortened(x):

    def short(part):
        return part.astype(jnp.bfloat16) if part.dtype == jnp.float32 else part

    return jax.tree.map(short, x)


def from_behind(x, axis, by):
    size = lax.axis_size(axis)
    pairs = [(i, i + by) for i in range(size) if 0 <= i + by < size]
    return lax.ppermute(x, axis, pairs)


def neighbours(bordered, direction):
    upper_index = [slice(None), slice(1, -1), slice(1, -1), slice(1, -1)]
    lower_index = [slice(None), slice(1, -1), slice(1, -1), slice(1, -1)]
    upper_index[direction] = slice(2, None)
    lower_index[direction] = slice(None, -2)
    return (bordered[tuple(upper_index)], bordered[tuple(lower_index)])


def advance(padded, factors, source, acoustic):
    bordered = jnp.pad(padded, ((0, 0), (0, 0), (0, 0), (1, 1)))
    middle = bordered[:, 1:-1, 1:-1, 1:-1]
    tendency = jnp.zeros_like(middle)
    couple_first = jnp.zeros_like(middle[0])
    couple_rest = []
    for direction in range(3):
        upper_cells, lower_cells = neighbours(bordered, direction + 1)
        gradient = 0.5 * (upper_cells - lower_cells)
        if acoustic:
            tendency = tendency - factors[direction] * gradient
            couple_first = couple_first + gradient[direction + 1]
            couple_rest.append(gradient[0])
        else:
            tendency = (
                tendency
                - middle[direction] * gradient
                + factors[direction] * (upper_cells - 2.0 * middle + lower_cells)
            )
    if acoustic:
        coupling = jnp.stack([couple_first] + couple_rest)
        tendency = tendency - coupling + source
    return middle + STEP * tendency


def both_sections(padded, factors, source):
    return lax.cond(
        lax.axis_index("sec") == 0,
        lambda: advance(padded, factors, source, False),
        lambda: advance(padded, factors, source, True),
    )


def rim_cells(values):
    beside_all = with_halo(values, (("az", 2),), 1, True)
    beside = with_halo(shortened(values), (("ax", 1),), 1, False).astype(values.dtype)
    lower_edge = jnp.pad(beside[:, :1], ((0, 0), (0, 0), (1, 1), (0, 0)))
    upper_edge = jnp.pad(beside[:, -1:], ((0, 0), (0, 0), (1, 1), (0, 0)))
    return jnp.concatenate([lower_edge, beside_all, upper_edge], axis=1)


def pack_blocks(les_first, send_ids):
    channels = les_first.shape[0]
    block_ids = send_ids.reshape(-1)
    blocks = les_first.astype(jnp.bfloat16).reshape(channels, -1, LINE)
    picked = jnp.take(blocks, jnp.maximum(block_ids, 0), axis=1)
    picked = jnp.where((block_ids >= 0)[None, :, None], picked, jnp.zeros_like(picked))
    return picked.reshape(channels, send_ids.shape[2], send_ids.shape[3], LINE)


def interpolate(received, weight_blocks, target_ids, weight_ids, tile_shape):
    channels = received.shape[0]
    slot_count = received.shape[1] * received.shape[2]
    block_count = tile_shape[1] * tile_shape[2] * tile_shape[3] // LINE
    line_data = received.reshape(channels, slot_count, LINE)
    chosen = jnp.take(weight_blocks.reshape(-1, LINE, LINE), weight_ids.reshape(slot_count), axis=0)
    contribution = jnp.einsum("sij,vsj->svi", chosen, line_data, preferred_element_type=jnp.float32)
    summed = jax.ops.segment_sum(
        contribution.reshape(slot_count, channels * LINE),
        target_ids.reshape(slot_count),
        num_segments=block_count,
    )
    return summed.reshape(block_count, channels, LINE).transpose(1, 0, 2).reshape(tile_shape)


def shards(fields, coefficients, old_source, weight_blocks, send_ids, target_ids, weight_ids):
    current = fields[0]
    factors = coefficients[0]
    stepped_once = both_sections(rim_cells(current), factors, old_source)
    packed = pack_blocks(stepped_once, send_ids)
    arrived = lax.all_to_all(packed, "ax", split_axis=1, concat_axis=1, tiled=True)
    received = from_behind(arrived, "sec", 1)
    new_source = interpolate(received, weight_blocks, target_ids, weight_ids, current.shape)
    stepped_twice = both_sections(rim_cells(stepped_once), factors, new_source)
    return stepped_twice[None]


def solution(mesh):
    return jax.shard_map(
        shards,
        mesh=mesh,
        in_specs=(
            P("sec", None, "ax", "az", None),
            P("sec", None, "ax", "az", None),
            P(None, "ax", "az", None),
            P("ax", "az", None, None, None),
            P("ax", "az", None, None),
            P("ax", "az", None, None),
            P("ax", "az", None, None),
        ),
        out_specs=P("sec", None, "ax", "az", None),
        check_vma=False,
    )
```

profile of v0, /device:TPU:36, one launch (start us, length us, event | category | flops | bytes accessed | tf_op | source)
XLA Modules:
  0.0 85.2 jit_solution(7270315384353833164)
XLA Ops:
  0.0 1.3 %copy-done.2 = f32[1,4,16,16,256]{4,3,2,1,0:T(8,128)S(1)} copy-done((f32[1,4,16,16,256]{4,3,2,1,0:T(8,128)S(1)}, f32[1,4,16,16,256]{4,3,2,1,0:T(8,128)}, u32[]{:S(2)}) %copy-start.2) | copy-done | bytes 1048600
  1.4 1.9 %collective-permute-start = (bf16[4,1,16,256]{3,2,1,0:T(8,128)(2,1)S(1)}, bf16[4,1,16,256]{3,2,1,0:T(8,128)(2,1)S(1)}, u32[]{:S(2)}, u32[]{:S(2)}) collective-permute-start(bf16[4,1,16,256]{3,2,1,0:T(8,128)(2,1)S(1)} %get-tuple-element.116), channel_id=1, source_target_pairs={{0,16},{16,32},{32,48},{48,64},{64,80},{80,96},{96,112},{112,128},... | collective-permute-start | bytes 98312 | tf_op jit(solution)/shard_map/ppermute | solution.py:19
  3.3 4.9 %collective-permute-start.1 = (bf16[4,1,16,256]{3,2,1,0:T(8,128)(2,1)S(1)}, bf16[4,1,16,256]{3,2,1,0:T(8,128)(2,1)S(1)}, u32[]{:S(2)}, u32[]{:S(2)}) collective-permute-start(bf16[4,1,16,256]{3,2,1,0:T(8,128)(2,1)S(1)} %get-tuple-element.117), channel_id=1, source_target_pairs={{16,0},{32,16},{48,32},{64,48},{80,64},{96,80},{112,96},{128,112},... | collective-permute-start | bytes 98312 | tf_op jit(solution)/shard_map/ppermute | solution.py:22
  8.2 0.1 fusion.24
  8.3 4.3 %collective-permute-start.2 = (f32[4,16,1,256]{3,2,1,0:T(1,128)S(1)}, f32[4,16,1,256]{3,2,1,0:T(1,128)S(1)}, u32[]{:S(2)}, u32[]{:S(2)}) collective-permute-start(f32[4,16,1,256]{3,2,1,0:T(1,128)S(1)} %get-tuple-element.108), channel_id=1, source_target_pairs={{0,1},{1,2},{2,3},{3,4},{4,5},{5,6},{6,7},{7,8},{8,9},{9,10},{10,1... | collective-permute-start | bytes 196616 | tf_op jit(solution)/shard_map/ppermute | solution.py:19
  12.6 9.2 %collective-permute-start.3 = (f32[4,16,1,256]{3,2,1,0:T(1,128)S(1)}, f32[4,16,1,256]{3,2,1,0:T(1,128)S(1)}, u32[]{:S(2)}, u32[]{:S(2)}) collective-permute-start(f32[4,16,1,256]{3,2,1,0:T(1,128)S(1)} %get-tuple-element.109), channel_id=1, source_target_pairs={{1,0},{2,1},{3,2},{4,3},{5,4},{6,5},{7,6},{8,7},{9,8},{10,9},{11,1... | collective-permute-start | bytes 196616 | tf_op jit(solution)/shard_map/ppermute | solution.py:22
  21.8 0.1 copy.31
  21.9 0.1 reshape.122
  22.0 0.1 reshape.120
  22.1 0.1 copy.29
  22.2 0.1 reshape.127
  22.3 0.1 copy.27
  22.4 0.1 copy.28
  22.6 0.1 reshape.143
  22.7 3.1 %gather_fusion.1 = bf16[128,128,128]{2,1,0:T(8,128)(2,1)} fusion(bf16[8,128,128]{2,1,0:T(8,128)(2,1)S(1)} %bitcast.72, s32[1024]{0:T(1024)S(1)} %pad_clamp_fusion), kind=kCustom, calls=%fused_computation.1 | custom fusion | bytes 8389120 | tf_op jit(solution)/shard_map/jit(_take)/gather | solution.py:104
  25.8 1.6 %select_maximum_fusion.2 = f32[4,18,18,256]{3,2,1,0:T(8,128)S(1)} fusion(f32[4,1,16,256]{3,2,1,0:T(8,128)S(1)} %get-tuple-element.113, f32[4,1,16,256]{3,2,1,0:T(8,128)S(1)} %get-tuple-element.112, f32[4,16,1,256]{3,2,1,0:T(1,128)S(1)} %collective-permute-done.3, f32[4,16,16,256]{3,2,1,0:T(8,128)} %bitcast.77, f32[4,16,1,256]{3,2,1,0:T(1,128)S(1)} %collective-permute-done.2), kind=kLoop, calls=%fused_computation.68 | loop fusion | flops 2654208 | bytes 2637824 | tf_op jit(solution)/shard_map/concatenate | solution.py:87
  27.4 0.1 copy-done.3
  27.5 1.5 %conditional.2 = (f32[4,18,18,256]{3,2,1,0:T(8,128)S(1)}, f32[4,16,16,256]{3,2,1,0:T(8,128)S(1)}, f32[4,16,16,256]{3,2,1,0:T(8,128)S(1)}, f32[4,16,16,256]{3,2,1,0:T(8,128)S(1)}) conditional(s32[]{:T(128)} %convert_element_type.27, (f32[4,18,18,256]{3,2,1,0:T(8,128)S(1)}, f32[3,16,16,256]{3,2,1,0:T(8,128)S(1)}, ...), branch_computations={%region_0.1_spmd, %region_1.2_spmd} | conditional | flops 5439488 | bytes 17236000 | solution.py:75
  27.6 1.2 %broadcast_multiply_fusion.2 = (f32[4,16,16,256]{3,2,1,0:T(8,128)S(1)}, f32[4,16,16,256]{3,2,1,0:T(8,128)S(1)}, f32[4,16,16,256]{3,2,1,0:T(8,128)S(1)}, f32[4,16,16,256]{3,2,1,0:T(8,128)S(1)}) fusion(f32[4,18,18,256]{3,2,1,0:T(8,128)S(1)} %get-tuple-element.120, f32[16,16,256]{2,1,0:T(8,128)S(1)} %get-tuple-element.73, ...), kind=kLoop, calls=%fused_computation.12 | loop fusion | flops 3407872 | bytes 10944512 | tf_op jit(solution)/shard_map/cond/branch_0_fun/mul | solution.py:57
  28.7 0.2 slice_add_fusion
  28.9 0.1 pad_maximum_fusion
  29.0 1.5 %fusion.22 = (bf16[4,16,16,256]{3,2,1,0:T(8,128)(2,1)S(1)}, f32[4,16,16,256]{3,2,1,0:T(8,128)}) fusion(f32[4,16,16,256]{3,2,1,0:T(8,128)S(1)} %get-tuple-element.52, f32[4,16,16,256]{3,2,1,0:T(8,128)S(1)} %get-tuple-element.50, f32[4,16,16,256]{3,2,1,0:T(8,128)S(1)} %get-tuple-element.51, f32[4,18,18,256]{3,2,1,0:T(8,128)S(1)} %get-tuple-element.49), kind=kLoop, calls=%fused_computation.97 | loop fusion | flops 1310720 | bytes 5767168 | tf_op jit(solution)/shard_map/convert_element_type | solution.py:30
  30.6 0.2 reshape.118
  30.7 0.4 copy.30
  31.2 0.7 gather_fusion
  31.9 1.0 %select_select_fusion = bf16[4,16,8,128]{3,0,2,1:T(4,128)(2,1)} fusion(bf16[4,16,8,128]{3,0,2,1:T(4,128)(2,1)S(1)} %bitcast.80, pred[16,8]{1,0:T(8,128)(4,1)S(1)} %copy.28, pred[16,8]{1,0:T(8,128)(4,1)S(1)} %copy.27), kind=kLoop, calls=%fused_computation.77 | loop fusion | flops 131072 | bytes 262400 | tf_op jit(solution)/shard_map/jit(_where)/select_n | solution.py:95
  32.9 7.2 %all-to-all-start = ((bf16[4,16,8,128]{3,0,2,1:T(4,128)(2,1)}), bf16[4,16,8,128]{3,0,2,1:T(4,128)(2,1)}, u32[]{:S(2)}, u32[]{:S(2)}) async-start(bf16[4,16,8,128]{3,0,2,1:T(4,128)(2,1)} %select_select_fusion), calls=%async_computation | async-start | bytes 262144 | tf_op jit(solution)/shard_map/all_to_all | solution.py:119
  40.1 2.0 %collective-permute-start.4 = (bf16[4,1,16,256]{3,2,1,0:T(8,128)(2,1)S(1)}, bf16[4,1,16,256]{3,2,1,0:T(8,128)(2,1)S(1)}, u32[]{:S(2)}, u32[]{:S(2)}) collective-permute-start(bf16[4,1,16,256]{3,2,1,0:T(8,128)(2,1)S(1)} %get-tuple-element.114), channel_id=1, source_target_pairs={{0,16},{16,32},{32,48},{48,64},{64,80},{80,96},{96,112},{112,128},... | collective-permute-start | bytes 98312 | tf_op jit(solution)/shard_map/ppermute | solution.py:19
  42.2 4.7 %collective-permute-start.5 = (bf16[4,1,16,256]{3,2,1,0:T(8,128)(2,1)S(1)}, bf16[4,1,16,256]{3,2,1,0:T(8,128)(2,1)S(1)}, u32[]{:S(2)}, u32[]{:S(2)}) collective-permute-start(bf16[4,1,16,256]{3,2,1,0:T(8,128)(2,1)S(1)} %get-tuple-element.115), channel_id=1, source_target_pairs={{16,0},{32,16},{48,32},{64,48},{80,64},{96,80},{112,96},{128,112},... | collective-permute-start | bytes 98312 | tf_op jit(solution)/shard_map/ppermute | solution.py:22
  46.9 1.3 %fusion.23 = (f32[4,16,1,256]{3,2,1,0:T(1,128)S(1)}, f32[4,16,1,256]{3,2,1,0:T(1,128)S(1)}) fusion(f32[4,16,16,256]{3,2,1,0:T(8,128)} %get-tuple-element.63), kind=kLoop, calls=%fused_computation.98 | loop fusion | bytes 262144 | tf_op jit(solution)/shard_map/slice | solution.py:20
  48.2 1.9 %collective-permute-start.6 = (f32[4,16,1,256]{3,2,1,0:T(1,128)S(1)}, f32[4,16,1,256]{3,2,1,0:T(1,128)S(1)}, u32[]{:S(2)}, u32[]{:S(2)}) collective-permute-start(f32[4,16,1,256]{3,2,1,0:T(1,128)S(1)} %get-tuple-element.106), channel_id=1, source_target_pairs={{0,1},{1,2},{2,3},{3,4},{4,5},{5,6},{6,7},{7,8},{8,9},{9,10},{10,1... | collective-permute-start | bytes 196616 | tf_op jit(solution)/shard_map/ppermute | solution.py:19
  50.1 6.0 %collective-permute-start.7 = (f32[4,16,1,256]{3,2,1,0:T(1,128)S(1)}, f32[4,16,1,256]{3,2,1,0:T(1,128)S(1)}, u32[]{:S(2)}, u32[]{:S(2)}) collective-permute-start(f32[4,16,1,256]{3,2,1,0:T(1,128)S(1)} %get-tuple-element.107), channel_id=1, source_target_pairs={{1,0},{2,1},{3,2},{4,3},{5,4},{6,5},{7,6},{8,7},{9,8},{10,9},{11,1... | collective-permute-start | bytes 196616 | tf_op jit(solution)/shard_map/ppermute | solution.py:22
  56.2 1.3 %collective-permute-start.8 = (bf16[4,16,8,128]{3,0,2,1:T(4,128)(2,1)}, bf16[4,16,8,128]{3,0,2,1:T(4,128)(2,1)S(1)}, u32[]{:S(2)}, u32[]{:S(2)}) collective-permute-start(bf16[4,16,8,128]{3,0,2,1:T(4,128)(2,1)} %all-to-all-done), channel_id=1, source_target_pairs={{0,256},{1,257},{2,258},{3,259},{4,260},{5,261},{6,262},{7,263},{8... | collective-permute-start | bytes 393224 | tf_op jit(solution)/shard_map/ppermute | solution.py:38
  57.5 0.5 collective-permute-done.7
  58.1 0.6 copy-done.8
  58.7 1.5 %select_maximum_fusion = f32[4,18,18,256]{3,2,1,0:T(8,128)S(1)} fusion(f32[4,1,16,256]{3,2,1,0:T(8,128)S(1)} %get-tuple-element.111, f32[4,1,16,256]{3,2,1,0:T(8,128)S(1)} %get-tuple-element.110, f32[4,16,1,256]{3,2,1,0:T(1,128)} %copy-done.8, f32[4,16,16,256]{3,2,1,0:T(8,128)} %get-tuple-element.63, f32[4,16,1,256]{3,2,1,0:T(1,128)S(1)} %collective-permute-done.6), kind=kLoop, calls=%fused_computation.66 | loop fusion | flops 2654208 | bytes 2637824 | tf_op jit(solution)/shard_map/concatenate | solution.py:87
  60.2 4.6 %collective-permute-done.8 = bf16[4,16,8,128]{3,0,2,1:T(4,128)(2,1)S(1)} collective-permute-done((bf16[4,16,8,128]{3,0,2,1:T(4,128)(2,1)}, bf16[4,16,8,128]{3,0,2,1:T(4,128)(2,1)S(1)}, u32[]{:S(2)}, u32[]{:S(2)}) %collective-permute-start.8) | collective-permute-done | bytes 131104 | tf_op jit(solution)/shard_map/ppermute | solution.py:38
  64.8 4.5 %fusion.10 = f32[128,4,128]{2,1,0:T(4,128)S(1)} fusion(bf16[4,128,128]{2,0,1:T(4,128)(2,1)S(1)} %bitcast.82, bf16[128,128,128]{2,1,0:T(8,128)(2,1)} %gather_fusion.1, pred[128]{0:T(512)(128)(4,1)S(1)} %compare_and_fusion), kind=kOutput, calls=%fused_computation.62 | convolution fusion | flops 18874368 | bytes 4587648 | tf_op jit(solution)/shard_map/sij,vsj->svi/dot_general | solution.py:105
  69.3 2.4 %scatter_custom_fusion = f32[512,512]{1,0:T(8,128)} fusion(s32[128]{0:T(128)S(1)} %reshape.143, f32[]{:T(128)} %constant.73.clone.1, f32[16,8,4,128]{3,2,1,0:T(4,128)S(1)} %bitcast.81), kind=kCustom, calls=%fused_computation.73 | custom fusion | flops 65536 | bytes 1310724 | tf_op jit(solution)/shard_map/scatter-add | solution.py:106
  71.7 2.6 %copy.33 = f32[512,512]{0,1:T(8,128)} copy(f32[512,512]{1,0:T(8,128)} %scatter_custom_fusion) | data formatting | bytes 2097152 | tf_op jit(solution)/shard_map/scatter-add | solution.py:106
  74.2 10.0 %conditional.3 = (f32[1,4,16,16,256]{4,3,2,1,0:T(8,128)S(1)}) conditional(s32[]{:T(128)} %convert_element_type.27, (f32[4,18,18,256]{3,2,1,0:T(8,128)S(1)}, f32[3,16,16,256]{3,2,1,0:T(8,128)S(1)}, f32[4,512,128]{1,2,0:T(8,128)}) %tuple.79, (f32[4,18,18,256]{3,2,1,0:T(8,128)S(1)}, f32[3,16,16,256]{3,2,1,0:T(8,128)S(1)}) %tuple.78), branch_computations={%region_3.4_spmd, %region_4.5_spmd} | conditional | flops 6488064 | bytes 31588444 | solution.py:75
  74.2 0.8 broadcast_multiply_fusion.5
  75.1 0.9 %slice_add_fusion.2 = (f32[1,16,16,256]{3,2,1,0:T(8,128)S(1)}, f32[1,16,16,256]{3,2,1,0:T(8,128)S(1)}, f32[1,16,16,256]{3,2,1,0:T(8,128)}, f32[1,16,16,256]{3,2,1,0:T(8,128)}) fusion(f32[4,16,16,256]{3,2,1,0:T(8,128)S(1)} %get-tuple-element.89, f32[4,16,16,256]{3,2,1,0:T(8,128)S(1)} %get-tuple-element.88, f32[4,16,16,256]{3,2,1,0:T(8,128)S(1)} %get-tuple-element.87), kind=kLoop, calls=%fused_computation.43 | loop fusion | flops 131072 | bytes 2621440 | tf_op jit(solution)/shard_map/cond/branch_0_fun/add | solution.py:60
  76.0 0.9 %multiply_bitcast_fusion.8 = (f32[16,16,256]{2,1,0:T(8,128)}, f32[16,16,256]{2,1,0:T(8,128)}, f32[16,16,256]{2,1,0:T(8,128)}) fusion(f32[3,16,16,256]{3,2,1,0:T(8,128)S(1)} %get-tuple-element.41), kind=kLoop, calls=%fused_computation.47 | loop fusion | flops 196608 | bytes 1572864 | tf_op jit(solution)/shard_map/cond/branch_0_fun/mul | solution.py:59
  76.9 2.6 %copy.34 = f32[4,512,128]{2,1,0:T(8,128)} copy(f32[4,512,128]{1,2,0:T(8,128)} %get-tuple-element.61) | data formatting | bytes 2097152 | tf_op jit(solution)/shard_map
  79.5 2.5 %reshape.110 = f32[4,16,16,256]{3,2,1,0:T(8,128)} reshape(f32[4,512,128]{2,1,0:T(8,128)} %copy.34) | data formatting | bytes 2097152 | tf_op jit(solution)/shard_map/reshape | solution.py:111
  82.0 2.2 %fusion.5 = f32[1,4,16,16,256]{4,3,2,1,0:T(8,128)S(1)} fusion(f32[4,16,16,256]{3,2,1,0:T(8,128)} %reshape.110, f32[1,16,16,256]{3,2,1,0:T(8,128)S(1)} %copy-done.5, f32[1,16,16,256]{3,2,1,0:T(8,128)S(1)} %copy-done.4, f32[1,16,16,256]{3,2,1,0:T(8,128)S(1)} %get-tuple-element.91, f32[1,16,16,256]{3,2,1,0:T(8,128)S(1)} %get-tuple-element.90, ...), kind=kLoop, calls=%fused_computation.37 | loop fusion | flops 4194304 | bytes 10944512 | tf_op jit(solution)/shard_map/broadcast_in_dim | solution.py:123
  84.2 1.0 %copy-done.7 = f32[1,4,16,16,256]{4,3,2,1,0:T(8,128)} copy-done((f32[1,4,16,16,256]{4,3,2,1,0:T(8,128)}, f32[1,4,16,16,256]{4,3,2,1,0:T(8,128)S(1)}, u32[]{:S(2)}) %copy-start.7) | copy-done | bytes 1048600
  (41 shorter events, 0.3 us)
Async XLA Ops:
  0.0 22.6 %copy-start = (bf16[1,1,8,128,128]{4,3,2,1,0:T(8,128)(2,1)S(1)}, bf16[1,1,8,128,128]{4,3,2,1,0:T(8,128)(2,1)}, u32[]{:S(2)}) copy-start(bf16[1,1,8,128,128]{4,3,2,1,0:T(8,128)(2,1)} %param.14) | copy-start | bytes 786436
  0.0 1.3 %copy-start.2 = (f32[1,4,16,16,256]{4,3,2,1,0:T(8,128)S(1)}, f32[1,4,16,16,256]{4,3,2,1,0:T(8,128)}, u32[]{:S(2)}) copy-start(f32[1,4,16,16,256]{4,3,2,1,0:T(8,128)} %param.11) | copy-start | bytes 3145732
  0.0 21.8 %copy-start.9 = (s32[1,1,16,8]{2,3,1,0:T(8,128)S(1)}, s32[1,1,16,8]{2,3,1,0:T(8,128)}, u32[]{:S(2)}) copy-start(s32[1,1,16,8]{2,3,1,0:T(8,128)} %param.15) | copy-start | bytes 1540
  0.0 22.5 %copy-start.11 = (s32[1,1,16,8]{2,3,1,0:T(8,128)S(1)}, s32[1,1,16,8]{2,3,1,0:T(8,128)}, u32[]{:S(2)}) copy-start(s32[1,1,16,8]{2,3,1,0:T(8,128)} %param.16) | copy-start | bytes 1540
  0.0 21.8 %copy-start.10 = (s32[1,1,16,8]{2,3,1,0:T(8,128)S(1)}, s32[1,1,16,8]{2,3,1,0:T(8,128)}, u32[]{:S(2)}) copy-start(s32[1,1,16,8]{2,3,1,0:T(8,128)} %param.17) | copy-start | bytes 1540
  1.4 24.4 %collective-permute-start = (bf16[4,1,16,256]{3,2,1,0:T(8,128)(2,1)S(1)}, bf16[4,1,16,256]{3,2,1,0:T(8,128)(2,1)S(1)}, u32[]{:S(2)}, u32[]{:S(2)}) collective-permute-start(bf16[4,1,16,256]{3,2,1,0:T(8,128)(2,1)S(1)} %get-tuple-element.116), channel_id=1, source_target_pairs={{0,16},{16,32},{32,48},{48,64},{64,80},{80,96},{96,112},{112,128},... | collective-permute-start | bytes 98312 | tf_op jit(solution)/shard_map/ppermute | solution.py:19
  3.3 22.4 %collective-permute-start.1 = (bf16[4,1,16,256]{3,2,1,0:T(8,128)(2,1)S(1)}, bf16[4,1,16,256]{3,2,1,0:T(8,128)(2,1)S(1)}, u32[]{:S(2)}, u32[]{:S(2)}) collective-permute-start(bf16[4,1,16,256]{3,2,1,0:T(8,128)(2,1)S(1)} %get-tuple-element.117), channel_id=1, source_target_pairs={{16,0},{32,16},{48,32},{64,48},{80,64},{96,80},{112,96},{128,112},... | collective-permute-start | bytes 98312 | tf_op jit(solution)/shard_map/ppermute | solution.py:22
  8.3 17.5 %collective-permute-start.2 = (f32[4,16,1,256]{3,2,1,0:T(1,128)S(1)}, f32[4,16,1,256]{3,2,1,0:T(1,128)S(1)}, u32[]{:S(2)}, u32[]{:S(2)}) collective-permute-start(f32[4,16,1,256]{3,2,1,0:T(1,128)S(1)} %get-tuple-element.108), channel_id=1, source_target_pairs={{0,1},{1,2},{2,3},{3,4},{4,5},{5,6},{6,7},{7,8},{8,9},{9,10},{10,1... | collective-permute-start | bytes 196616 | tf_op jit(solution)/shard_map/ppermute | solution.py:19
  12.6 13.2 %collective-permute-start.3 = (f32[4,16,1,256]{3,2,1,0:T(1,128)S(1)}, f32[4,16,1,256]{3,2,1,0:T(1,128)S(1)}, u32[]{:S(2)}, u32[]{:S(2)}) collective-permute-start(f32[4,16,1,256]{3,2,1,0:T(1,128)S(1)} %get-tuple-element.109), channel_id=1, source_target_pairs={{1,0},{2,1},{3,2},{4,3},{5,4},{6,5},{7,6},{8,7},{9,8},{10,9},{11,1... | collective-permute-start | bytes 196616 | tf_op jit(solution)/shard_map/ppermute | solution.py:22
  25.7 1.7 %copy-start.1 = (f32[1,3,16,16,256]{4,3,2,1,0:T(8,128)S(1)}, f32[1,3,16,16,256]{4,3,2,1,0:T(8,128)}, u32[]{:S(2)}) copy-start(f32[1,3,16,16,256]{4,3,2,1,0:T(8,128)} %param.12) | copy-start | bytes 2359300
  25.7 1.8 %copy-start.3 = (f32[4,16,16,256]{3,2,1,0:T(8,128)S(1)}, f32[4,16,16,256]{3,2,1,0:T(8,128)}, u32[]{:S(2)}) copy-start(f32[4,16,16,256]{3,2,1,0:T(8,128)} %param.13) | copy-start | bytes 3145732
  32.9 23.3 %all-to-all-start = ((bf16[4,16,8,128]{3,0,2,1:T(4,128)(2,1)}), bf16[4,16,8,128]{3,0,2,1:T(4,128)(2,1)}, u32[]{:S(2)}, u32[]{:S(2)}) async-start(bf16[4,16,8,128]{3,0,2,1:T(4,128)(2,1)} %select_select_fusion), calls=%async_computation | async-start | bytes 262144 | tf_op jit(solution)/shard_map/all_to_all | solution.py:119
  40.1 16.0 %collective-permute-start.4 = (bf16[4,1,16,256]{3,2,1,0:T(8,128)(2,1)S(1)}, bf16[4,1,16,256]{3,2,1,0:T(8,128)(2,1)S(1)}, u32[]{:S(2)}, u32[]{:S(2)}) collective-permute-start(bf16[4,1,16,256]{3,2,1,0:T(8,128)(2,1)S(1)} %get-tuple-element.114), channel_id=1, source_target_pairs={{0,16},{16,32},{32,48},{48,64},{64,80},{80,96},{96,112},{112,128},... | collective-permute-start | bytes 98312 | tf_op jit(solution)/shard_map/ppermute | solution.py:19
  42.2 14.0 %collective-permute-start.5 = (bf16[4,1,16,256]{3,2,1,0:T(8,128)(2,1)S(1)}, bf16[4,1,16,256]{3,2,1,0:T(8,128)(2,1)S(1)}, u32[]{:S(2)}, u32[]{:S(2)}) collective-permute-start(bf16[4,1,16,256]{3,2,1,0:T(8,128)(2,1)S(1)} %get-tuple-element.115), channel_id=1, source_target_pairs={{16,0},{32,16},{48,32},{64,48},{80,64},{96,80},{112,96},{128,112},... | collective-permute-start | bytes 98312 | tf_op jit(solution)/shard_map/ppermute | solution.py:22
  48.2 9.3 %collective-permute-start.6 = (f32[4,16,1,256]{3,2,1,0:T(1,128)S(1)}, f32[4,16,1,256]{3,2,1,0:T(1,128)S(1)}, u32[]{:S(2)}, u32[]{:S(2)}) collective-permute-start(f32[4,16,1,256]{3,2,1,0:T(1,128)S(1)} %get-tuple-element.106), channel_id=1, source_target_pairs={{0,1},{1,2},{2,3},{3,4},{4,5},{5,6},{6,7},{7,8},{8,9},{9,10},{10,1... | collective-permute-start | bytes 196616 | tf_op jit(solution)/shard_map/ppermute | solution.py:19
  50.1 7.9 %collective-permute-start.7 = (f32[4,16,1,256]{3,2,1,0:T(1,128)S(1)}, f32[4,16,1,256]{3,2,1,0:T(1,128)S(1)}, u32[]{:S(2)}, u32[]{:S(2)}) collective-permute-start(f32[4,16,1,256]{3,2,1,0:T(1,128)S(1)} %get-tuple-element.107), channel_id=1, source_target_pairs={{1,0},{2,1},{3,2},{4,3},{5,4},{6,5},{7,6},{8,7},{9,8},{10,9},{11,1... | collective-permute-start | bytes 196616 | tf_op jit(solution)/shard_map/ppermute | solution.py:22
  56.2 8.6 %collective-permute-start.8 = (bf16[4,16,8,128]{3,0,2,1:T(4,128)(2,1)}, bf16[4,16,8,128]{3,0,2,1:T(4,128)(2,1)S(1)}, u32[]{:S(2)}, u32[]{:S(2)}) collective-permute-start(bf16[4,16,8,128]{3,0,2,1:T(4,128)(2,1)} %all-to-all-done), channel_id=1, source_target_pairs={{0,256},{1,257},{2,258},{3,259},{4,260},{5,261},{6,262},{7,263},{8... | collective-permute-start | bytes 393224 | tf_op jit(solution)/shard_map/ppermute | solution.py:38
  58.1 0.6 copy-start.8
  76.9 5.1 %copy-start.4 = (f32[1,16,16,256]{3,2,1,0:T(8,128)S(1)}, f32[1,16,16,256]{3,2,1,0:T(8,128)}, u32[]{:S(2)}) copy-start(f32[1,16,16,256]{3,2,1,0:T(8,128)} %get-tuple-element.92) | copy-start | bytes 786436 | tf_op jit(solution)/shard_map/cond
  76.9 5.1 %copy-start.5 = (f32[1,16,16,256]{3,2,1,0:T(8,128)S(1)}, f32[1,16,16,256]{3,2,1,0:T(8,128)}, u32[]{:S(2)}) copy-start(f32[1,16,16,256]{3,2,1,0:T(8,128)} %get-tuple-element.93) | copy-start | bytes 786436 | tf_op jit(solution)/shard_map/cond
  76.9 5.1 %copy-start.6 = (f32[16,16,256]{2,1,0:T(8,128)S(1)}, f32[16,16,256]{2,1,0:T(8,128)}, u32[]{:S(2)}) copy-start(f32[16,16,256]{2,1,0:T(8,128)} %get-tuple-element.94) | copy-start | bytes 786436 | tf_op jit(solution)/shard_map/cond
  84.2 1.0 %copy-start.7 = (f32[1,4,16,16,256]{4,3,2,1,0:T(8,128)}, f32[1,4,16,16,256]{4,3,2,1,0:T(8,128)S(1)}, u32[]{:S(2)}) copy-start(f32[1,4,16,16,256]{4,3,2,1,0:T(8,128)S(1)} %get-tuple-element.130) | copy-start | bytes 3145732
where the time goes:
time: 85.9 us; the launch traced here: 85.2 us
  starting transfers between devices  43.5 us (51%)
  local copies, waits for them, and re-layouts  17.1 us (20%)
  other arithmetic  14.5 us (17%)
  waiting for transfers between devices  5.15 us (6%)
  matrix products  4.52 us (5%)
    ppermute x4, starting transfers between devices, with_halo(): lax.ppermute(lax.slice_in_dim(block, 0, width, axis=dim), axis, backward)  24.8 us
    ppermute x4, starting transfers between devices, with_halo(): lax.ppermute(lax.slice_in_dim(block, block.shape[dim] - width, None, axis...  10.2 us
    all_to_all x1, starting transfers between devices, shards(): lax.all_to_all(packed, 'ax', split_axis=1, concat_axis=1, tiled=True)  7.22 us
    ppermute x1, waiting for transfers between devices, from_behind(): return lax.ppermute(x, axis, pairs)  4.61 us
    dot_general x1, matrix products, interpolate(): jnp.einsum('sij,vsj->svi', chosen, line_data, preferred_element_type=jnp....  4.52 us
    concatenate x2, other arithmetic, rim_cells(): return jnp.concatenate([lower_edge, beside_all, upper_edge], axis=1)  3.11 us
    unnamed x20, local copies, waits for them, and re-layouts  3.11 us
    gather x1, local copies, waits for them, and re-layouts, interpolate(): jnp.take(weight_blocks.reshape(-1, LINE, LINE), weight_ids.reshape(slot_c...  3.06 us
  transfers between devices with their start and end apart: 10, of which 2 were waited for; matrix products, arithmetic and copies ran while one was open for 8% of the time, Pallas kernels for 0%

commit v1 on v0

v1 whole, which is shorter than its diff:
```python
import jax
import jax.numpy as jnp
from jax import lax
from jax.experimental import pallas as pl
from jax.experimental.pallas import tpu as pltpu
from jax.sharding import PartitionSpec as P

F32 = jnp.float32
BF16 = jnp.bfloat16
NV = 4
C1 = 16
C2 = 16
C3 = 256
LINE = 128
CAP = 8
NW = 8

NEAR = 0
FAR = 4
COEF = 8
SOURCE = 11
CORNER = 15
PLANES = 16

VMEM = pl.BlockSpec(memory_space=pltpu.VMEM)
SMEM = pl.BlockSpec(memory_space=pltpu.SMEM)


def shift(x, axis, by, periodic):
    count = lax.axis_size(axis)
    pairs = [(i, (i + by) % count) for i in range(count) if periodic or 0 <= i + by < count]
    return lax.ppermute(x, axis, pairs)


def rows_of(shape, axis):
    return lax.broadcasted_iota(jnp.int32, shape, axis)


def next_row(x, end):
    return jnp.where(rows_of(x.shape, 0) == x.shape[0] - 1, end, pltpu.roll(x, x.shape[0] - 1, 0))


def previous_row(x, end):
    return jnp.where(rows_of(x.shape, 0) == 0, end, pltpu.roll(x, 1, 0))


def next_lane(x):
    return pltpu.roll(x, x.shape[1] - 1, 1)


def previous_lane(x):
    return pltpu.roll(x, 1, 1)


def eddy_plane(cells, upper, lower, ends, factors, across):
    along = 1 - across
    scaled = [0.25 * factors[k] for k in range(3)]
    carried = [0.125 * cells[k] for k in range(3)]
    up = [scaled[k] - carried[k] for k in range(3)]
    down = [scaled[k] + carried[k] for k in range(3)]
    lanes = rows_of(cells[0].shape, 1)
    up[2] = jnp.where(lanes == C3 - 1, 0.0, up[2])
    down[2] = jnp.where(lanes == 0, 0.0, down[2])
    own = 1.0 - 2.0 * (scaled[0] + scaled[1] + scaled[2])
    results = []
    for v in range(NV):
        cell = cells[v]
        low_end, high_end = ends[v]
        result = own * cell + up[across] * upper[v] + down[across] * lower[v]
        result += up[along] * next_row(cell, high_end) + down[along] * previous_row(cell, low_end)
        result += up[2] * next_lane(cell) + down[2] * previous_lane(cell)
        results.append(result)
    return results


def acoustic_plane(cells, upper, lower, ends, factors, across, source):
    along = 1 - across
    lanes = rows_of(cells[0].shape, 1)
    scaled = [0.125 * factors[k] for k in range(3)]
    change = [[None] * NV for _ in range(3)]
    for v in range(NV):
        cell = cells[v]
        low_end, high_end = ends[v]
        change[across][v] = upper[v] - lower[v]
        change[along][v] = next_row(cell, high_end) - previous_row(cell, low_end)
        change[2][v] = jnp.where(lanes == C3 - 1, 0.0, next_lane(cell)) - jnp.where(
            lanes == 0, 0.0, previous_lane(cell)
        )
    results = []
    for v in range(NV):
        if v == 0:
            coupling = change[0][1] + change[1][2] + change[2][3]
        else:
            coupling = change[v - 1][0]
        result = cells[v] - 0.125 * coupling
        for k in range(3):
            result -= scaled[k] * change[k][v]
        if source is not None:
            result += 0.25 * source[v]
        results.append(result)
    return results


def plane_step(acoustic, cells, upper, lower, ends, factors, across, source):
    if acoustic:
        return acoustic_plane(cells, upper, lower, ends, factors, across, source)
    return eddy_plane(cells, upper, lower, ends, factors, across)


def pack_slabs(low_q, high_q, low_c, high_c, low_s, high_s, low_out, high_out):
    for v in range(NV):
        low_out[NEAR + v] = low_q[0, v, 0].astype(BF16)
        low_out[FAR + v] = low_q[0, v, 1].astype(BF16)
        high_out[NEAR + v] = high_q[0, v, 1].astype(BF16)
        high_out[FAR + v] = high_q[0, v, 0].astype(BF16)
        low_out[SOURCE + v] = low_s[v, 0].astype(BF16)
        high_out[SOURCE + v] = high_s[v, 1].astype(BF16)
    for k in range(3):
        low_out[COEF + k] = low_c[0, k, 0].astype(BF16)
        high_out[COEF + k] = high_c[0, k, 1].astype(BF16)


def pack_sectors(q, c, s, below, above, low_out, high_out):
    def column(ref, component, j):
        return ref[component, :, j, :].astype(BF16)

    for v in range(NV):
        low_out[NEAR + v] = column(q, v, 0)
        low_out[FAR + v] = column(q, v, 1)
        high_out[NEAR + v] = column(q, v, C2 - 1)
        high_out[FAR + v] = column(q, v, C2 - 2)
        low_out[SOURCE + v] = column(s, v, 0)
        high_out[SOURCE + v] = column(s, v, C2 - 1)
    for k in range(3):
        low_out[COEF + k] = column(c, k, 0)
        high_out[COEF + k] = column(c, k, C2 - 1)
    for out, j in ((low_out, 0), (high_out, C2 - 1)):
        rows = []
        for v in range(NV):
            rows.append(below[NEAR + v].astype(F32)[j : j + 1])
            rows.append(above[NEAR + v].astype(F32)[j : j + 1])
        rows.append(jnp.zeros((C1 - 2 * NV, C3), F32))
        out[CORNER] = jnp.concatenate(rows, axis=0).astype(BF16)


def first_step(where, ids, q, c, s, below, above, left, right, stepped, rims, packed, sides, stage):
    for side, message in enumerate((left, right)):
        for v in range(NV):
            sides[side, v] = message[NEAR + v].astype(F32)

    def fields_of(message, start, count=NV):
        return [message[start + v].astype(F32) for v in range(count)]

    def run(acoustic):
        corners = [message[CORNER].astype(F32) for message in (left, right)]

        for side, message in enumerate((left, right)):
            near = [sides[side, v] for v in range(NV)]
            far = fields_of(message, FAR)
            own = [q[v, :, 0 if side == 0 else C2 - 1, :] for v in range(NV)]
            ends = [
                (corners[side][2 * v : 2 * v + 1], corners[side][2 * v + 1 : 2 * v + 2])
                for v in range(NV)
            ]
            upper, lower = (own, far) if side == 0 else (far, own)
            source = fields_of(message, SOURCE) if acoustic else None
            results = plane_step(
                acoustic, near, upper, lower, ends, fields_of(message, COEF, 3), 1, source
            )
            for v in range(NV):
                rims[side, v] = results[v]

        for side, message in enumerate((below, above)):
            near = fields_of(message, NEAR)
            far = fields_of(message, FAR)
            own = [q[v, 0 if side == 0 else C1 - 1] for v in range(NV)]
            ends = [
                (
                    corners[0][2 * v + side : 2 * v + side + 1],
                    corners[1][2 * v + side : 2 * v + side + 1],
                )
                for v in range(NV)
            ]
            upper, lower = (own, far) if side == 0 else (far, own)
            source = fields_of(message, SOURCE) if acoustic else None
            results = plane_step(
                acoustic, near, upper, lower, ends, fields_of(message, COEF, 3), 0, source
            )
            inside = where[1] > 0 if side == 0 else where[1] < where[2] - 1
            for v in range(NV):
                rims[2 + side, v] = jnp.where(inside, results[v], 0.0)

        def row(i, upper, lower):
            cells = [q[v, i] for v in range(NV)]
            ends = [(sides[0, v, pl.ds(i, 1), :], sides[1, v, pl.ds(i, 1), :]) for v in range(NV)]
            factors = [c[k, i] for k in range(3)]
            source = [s[v, i] for v in range(NV)] if acoustic else None
            results = plane_step(acoustic, cells, upper, lower, ends, factors, 0, source)
            for v in range(NV):
                stepped[v, i] = results[v]

        row(0, [q[v, 1] for v in range(NV)], fields_of(below, NEAR))
        row(C1 - 1, fields_of(above, NEAR), [q[v, C1 - 2] for v in range(NV)])

        @pl.loop(1, C1 - 1)
        def _(i):
            row(i, [q[v, i + 1] for v in range(NV)], [q[v, i - 1] for v in range(NV)])

    @pl.when(where[0] == 0)
    def _():
        run(False)

        @pl.loop(0, packed.shape[0] // 2)
        def _(r):
            packed[r] = jnp.zeros(packed.shape[1:], BF16)
            for k in range(CAP):
                block = ids[k, r]
                chosen = jnp.maximum(block, 0)
                i = chosen // (2 * C2)
                j = (chosen // 2) % C2
                for v in range(NV):
                    line = stepped[v, i, pl.ds(j, 1), :]
                    half = jnp.where(chosen % 2 == 0, line[:, :LINE], line[:, LINE:])
                    stage[pl.ds(k * NV + v, 1), :] = jnp.where(block >= 0, half, 0.0)
            packed[packed.shape[0] // 2 + r] = stage[...].astype(BF16)

    @pl.when(where[0] != 0)
    def _():
        run(True)
        packed[...] = jnp.zeros(packed.shape, BF16)


def second_step(where, q, c, rims, out):
    def run(acoustic):
        def row(i, upper, lower):
            cells = [q[v, i] for v in range(NV)]
            ends = [(rims[0, v, pl.ds(i, 1), :], rims[1, v, pl.ds(i, 1), :]) for v in range(NV)]
            factors = [c[k, i] for k in range(3)]
            results = plane_step(acoustic, cells, upper, lower, ends, factors, 0, None)
            for v in range(NV):
                out[v, i] = results[v]

        row(0, [q[v, 1] for v in range(NV)], [rims[2, v] for v in range(NV)])
        row(C1 - 1, [rims[3, v] for v in range(NV)], [q[v, C1 - 2] for v in range(NV)])

        @pl.loop(1, C1 - 1)
        def _(i):
            row(i, [q[v, i + 1] for v in range(NV)], [q[v, i - 1] for v in range(NV)])

    @pl.when(where[0] == 0)
    def _():
        run(False)

    @pl.when(where[0] != 0)
    def _():
        run(True)


def add_source(where, targets, weights, received, blocks, base, out, products, sums):
    @pl.when(where[0] == 0)
    def _():
        out[...] = base[...]

    @pl.when(where[0] != 0)
    def _():
        count = received.shape[0] // 2
        lines = received[0:count].reshape(count * CAP * NV, LINE)
        for w in range(NW):
            products[w] = lax.dot_general(
                lines, blocks[w], (((1,), (1,)), ((), ())), preferred_element_type=F32
            )
        sums[...] = jnp.zeros(sums.shape, F32)

        @pl.loop(0, count)
        def _(a):
            for k in range(CAP):
                target = targets[k, a]
                w = weights[k, a]
                i = target // (2 * C2)
                j = (target // 2) % C2
                half = target % 2
                held = []
                for v in range(NV):
                    added = products[w, pl.ds(a * (CAP * NV) + k * NV + v, 1), :]
                    held.append(sums[half, v, i, pl.ds(j, 1), :] + added)
                for v in range(NV):
                    sums[half, v, i, pl.ds(j, 1), :] = held[v]

        for half in range(2):
            lanes = slice(half * LINE, (half + 1) * LINE)
            out[:, :, :, lanes] = base[:, :, :, lanes] + 0.25 * sums[half]


def shards(fields, coefficients, old_source, weight_blocks, send_ids, target_ids, weight_ids):
    current = fields[0]
    factors = coefficients[0]
    peers = lax.axis_size("sec") * lax.axis_size("ax")
    where = jnp.stack(
        [lax.axis_index("sec"), lax.axis_index("ax"), jnp.int32(lax.axis_size("ax"))]
    ).astype(jnp.int32)

    def struct(*shape, dtype=F32):
        return jax.ShapeDtypeStruct(shape, dtype)

    message = struct(PLANES, C1, C3, dtype=BF16)

    last = C1 // 2 - 1
    slab_specs = []
    for lead in ((1, NV), (1, 3), (NV,)):
        for at in (0, last):
            slab_specs.append(
                pl.BlockSpec(
                    lead + (2, C2, C3),
                    lambda _, at=at, lead=lead: (0,) * len(lead) + (at, 0, 0),
                )
            )
    whole = pl.BlockSpec((PLANES, C2, C3), lambda _: (0, 0, 0))
    low_slab, high_slab = pl.pallas_call(
        pack_slabs,
        grid=(1,),
        in_specs=slab_specs,
        out_specs=[whole, whole],
        out_shape=[message, message],
        name="pack_slabs",
    )(fields, fields, coefficients, coefficients, old_source, old_source)
    below = shift(high_slab, "ax", 1, False)
    above = shift(low_slab, "ax", -1, False)

    low_sector, high_sector = pl.pallas_call(
        pack_sectors,
        in_specs=[VMEM] * 5,
        out_specs=[VMEM, VMEM],
        out_shape=[message, message],
        name="pack_sectors",
    )(current, factors, old_source, below, above)
    left = shift(high_sector, "az", 1, True)
    right = shift(low_sector, "az", -1, True)

    stepped, rims, packed = pl.pallas_call(
        first_step,
        in_specs=[SMEM, SMEM] + [VMEM] * 7,
        out_specs=[VMEM] * 3,
        out_shape=[
            struct(NV, C1, C2, C3),
            struct(4, NV, C1, C3),
            struct(peers, CAP * NV, LINE, dtype=BF16),
        ],
        scratch_shapes=[pltpu.VMEM((2, NV, C1, C3), F32), pltpu.VMEM((CAP * NV, LINE), F32)],
        name="first_step",
    )(
        where,
        send_ids[0, 0].T,
        current,
        factors,
        old_source,
        below,
        above,
        left,
        right,
    )
    received = lax.all_to_all(packed, ("sec", "ax"), split_axis=0, concat_axis=0, tiled=True)
    base = pl.pallas_call(
        second_step,
        in_specs=[SMEM] + [VMEM] * 3,
        out_specs=VMEM,
        out_shape=struct(NV, C1, C2, C3),
        name="second_step",
    )(where, stepped, factors, rims)
    advanced = pl.pallas_call(
        add_source,
        in_specs=[SMEM] * 3 + [VMEM] * 3,
        out_specs=VMEM,
        out_shape=struct(NV, C1, C2, C3),
        scratch_shapes=[
            pltpu.VMEM((NW, peers // 2 * CAP * NV, LINE), F32),
            pltpu.VMEM((2, NV, C1, C2, LINE), F32),
        ],
        name="add_source",
    )(where, target_ids[0, 0].T, weight_ids[0, 0].T, received, weight_blocks[0, 0], base)
    return advanced[None]


def solution(mesh):
    return jax.shard_map(
        shards,
        mesh=mesh,
        in_specs=(
            P("sec", None, "ax", "az", None),
            P("sec", None, "ax", "az", None),
            P(None, "ax", "az", None),
            P("ax", "az", None, None, None),
            P("ax", "az", None, None),
            P("ax", "az", None, None),
            P("ax", "az", None, None),
        ),
        out_specs=P("sec", None, "ax", "az", None),
        check_vma=False,
    )
```

time: 85.9 us -> 65.3 us (0.76)
  the two profiles are of different devices: /device:TPU:36 before, /device:TPU:1 now
where the time goes in v1:
time: 65.3 us; the launch traced here: 64.9 us
  starting transfers between devices  32.1 us (49%)
  Pallas kernels  18.1 us (28%)
  waiting for transfers between devices  12 us (18%)
  local copies, waits for them, and re-layouts  2.01 us (3%)
  other arithmetic  0.67 us (1%)
    ppermute x4, starting transfers between devices, shift(): return lax.ppermute(x, axis, pairs)  23.4 us
    all_to_all x1, waiting for transfers between devices, shards(): lax.all_to_all(packed, ('sec', 'ax'), split_axis=0, concat_axis=0, tiled=...  9.32 us
    all_to_all x1, starting transfers between devices, shards(): lax.all_to_all(packed, ('sec', 'ax'), split_axis=0, concat_axis=0, tiled=...  8.68 us
    pallas_call x1, Pallas kernels, shards(): pl.pallas_call(first_step, in_specs=[SMEM, SMEM] + [VMEM] * 7, out_specs=...  6.58 us
    pallas_call x1, Pallas kernels, shards(): pl.pallas_call(second_step, in_specs=[SMEM] + [VMEM] * 3, out_specs=VMEM,...  4.1 us
    pallas_call x1, Pallas kernels, shards(): pl.pallas_call(pack_sectors, in_specs=[VMEM] * 5, out_specs=[VMEM, VMEM],...  3.01 us
    ppermute x4, waiting for transfers between devices, shift(): return lax.ppermute(x, axis, pairs)  2.72 us
    pallas_call x1, Pallas kernels, shards(): pl.pallas_call(add_source, in_specs=[SMEM] * 3 + [VMEM] * 3, out_specs=VM...  2.45 us
  transfers between devices with their start and end apart: 5, of which 3 were waited for; matrix products, arithmetic and copies ran while one was open for 1% of the time, Pallas kernels for 6%

profile of v1, /device:TPU:1, one launch (start us, length us, event | category | flops | bytes accessed | tf_op | source)
XLA Modules:
  0.0 64.9 jit_solution(12184766464658914855)
XLA Ops:
  0.0 1.9 %pack_slabs.1 = (bf16[16,16,256]{2,1,0:T(8,128)(2,1)}, bf16[16,16,256]{2,1,0:T(8,128)(2,1)}) custom-call(f32[1,4,16,16,256]{4,3,2,1,0:T(8,128)} %high_q.1, f32[1,4,16,16,256]{4,3,2,1,0:T(8,128)} %high_q.1, f32[1,3,16,16,256]{4,3,2,1,0:T(8,128)} %high_c.1, f32[1,3,16,16,256]{4,3,2,1,0:T(8,128)} %high_c.1, f32[4,16,16,256]{3,2,1,0:T(8,128)} %s.3, ...), custom_call_target="tpu_custom_call" | custom-call | tf_op jit(solution)/shard_map/pack_slabs/pallas_call | solution.py:318
  1.9 4.6 %collective-permute-start = (bf16[16,16,256]{2,1,0:T(8,128)(2,1)}, bf16[16,16,256]{2,1,0:T(8,128)(2,1)S(1)}, u32[]{:S(2)}, u32[]{:S(2)}) collective-permute-start(bf16[16,16,256]{2,1,0:T(8,128)(2,1)} %get-tuple-element.12), channel_id=1, source_target_pairs={{0,16},{16,32},{32,48},{48,64},{64,80},{80,96},{96,112},{112,128},... | collective-permute-start | bytes 393224 | tf_op jit(solution)/shard_map/ppermute | solution.py:32
  6.5 5.5 %collective-permute-start.1 = (bf16[16,16,256]{2,1,0:T(8,128)(2,1)}, bf16[16,16,256]{2,1,0:T(8,128)(2,1)S(1)}, u32[]{:S(2)}, u32[]{:S(2)}) collective-permute-start(bf16[16,16,256]{2,1,0:T(8,128)(2,1)} %get-tuple-element.13), channel_id=1, source_target_pairs={{16,0},{32,16},{48,32},{64,48},{80,64},{96,80},{112,96},{128,112},... | collective-permute-start | bytes 393224 | tf_op jit(solution)/shard_map/ppermute | solution.py:32
  12.0 0.0 collective-permute-done.below
  12.0 0.0 copy-start.1
  12.0 1.2 %collective-permute-done.1.above = bf16[16,16,256]{2,1,0:T(8,128)(2,1)S(1)} collective-permute-done((bf16[16,16,256]{2,1,0:T(8,128)(2,1)}, bf16[16,16,256]{2,1,0:T(8,128)(2,1)S(1)}, u32[]{:S(2)}, u32[]{:S(2)}) %collective-permute-start.1) | collective-permute-done | bytes 131104 | tf_op jit(solution)/shard_map/ppermute | solution.py:32
  13.2 0.0 copy-start.2
  13.2 0.0 copy-done.1
  13.2 0.6 copy-done.2
  13.8 3.0 %pack_sectors.1 = (bf16[16,16,256]{2,1,0:T(8,128)(2,1)}, bf16[16,16,256]{2,1,0:T(8,128)(2,1)}) custom-call(f32[4,16,16,256]{3,2,1,0:T(8,128)} %bitcast.18, f32[3,16,16,256]{3,2,1,0:T(8,128)} %bitcast.15, f32[4,16,16,256]{3,2,1,0:T(8,128)} %s.3, bf16[16,16,256]{2,1,0:T(8,128)(2,1)} %copy-done.1, bf16[16,16,256]{2,1,0:T(8,128)(2,1)} %copy-done.2), custom_call_target="tpu_custom_call" | custom-call | tf_op jit(solution)/shard_map/pack_sectors/pallas_call | solution.py:329
  16.8 3.8 %collective-permute-start.2 = (bf16[16,16,256]{2,1,0:T(8,128)(2,1)}, bf16[16,16,256]{2,1,0:T(8,128)(2,1)S(1)}, u32[]{:S(2)}, u32[]{:S(2)}) collective-permute-start(bf16[16,16,256]{2,1,0:T(8,128)(2,1)} %get-tuple-element.14), channel_id=1, source_target_pairs={{0,1},{1,2},{2,3},{3,4},{4,5},{5,6},{6,7},{7,8},{8,9},{9,10},{10,1... | collective-permute-start | bytes 393224 | tf_op jit(solution)/shard_map/ppermute | solution.py:32
  20.7 9.5 %collective-permute-start.3 = (bf16[16,16,256]{2,1,0:T(8,128)(2,1)}, bf16[16,16,256]{2,1,0:T(8,128)(2,1)S(1)}, u32[]{:S(2)}, u32[]{:S(2)}) collective-permute-start(bf16[16,16,256]{2,1,0:T(8,128)(2,1)} %get-tuple-element.15), channel_id=1, source_target_pairs={{0,15},{1,0},{2,1},{3,2},{4,3},{5,4},{6,5},{7,6},{8,7},{9,8},{10,9... | collective-permute-start | bytes 393224 | tf_op jit(solution)/shard_map/ppermute | solution.py:32
  30.2 0.7 %pad_add_fusion.where = s32[3]{0:T(128)} fusion(s32[1]{0:T(128)} %constant.12.clone.1, s32[1]{0:T(128)} %bitcast.1, s32[1]{0:T(128)} %bitcast), kind=kLoop, calls=%fused_computation | loop fusion | flops 6 | bytes 24 | tf_op jit(solution)/shard_map/stack | solution.py:298
  30.9 0.0 collective-permute-done.2.left
  30.9 0.0 copy-start.3
  30.9 1.6 %collective-permute-done.3.right = bf16[16,16,256]{2,1,0:T(8,128)(2,1)S(1)} collective-permute-done((bf16[16,16,256]{2,1,0:T(8,128)(2,1)}, bf16[16,16,256]{2,1,0:T(8,128)(2,1)S(1)}, u32[]{:S(2)}, u32[]{:S(2)}) %collective-permute-start.3) | collective-permute-done | bytes 131104 | tf_op jit(solution)/shard_map/ppermute | solution.py:32
  32.4 0.0 copy-start.4
  32.4 0.0 copy-done.3
  32.4 0.6 copy-done.4
  33.1 6.6 %first_step.1 = (f32[4,16,16,256]{3,2,1,0:T(8,128)}, f32[4,4,16,256]{3,2,1,0:T(8,128)}, bf16[32,32,128]{2,1,0:T(8,128)(2,1)}) custom-call(s32[3]{0:T(128)} %pad_add_fusion.where, s32[8,16]{1,0:T(8,128)} %bitcast.21, f32[4,16,16,256]{3,2,1,0:T(8,128)} %bitcast.19, f32[3,16,16,256]{3,2,1,0:T(8,128)} %bitcast.16, f32[4,16,16,256]{3,2,1,0:T(8,128)} %s.3, ...), custom_call_target="tpu_custom_call" | custom-call | tf_op jit(solution)/shard_map/first_step/pallas_call | solution.py:339
  39.6 8.7 %all-to-all-start = ((bf16[32,32,128]{2,1,0:T(8,128)(2,1)}), bf16[32,32,128]{2,1,0:T(8,128)(2,1)S(1)}, u32[]{:S(2)}, u32[]{:S(2)}) async-start(bf16[32,32,128]{2,1,0:T(8,128)(2,1)} %get-tuple-element.16), calls=%async_computation | async-start | bytes 524288 | tf_op jit(solution)/shard_map/all_to_all | solution.py:361
  48.3 4.1 %second_step.1.base = f32[4,16,16,256]{3,2,1,0:T(8,128)} custom-call(s32[3]{0:T(128)} %pad_add_fusion.where, f32[4,16,16,256]{3,2,1,0:T(8,128)} %get-tuple-element.17.q, f32[3,16,16,256]{3,2,1,0:T(8,128)} %bitcast.17, f32[4,4,16,256]{3,2,1,0:T(8,128)} %get-tuple-element.18.rims), custom_call_target="tpu_custom_call" | custom-call | tf_op jit(solution)/shard_map/second_step/pallas_call | solution.py:362
  52.4 9.3 %all-to-all-done.received = bf16[32,32,128]{2,1,0:T(8,128)(2,1)S(1)} async-done(((bf16[32,32,128]{2,1,0:T(8,128)(2,1)}), bf16[32,32,128]{2,1,0:T(8,128)(2,1)S(1)}, u32[]{:S(2)}, u32[]{:S(2)}) %all-to-all-start) | async-done | bytes 262176 | tf_op jit(solution)/shard_map/all_to_all | solution.py:361
  61.8 0.0 copy-start
  61.8 0.7 %copy-done = bf16[32,32,128]{2,1,0:T(8,128)(2,1)} copy-done((bf16[32,32,128]{2,1,0:T(8,128)(2,1)}, bf16[32,32,128]{2,1,0:T(8,128)(2,1)S(1)}, u32[]{:S(2)}) %copy-start) | copy-done | bytes 262168
  62.5 2.5 %add_source.1 = f32[4,16,16,256]{3,2,1,0:T(8,128)} custom-call(s32[3]{0:T(128)} %pad_add_fusion.where, s32[8,16]{1,0:T(8,128)} %bitcast.22, s32[8,16]{1,0:T(8,128)} %bitcast.23, bf16[32,32,128]{2,1,0:T(8,128)(2,1)} %copy-done, bf16[8,128,128]{2,1,0:T(8,128)(2,1)} %bitcast.20, f32[4,16,16,256]{3,2,1,0:T(8,128)} %second_step.1.base), custom_call_target="tpu_custom_call" | custom-call | tf_op jit(solution)/shard_map/add_source/pallas_call | solution.py:369
Async XLA Ops:
  1.9 10.1 %collective-permute-start = (bf16[16,16,256]{2,1,0:T(8,128)(2,1)}, bf16[16,16,256]{2,1,0:T(8,128)(2,1)S(1)}, u32[]{:S(2)}, u32[]{:S(2)}) collective-permute-start(bf16[16,16,256]{2,1,0:T(8,128)(2,1)} %get-tuple-element.12), channel_id=1, source_target_pairs={{0,16},{16,32},{32,48},{48,64},{64,80},{80,96},{96,112},{112,128},... | collective-permute-start | bytes 393224 | tf_op jit(solution)/shard_map/ppermute | solution.py:32
  6.5 6.7 %collective-permute-start.1 = (bf16[16,16,256]{2,1,0:T(8,128)(2,1)}, bf16[16,16,256]{2,1,0:T(8,128)(2,1)S(1)}, u32[]{:S(2)}, u32[]{:S(2)}) collective-permute-start(bf16[16,16,256]{2,1,0:T(8,128)(2,1)} %get-tuple-element.13), channel_id=1, source_target_pairs={{16,0},{32,16},{48,32},{64,48},{80,64},{96,80},{112,96},{128,112},... | collective-permute-start | bytes 393224 | tf_op jit(solution)/shard_map/ppermute | solution.py:32
  12.0 1.2 %copy-start.1 = (bf16[16,16,256]{2,1,0:T(8,128)(2,1)}, bf16[16,16,256]{2,1,0:T(8,128)(2,1)S(1)}, u32[]{:S(2)}) copy-start(bf16[16,16,256]{2,1,0:T(8,128)(2,1)S(1)} %collective-permute-done.below) | copy-start | bytes 393220
  13.2 0.6 copy-start.2
  16.8 14.0 %collective-permute-start.2 = (bf16[16,16,256]{2,1,0:T(8,128)(2,1)}, bf16[16,16,256]{2,1,0:T(8,128)(2,1)S(1)}, u32[]{:S(2)}, u32[]{:S(2)}) collective-permute-start(bf16[16,16,256]{2,1,0:T(8,128)(2,1)} %get-tuple-element.14), channel_id=1, source_target_pairs={{0,1},{1,2},{2,3},{3,4},{4,5},{5,6},{6,7},{7,8},{8,9},{9,10},{10,1... | collective-permute-start | bytes 393224 | tf_op jit(solution)/shard_map/ppermute | solution.py:32
  20.7 11.8 %collective-permute-start.3 = (bf16[16,16,256]{2,1,0:T(8,128)(2,1)}, bf16[16,16,256]{2,1,0:T(8,128)(2,1)S(1)}, u32[]{:S(2)}, u32[]{:S(2)}) collective-permute-start(bf16[16,16,256]{2,1,0:T(8,128)(2,1)} %get-tuple-element.15), channel_id=1, source_target_pairs={{0,15},{1,0},{2,1},{3,2},{4,3},{5,4},{6,5},{7,6},{8,7},{9,8},{10,9... | collective-permute-start | bytes 393224 | tf_op jit(solution)/shard_map/ppermute | solution.py:32
  30.9 1.6 %copy-start.3 = (bf16[16,16,256]{2,1,0:T(8,128)(2,1)}, bf16[16,16,256]{2,1,0:T(8,128)(2,1)S(1)}, u32[]{:S(2)}) copy-start(bf16[16,16,256]{2,1,0:T(8,128)(2,1)S(1)} %collective-permute-done.2.left) | copy-start | bytes 393220
  32.4 0.6 copy-start.4
  39.6 22.1 %all-to-all-start = ((bf16[32,32,128]{2,1,0:T(8,128)(2,1)}), bf16[32,32,128]{2,1,0:T(8,128)(2,1)S(1)}, u32[]{:S(2)}, u32[]{:S(2)}) async-start(bf16[32,32,128]{2,1,0:T(8,128)(2,1)} %get-tuple-element.16), calls=%async_computation | async-start | bytes 524288 | tf_op jit(solution)/shard_map/all_to_all | solution.py:361
  61.8 0.7 %copy-start = (bf16[32,32,128]{2,1,0:T(8,128)(2,1)}, bf16[32,32,128]{2,1,0:T(8,128)(2,1)S(1)}, u32[]{:S(2)}) copy-start(bf16[32,32,128]{2,1,0:T(8,128)(2,1)S(1)} %all-to-all-done.received) | copy-start | bytes 786436

commit v2 on v1

v2 whole, which is shorter than its diff:
```python
import jax
import jax.numpy as jnp
from jax import lax
from jax.experimental import pallas as pl
from jax.experimental.pallas import tpu as pltpu
from jax.sharding import PartitionSpec as P

F32 = jnp.float32
BF16 = jnp.bfloat16
NV = 4
C1 = 16
C2 = 16
C3 = 256
LINE = 128
CAP = 8
NW = 8

NEAR = 0
FAR = 4
COEF = 8
SOURCE = 11
PLANES = 15

VMEM = pl.BlockSpec(memory_space=pltpu.VMEM)
ANY = pl.BlockSpec(memory_space=pl.ANY)
SMEM = pl.BlockSpec(memory_space=pltpu.SMEM)
PARAMS = pltpu.CompilerParams(vmem_limit_bytes=16 << 20)


def off_chip(x):
    return pltpu.with_memory_space_constraint(x, pltpu.HBM)


def shift(x, axis, by, periodic):
    count = lax.axis_size(axis)
    pairs = [(i, (i + by) % count) for i in range(count) if periodic or 0 <= i + by < count]
    return lax.ppermute(x, axis, pairs)


def rows_of(shape, axis):
    return lax.broadcasted_iota(jnp.int32, shape, axis)


def next_row(x, end):
    return jnp.where(rows_of(x.shape, 0) == x.shape[0] - 1, end, pltpu.roll(x, x.shape[0] - 1, 0))


def previous_row(x, end):
    return jnp.where(rows_of(x.shape, 0) == 0, end, pltpu.roll(x, 1, 0))


def next_lane(x):
    return pltpu.roll(x, x.shape[1] - 1, 1)


def previous_lane(x):
    return pltpu.roll(x, 1, 1)


def eddy_plane(cells, upper, lower, ends, factors, across):
    along = 1 - across
    scaled = [0.25 * factors[k] for k in range(3)]
    carried = [0.125 * cells[k] for k in range(3)]
    up = [scaled[k] - carried[k] for k in range(3)]
    down = [scaled[k] + carried[k] for k in range(3)]
    lanes = rows_of(cells[0].shape, 1)
    up[2] = jnp.where(lanes == C3 - 1, 0.0, up[2])
    down[2] = jnp.where(lanes == 0, 0.0, down[2])
    own = 1.0 - 2.0 * (scaled[0] + scaled[1] + scaled[2])
    results = []
    for v in range(NV):
        cell = cells[v]
        low_end, high_end = ends[v]
        result = own * cell + up[across] * upper[v] + down[across] * lower[v]
        result += up[along] * next_row(cell, high_end) + down[along] * previous_row(cell, low_end)
        result += up[2] * next_lane(cell) + down[2] * previous_lane(cell)
        results.append(result)
    return results


def acoustic_plane(cells, upper, lower, ends, factors, across, source):
    along = 1 - across
    lanes = rows_of(cells[0].shape, 1)
    scaled = [0.125 * factors[k] for k in range(3)]
    change = [[None] * NV for _ in range(3)]
    for v in range(NV):
        cell = cells[v]
        low_end, high_end = ends[v]
        change[across][v] = upper[v] - lower[v]
        change[along][v] = next_row(cell, high_end) - previous_row(cell, low_end)
        change[2][v] = jnp.where(lanes == C3 - 1, 0.0, next_lane(cell)) - jnp.where(
            lanes == 0, 0.0, previous_lane(cell)
        )
    results = []
    for v in range(NV):
        if v == 0:
            coupling = change[0][1] + change[1][2] + change[2][3]
        else:
            coupling = change[v - 1][0]
        result = cells[v] - 0.125 * coupling
        for k in range(3):
            result -= scaled[k] * change[k][v]
        if source is not None:
            result += 0.25 * source[v]
        results.append(result)
    return results


def plane_step(acoustic, cells, upper, lower, ends, factors, across, source):
    if acoustic:
        return acoustic_plane(cells, upper, lower, ends, factors, across, source)
    return eddy_plane(cells, upper, lower, ends, factors, across)


def column(ref, component, j):
    return ref[component, :, j, :]


def pack_halos(q, c, s, low_slab, high_slab, low_sector, high_sector, cells, factors, source, done):
    parts = []
    for v in range(NV):
        parts.append((q.at[v], cells.at[v]))
    for k in range(3):
        parts.append((c.at[k], factors.at[k]))
    for v in range(NV):
        parts.append((s.at[v], source.at[v]))
    copies = [pltpu.make_async_copy(*part, done.at[n]) for n, part in enumerate(parts)]
    for copy in copies:
        copy.start()
    for n, copy in enumerate(copies):
        copy.wait()
        if n < NV:
            ref, component, plane = cells, n, NEAR + n
        elif n < NV + 3:
            ref, component, plane = factors, n - NV, COEF + n - NV
        else:
            ref, component, plane = source, n - NV - 3, SOURCE + n - NV - 3
        low_slab[plane] = ref[component, 0].astype(BF16)
        high_slab[plane] = ref[component, C1 - 1].astype(BF16)
        low_sector[plane] = column(ref, component, 0).astype(BF16)
        high_sector[plane] = column(ref, component, C2 - 1).astype(BF16)
        if n < NV:
            low_slab[FAR + n] = ref[component, 1].astype(BF16)
            high_slab[FAR + n] = ref[component, C1 - 2].astype(BF16)
            low_sector[FAR + n] = column(ref, component, 1).astype(BF16)
            high_sector[FAR + n] = column(ref, component, C2 - 2).astype(BF16)


def fields_of(message, start, count=NV):
    return [message[start + v].astype(F32) for v in range(count)]


def step_rows(acoustic, q, c, s, below, above, ends_of, out):
    def row(i, upper, lower):
        cells = [q[v, i] for v in range(NV)]
        factors = [c[k, i] for k in range(3)]
        source = None if s is None else [s[v, i] for v in range(NV)]
        results = plane_step(acoustic, cells, upper, lower, ends_of(i), factors, 0, source)
        for v in range(NV):
            out[v, i] = results[v]

    row(0, [q[v, 1] for v in range(NV)], below)
    row(C1 - 1, above, [q[v, C1 - 2] for v in range(NV)])

    @pl.loop(1, C1 - 1)
    def _(i):
        row(i, [q[v, i + 1] for v in range(NV)], [q[v, i - 1] for v in range(NV)])


def ends_from(sides):
    def ends_of(i):
        return [(sides[0, v, pl.ds(i, 1), :], sides[1, v, pl.ds(i, 1), :]) for v in range(NV)]

    return ends_of


def first_step(ids, q, c, s, below, above, left, right, stepped, packed, sides, stage):
    section = lax.axis_index("sec")
    slab = lax.axis_index("ax")
    slabs = packed.shape[0] // 2
    for side, message in enumerate((left, right)):
        for v in range(NV):
            sides[side, v] = message[NEAR + v].astype(F32)

    def run(acoustic):
        step_rows(
            acoustic,
            q,
            c,
            s if acoustic else None,
            fields_of(below, NEAR),
            fields_of(above, NEAR),
            ends_from(sides),
            stepped,
        )

    @pl.when(section == 0)
    def _():
        run(False)

        @pl.loop(0, slabs)
        def _(r):
            packed[r] = jnp.zeros(packed.shape[1:], BF16)
            for k in range(CAP):
                block = ids[k, r]
                chosen = jnp.maximum(block, 0)
                i = chosen // (2 * C2)
                j = (chosen // 2) % C2
                for v in range(NV):
                    line = stepped[v, i, pl.ds(j, 1), :]
                    half = jnp.where(chosen % 2 == 0, line[:, :LINE], line[:, LINE:])
                    stage[pl.ds(k * NV + v, 1), :] = jnp.where(block >= 0, half, 0.0)
            packed[slabs + r] = stage[...].astype(BF16)

    @pl.when(section != 0)
    def _():
        run(True)
        packed[...] = jnp.zeros(packed.shape, BF16)

    def send_corners(peer, i):
        rows = []
        for v in range(NV):
            for side in range(2):
                row = sides[side, v, i : i + 1, :]
                rows += [row[:, :LINE], row[:, LINE:]]
        rows.append(jnp.zeros((CAP * NV - len(rows), LINE), F32))
        packed[section * slabs + peer] = jnp.concatenate(rows, axis=0).astype(BF16)

    @pl.when(slab > 0)
    def _():
        send_corners(slab - 1, 0)

    @pl.when(slab < slabs - 1)
    def _():
        send_corners(slab + 1, C1 - 1)


def second_step(stepped, q, c, below, above, left, right, out, paths, rims):
    section = lax.axis_index("sec")
    slab = lax.axis_index("ax")
    slabs = lax.axis_size("ax")

    def run(acoustic):
        nothing = jnp.zeros((1, C3), F32)
        ends = [(nothing, nothing)] * NV

        def rim(message, across, own, side):
            near = fields_of(message, NEAR)
            far = fields_of(message, FAR)
            upper, lower = (own, far) if side == 0 else (far, own)
            source = fields_of(message, SOURCE) if acoustic else None
            factors = fields_of(message, COEF, 3)
            return plane_step(acoustic, near, upper, lower, ends, factors, across, source)

        for side, message in enumerate((left, right)):
            own = [column(q, v, side * (C2 - 1)) for v in range(NV)]
            results = rim(message, 1, own, side)
            for v in range(NV):
                rims[side, v] = results[v]

        for side, message in enumerate((below, above)):
            own = [q[v, side * (C1 - 1)] for v in range(NV)]
            results = rim(message, 0, own, side)
            inside = slab > 0 if side == 0 else slab < slabs - 1
            for v in range(NV):
                rims[2 + side, v] = jnp.where(inside, results[v], 0.0)

        step_rows(
            acoustic,
            stepped,
            c,
            None,
            [rims[2, v] for v in range(NV)],
            [rims[3, v] for v in range(NV)],
            ends_from(rims),
            out,
        )

        for low in range(2):
            for side in range(2):
                i = low * (C1 - 1)
                j = side * (C2 - 1)
                slab_rim = (below, above)[low]
                sector_rim = (left, right)[side]

                def rim_row(message, plane, at):
                    return message[plane].astype(F32)[at : at + 1]

                if acoustic:
                    paths[low, side, 0:1] = 0.125 * rim_row(sector_rim, COEF, i)
                    paths[low, side, 1:2] = 0.125 * c[1, i, j : j + 1]
                    paths[low, side, 2:3] = 0.125 * rim_row(slab_rim, COEF + 1, j)
                    paths[low, side, 3:4] = 0.125 * c[0, i, j : j + 1]
                else:
                    toward_slab = 0.125 - 0.25 * low
                    toward_sector = 0.125 - 0.25 * side
                    over_sector = 0.25 * c[1, i, j : j + 1]
                    over_sector += toward_sector * stepped[1, i, j : j + 1]
                    over_sector *= 0.25 * rim_row(
                        sector_rim, COEF, i
                    ) + toward_slab * rim_row(sector_rim, NEAR, i)
                    over_slab = 0.25 * c[0, i, j : j + 1]
                    over_slab += toward_slab * stepped[0, i, j : j + 1]
                    over_slab *= 0.25 * rim_row(
                        slab_rim, COEF + 1, j
                    ) + toward_sector * rim_row(slab_rim, NEAR + 1, j)
                    paths[low, side, 0:1] = over_sector + over_slab

    @pl.when(section == 0)
    def _():
        run(False)

    @pl.when(section != 0)
    def _():
        run(True)


def coupled(values, factor, k):
    results = [factor * value for value in values]
    results[0] += 0.125 * values[k + 1]
    results[k + 1] += 0.125 * values[0]
    return results


def add_source(targets, weights, received, blocks, base, paths, out, products, sums, total, done):
    section = lax.axis_index("sec")
    slab = lax.axis_index("ax")
    slabs = received.shape[0] // 2

    def corner_terms(acoustic):
        terms = {}
        for low in range(2):
            inside = slab > 0 if low == 0 else slab < slabs - 1
            peer = jnp.clip(slab + 2 * low - 1, 0, slabs - 1)
            rows = received[section * slabs + peer].astype(F32)
            rows = jnp.where(inside, rows, 0.0)
            for side in range(2):
                corner = []
                for v in range(NV):
                    at = 2 * (2 * v + side)
                    corner.append(
                        jnp.concatenate([rows[at : at + 1], rows[at + 1 : at + 2]], axis=1)
                    )
                if not acoustic:
                    terms[low, side] = [paths[low, side, 0:1] * corner[v] for v in range(NV)]
                    continue
                sign = 1.0 if low == side else -1.0
                factors = [paths[low, side, n : n + 1] for n in range(4)]
                over_sector = coupled(coupled(corner, factors[0], 0), factors[1], 1)
                over_slab = coupled(coupled(corner, factors[2], 1), factors[3], 0)
                terms[low, side] = [sign * (a + b) for a, b in zip(over_sector, over_slab)]
        return terms

    def finish(acoustic):
        terms = corner_terms(acoustic)
        copies = []
        for v in range(NV):
            if acoustic:
                for half in range(2):
                    lanes = slice(half * LINE, (half + 1) * LINE)
                    total[v, :, :, lanes] = base[v, :, :, lanes] + 0.25 * sums[half, v]
            else:
                total[v] = base[v]
            for (low, side), term in terms.items():
                j = side * (C2 - 1)
                total[v, low * (C1 - 1), j : j + 1, :] += term[v]
            copies.append(pltpu.make_async_copy(total.at[v], out.at[v], done.at[v]))
            copies[-1].start()
        for copy in copies:
            copy.wait()

    @pl.when(section == 0)
    def _():
        finish(False)

    @pl.when(section != 0)
    def _():
        lines = received[0:slabs].reshape(slabs * CAP * NV, LINE)
        for w in range(NW):
            products[w] = lax.dot_general(
                lines, blocks[w], (((1,), (1,)), ((), ())), preferred_element_type=F32
            )
        sums[...] = jnp.zeros(sums.shape, F32)

        @pl.loop(0, slabs)
        def _(a):
            for k in range(CAP):
                target = targets[k, a]
                w = weights[k, a]
                i = target // (2 * C2)
                j = (target // 2) % C2
                half = target % 2
                held = []
                for v in range(NV):
                    added = products[w, pl.ds(a * (CAP * NV) + k * NV + v, 1), :]
                    held.append(sums[half, v, i, pl.ds(j, 1), :] + added)
                for v in range(NV):
                    sums[half, v, i, pl.ds(j, 1), :] = held[v]

        finish(True)


def shards(fields, coefficients, old_source, weight_blocks, send_ids, target_ids, weight_ids):
    current = fields[0]
    factors = coefficients[0]
    peers = lax.axis_size("sec") * lax.axis_size("ax")
    message = jax.ShapeDtypeStruct((PLANES, C1, C3), BF16)
    field = jax.ShapeDtypeStruct((NV, C1, C2, C3), F32)
    cells = pltpu.VMEM((NV, C1, C2, C3), F32)

    low_slab, high_slab, low_sector, high_sector = pl.pallas_call(
        pack_halos,
        in_specs=[ANY] * 3,
        out_specs=[VMEM] * 4,
        out_shape=[message] * 4,
        scratch_shapes=[
            cells,
            pltpu.VMEM((3, C1, C2, C3), F32),
            cells,
            pltpu.SemaphoreType.DMA((2 * NV + 3,)),
        ],
        compiler_params=PARAMS,
        name="pack_halos",
    )(off_chip(current), off_chip(factors), off_chip(old_source))
    below = shift(high_slab, "ax", 1, False)
    above = shift(low_slab, "ax", -1, False)
    left = shift(high_sector, "az", 1, True)
    right = shift(low_sector, "az", -1, True)

    stepped, packed = pl.pallas_call(
        first_step,
        in_specs=[SMEM] + [VMEM] * 7,
        out_specs=[VMEM] * 2,
        out_shape=[field, pltpu.HBM((peers, CAP * NV, LINE), BF16)],
        scratch_shapes=[pltpu.VMEM((2, NV, C1, C3), F32), pltpu.VMEM((CAP * NV, LINE), F32)],
        compiler_params=PARAMS,
        name="first_step",
    )(
        send_ids[0, 0].T,
        current,
        factors,
        old_source,
        below,
        above,
        left,
        right,
    )
    received = lax.all_to_all(packed, ("sec", "ax"), split_axis=0, concat_axis=0, tiled=True)
    base, paths = pl.pallas_call(
        second_step,
        in_specs=[VMEM] * 7,
        out_specs=[VMEM] * 2,
        out_shape=[
            field,
            jax.ShapeDtypeStruct((2, 2, 8, C3), F32),
        ],
        scratch_shapes=[pltpu.VMEM((4, NV, C1, C3), F32)],
        compiler_params=PARAMS,
        name="second_step",
    )(stepped, off_chip(current), off_chip(factors), below, above, left, right)
    advanced = pl.pallas_call(
        add_source,
        in_specs=[SMEM] * 2 + [VMEM] * 4,
        out_specs=ANY,
        out_shape=jax.ShapeDtypeStruct((NV, C1, C2, C3), F32),
        scratch_shapes=[
            pltpu.VMEM((NW, peers // 2 * CAP * NV, LINE), F32),
            pltpu.VMEM((2, NV, C1, C2, LINE), F32),
            cells,
            pltpu.SemaphoreType.DMA((NV,)),
        ],
        compiler_params=PARAMS,
        name="add_source",
    )(
        target_ids[0, 0].T,
        weight_ids[0, 0].T,
        received,
        weight_blocks[0, 0],
        base,
        paths,
    )
    return advanced[None]


def solution(mesh):
    return jax.shard_map(
        shards,
        mesh=mesh,
        in_specs=(
            P("sec", None, "ax", "az", None),
            P("sec", None, "ax", "az", None),
            P(None, "ax", "az", None),
            P("ax", "az", None, None, None),
            P("ax", "az", None, None),
            P("ax", "az", None, None),
            P("ax", "az", None, None),
        ),
        out_specs=P("sec", None, "ax", "az", None),
        check_vma=False,
    )
```

time: 65.3 us -> 55.2 us (0.85)
  Pallas kernels: 18.1 us -> 11.8 us
  starting transfers between devices: 32.1 us -> 30.5 us
  local copies, waits for them, and re-layouts: 2.01 us -> 0.72 us
  other arithmetic: 0.67 us -> 0 us
    pallas_call x5 -> x4, Pallas kernels: 18.1 us -> 11.8 us  [the longest x1 4.62 us: shards(): pl.pallas_call(first_step, in_specs=[SMEM] + [VMEM] * 7, out_specs=[VMEM]...]
    ppermute x4, starting transfers between devices: 23.4 us -> 20 us  [shift(): return lax.ppermute(x, axis, pairs)]
    all_to_all x1, starting transfers between devices: 8.68 us -> 10.5 us  [shards(): lax.all_to_all(packed, ('sec', 'ax'), split_axis=0, concat_axis=0, tiled=...]
    unnamed x10 -> x14, local copies, waits for them, and re-layouts: 2.01 us -> 0.72 us
    ppermute x4, waiting for transfers between devices: 2.72 us -> 1.83 us  [shift(): return lax.ppermute(x, axis, pairs)]
    another operation x1 -> x0, other arithmetic: 0.67 us -> none  [shards(): jnp.stack([lax.axis_index('sec'), lax.axis_index('ax'), jnp.int32(lax.axi...]
  transfers between devices with their start and end apart: 5 -> 5, of which waited for: 3 -> 3; matrix products, arithmetic and copies ran while one was open for 1% -> 0% of each run, Pallas kernels for 6% -> 6%
where the time goes in v2:
time: 55.2 us; the launch traced here: 54.9 us
  starting transfers between devices  30.5 us (55%)
  Pallas kernels  11.8 us (21%)
  waiting for transfers between devices  11.8 us (21%)
  local copies, waits for them, and re-layouts  0.72 us (1%)
    ppermute x4, starting transfers between devices, shift(): return lax.ppermute(x, axis, pairs)  20 us
    all_to_all x1, starting transfers between devices, shards(): lax.all_to_all(packed, ('sec', 'ax'), split_axis=0, concat_axis=0, tiled=...  10.5 us
    all_to_all x1, waiting for transfers between devices, shards(): lax.all_to_all(packed, ('sec', 'ax'), split_axis=0, concat_axis=0, tiled=...  9.96 us
    pallas_call x1, Pallas kernels, shards(): pl.pallas_call(first_step, in_specs=[SMEM] + [VMEM] * 7, out_specs=[VMEM]...  4.62 us
    pallas_call x1, Pallas kernels, shards(): pl.pallas_call(second_step, in_specs=[VMEM] * 7, out_specs=[VMEM] * 2, ou...  3.44 us
    pallas_call x1, Pallas kernels, shards(): pl.pallas_call(pack_halos, in_specs=[ANY] * 3, out_specs=[VMEM] * 4, out_...  2.02 us
    ppermute x4, waiting for transfers between devices, shift(): return lax.ppermute(x, axis, pairs)  1.83 us
    pallas_call x1, Pallas kernels, shards(): pl.pallas_call(add_source, in_specs=[SMEM] * 2 + [VMEM] * 4, out_specs=AN...  1.69 us
  transfers between devices with their start and end apart: 5, of which 3 were waited for; matrix products, arithmetic and copies ran while one was open for 0% of the time, Pallas kernels for 6%

profile of v2, /device:TPU:1, one launch (start us, length us, event | category | flops | bytes accessed | tf_op | source)
XLA Modules:
  0.0 54.9 jit_solution(15803802326523511849)
XLA Ops:
  0.0 0.0 copy-start
  0.0 0.0 copy-start.1
  0.0 0.0 copy-start.2
  0.0 2.0 %pack_halos.1 = (bf16[15,16,256]{2,1,0:T(8,128)(2,1)S(1)}, bf16[15,16,256]{2,1,0:T(8,128)(2,1)S(1)}, bf16[15,16,256]{2,1,0:T(8,128)(2,1)S(1)}, bf16[15,16,256]{2,1,0:T(8,128)(2,1)S(1)}) custom-call(f32[4,16,16,256]{3,2,1,0:T(8,128)} %bitcast.13, f32[3,16,16,256]{3,2,1,0:T(8,128)} %bitcast.16, f32[4,16,16,256]{3,2,1,0:T(8,128)} %s.3), custom_call_target="tpu_custom_call" | custom-call | tf_op jit(solution)/shard_map/pack_halos/pallas_call | solution.py:411
  2.0 0.0 copy-start.4
  2.1 4.6 %collective-permute-start = (bf16[15,16,256]{2,1,0:T(8,128)(2,1)S(1)}, bf16[15,16,256]{2,1,0:T(8,128)(2,1)S(1)}, u32[]{:S(2)}, u32[]{:S(2)}) collective-permute-start(bf16[15,16,256]{2,1,0:T(8,128)(2,1)S(1)} %get-tuple-element.13), channel_id=1, source_target_pairs={{0,16},{16,32},{32,48},{48,64},{64,80},{80,96},{96,112},{112,128},... | collective-permute-start | bytes 368648 | tf_op jit(solution)/shard_map/ppermute | solution.py:37
  6.7 5.5 %collective-permute-start.1 = (bf16[15,16,256]{2,1,0:T(8,128)(2,1)S(1)}, bf16[15,16,256]{2,1,0:T(8,128)(2,1)S(1)}, u32[]{:S(2)}, u32[]{:S(2)}) collective-permute-start(bf16[15,16,256]{2,1,0:T(8,128)(2,1)S(1)} %get-tuple-element.14), channel_id=1, source_target_pairs={{16,0},{32,16},{48,32},{64,48},{80,64},{96,80},{112,96},{128,112},... | collective-permute-start | bytes 368648 | tf_op jit(solution)/shard_map/ppermute | solution.py:37
  12.1 1.9 %collective-permute-start.2 = (bf16[15,16,256]{2,1,0:T(8,128)(2,1)S(1)}, bf16[15,16,256]{2,1,0:T(8,128)(2,1)S(1)}, u32[]{:S(2)}, u32[]{:S(2)}) collective-permute-start(bf16[15,16,256]{2,1,0:T(8,128)(2,1)S(1)} %get-tuple-element.15), channel_id=1, source_target_pairs={{0,1},{1,2},{2,3},{3,4},{4,5},{5,6},{6,7},{7,8},{8,9},{9,10},{10,1... | collective-permute-start | bytes 368648 | tf_op jit(solution)/shard_map/ppermute | solution.py:37
  14.1 8.0 %collective-permute-start.3 = (bf16[15,16,256]{2,1,0:T(8,128)(2,1)S(1)}, bf16[15,16,256]{2,1,0:T(8,128)(2,1)S(1)}, u32[]{:S(2)}, u32[]{:S(2)}) collective-permute-start(bf16[15,16,256]{2,1,0:T(8,128)(2,1)S(1)} %get-tuple-element.16), channel_id=1, source_target_pairs={{0,15},{1,0},{2,1},{3,2},{4,3},{5,4},{6,5},{7,6},{8,7},{9,8},{10,9... | collective-permute-start | bytes 368648 | tf_op jit(solution)/shard_map/ppermute | solution.py:37
  22.1 0.0 collective-permute-done.below
  22.1 0.0 collective-permute-done.1.above
  22.1 0.3 collective-permute-done.2.left
  22.4 1.5 %collective-permute-done.3.right = bf16[15,16,256]{2,1,0:T(8,128)(2,1)S(1)} collective-permute-done((bf16[15,16,256]{2,1,0:T(8,128)(2,1)S(1)}, bf16[15,16,256]{2,1,0:T(8,128)(2,1)S(1)}, u32[]{:S(2)}, u32[]{:S(2)}) %collective-permute-start.3) | collective-permute-done | bytes 122912 | tf_op jit(solution)/shard_map/ppermute | solution.py:37
  24.0 0.0 copy-done
  24.0 0.0 copy-done.1
  24.0 0.0 copy-done.2
  24.0 0.0 copy-done.4
  24.0 4.6 %first_step.1 = (f32[4,16,16,256]{3,2,1,0:T(8,128)S(1)}, bf16[32,32,128]{2,1,0:T(8,128)(2,1)}) custom-call(s32[8,16]{1,0:T(8,128)S(1)} %bitcast.20, f32[4,16,16,256]{3,2,1,0:T(8,128)S(1)} %bitcast.15, f32[3,16,16,256]{3,2,1,0:T(8,128)S(1)} %bitcast.18, f32[4,16,16,256]{3,2,1,0:T(8,128)S(1)} %copy-done.2, ...), custom_call_target="tpu_custom_call" | custom-call | tf_op jit(solution)/shard_map/first_step/pallas_call | solution.py:430
  28.6 10.5 %all-to-all-start = ((bf16[32,32,128]{2,1,0:T(8,128)(2,1)}), bf16[32,32,128]{2,1,0:T(8,128)(2,1)S(1)}, u32[]{:S(2)}, u32[]{:S(2)}) async-start(bf16[32,32,128]{2,1,0:T(8,128)(2,1)} %get-tuple-element.17), calls=%async_computation | async-start | bytes 524288 | tf_op jit(solution)/shard_map/all_to_all | solution.py:448
  39.1 0.0 copy-start.3
  39.1 3.4 %second_step.1 = (f32[4,16,16,256]{3,2,1,0:T(8,128)S(1)}, f32[2,2,8,256]{3,2,1,0:T(8,128)S(1)}) custom-call(f32[4,16,16,256]{3,2,1,0:T(8,128)S(1)} %get-tuple-element.18.stepped, f32[4,16,16,256]{3,2,1,0:T(8,128)} %bitcast.14, f32[3,16,16,256]{3,2,1,0:T(8,128)} %bitcast.17, bf16[15,16,256]{2,1,0:T(8,128)(2,1)S(1)} %collective-permute-done.below, ...), custom_call_target="tpu_custom_call" | custom-call | tf_op jit(solution)/shard_map/second_step/pallas_call | solution.py:449
  42.5 10.0 %all-to-all-done.received = bf16[32,32,128]{2,1,0:T(8,128)(2,1)S(1)} async-done(((bf16[32,32,128]{2,1,0:T(8,128)(2,1)}), bf16[32,32,128]{2,1,0:T(8,128)(2,1)S(1)}, u32[]{:S(2)}, u32[]{:S(2)}) %all-to-all-start) | async-done | bytes 262176 | tf_op jit(solution)/shard_map/all_to_all | solution.py:448
  52.5 0.0 copy-start.6
  52.5 0.0 copy-start.5
  52.5 0.0 copy-done.3
  52.5 0.7 %copy-done.6 = s32[1,1,16,8]{2,3,1,0:T(8,128)S(1)} copy-done((s32[1,1,16,8]{2,3,1,0:T(8,128)S(1)}, s32[1,1,16,8]{2,3,1,0:T(8,128)}, u32[]{:S(2)}) %copy-start.6) | copy-done | bytes 536
  53.2 0.0 copy-done.5
  53.2 1.7 %add_source.1 = f32[4,16,16,256]{3,2,1,0:T(8,128)} custom-call(s32[8,16]{1,0:T(8,128)S(1)} %bitcast.21, s32[8,16]{1,0:T(8,128)S(1)} %bitcast.22, bf16[32,32,128]{2,1,0:T(8,128)(2,1)S(1)} %all-to-all-done.received, bf16[8,128,128]{2,1,0:T(8,128)(2,1)S(1)} %bitcast.19, f32[4,16,16,256]{3,2,1,0:T(8,128)S(1)} %get-tuple-element.19.base, ...), custom_call_target="tpu_custom_call" | custom-call | tf_op jit(solution)/shard_map/add_source/pallas_call | solution.py:461
Async XLA Ops:
  0.0 24.0 %copy-start = (f32[1,4,16,16,256]{4,3,2,1,0:T(8,128)S(1)}, f32[1,4,16,16,256]{4,3,2,1,0:T(8,128)}, u32[]{:S(2)}) copy-start(f32[1,4,16,16,256]{4,3,2,1,0:T(8,128)} %param.7) | copy-start | bytes 3145732
  0.0 24.0 %copy-start.1 = (f32[1,3,16,16,256]{4,3,2,1,0:T(8,128)S(1)}, f32[1,3,16,16,256]{4,3,2,1,0:T(8,128)}, u32[]{:S(2)}) copy-start(f32[1,3,16,16,256]{4,3,2,1,0:T(8,128)} %param.8) | copy-start | bytes 2359300
  0.0 24.0 %copy-start.2 = (f32[4,16,16,256]{3,2,1,0:T(8,128)S(1)}, f32[4,16,16,256]{3,2,1,0:T(8,128)}, u32[]{:S(2)}) copy-start(f32[4,16,16,256]{3,2,1,0:T(8,128)} %s.3) | copy-start | bytes 3145732
  2.0 21.9 %copy-start.4 = (s32[1,1,16,8]{2,3,1,0:T(8,128)S(1)}, s32[1,1,16,8]{2,3,1,0:T(8,128)}, u32[]{:S(2)}) copy-start(s32[1,1,16,8]{2,3,1,0:T(8,128)} %param.11) | copy-start | bytes 1540
  2.1 20.1 %collective-permute-start = (bf16[15,16,256]{2,1,0:T(8,128)(2,1)S(1)}, bf16[15,16,256]{2,1,0:T(8,128)(2,1)S(1)}, u32[]{:S(2)}, u32[]{:S(2)}) collective-permute-start(bf16[15,16,256]{2,1,0:T(8,128)(2,1)S(1)} %get-tuple-element.13), channel_id=1, source_target_pairs={{0,16},{16,32},{32,48},{48,64},{64,80},{80,96},{96,112},{112,128},... | collective-permute-start | bytes 368648 | tf_op jit(solution)/shard_map/ppermute | solution.py:37
  6.7 15.5 %collective-permute-start.1 = (bf16[15,16,256]{2,1,0:T(8,128)(2,1)S(1)}, bf16[15,16,256]{2,1,0:T(8,128)(2,1)S(1)}, u32[]{:S(2)}, u32[]{:S(2)}) collective-permute-start(bf16[15,16,256]{2,1,0:T(8,128)(2,1)S(1)} %get-tuple-element.14), channel_id=1, source_target_pairs={{16,0},{32,16},{48,32},{64,48},{80,64},{96,80},{112,96},{128,112},... | collective-permute-start | bytes 368648 | tf_op jit(solution)/shard_map/ppermute | solution.py:37
  12.1 10.3 %collective-permute-start.2 = (bf16[15,16,256]{2,1,0:T(8,128)(2,1)S(1)}, bf16[15,16,256]{2,1,0:T(8,128)(2,1)S(1)}, u32[]{:S(2)}, u32[]{:S(2)}) collective-permute-start(bf16[15,16,256]{2,1,0:T(8,128)(2,1)S(1)} %get-tuple-element.15), channel_id=1, source_target_pairs={{0,1},{1,2},{2,3},{3,4},{4,5},{5,6},{6,7},{7,8},{8,9},{9,10},{10,1... | collective-permute-start | bytes 368648 | tf_op jit(solution)/shard_map/ppermute | solution.py:37
  14.1 9.9 %collective-permute-start.3 = (bf16[15,16,256]{2,1,0:T(8,128)(2,1)S(1)}, bf16[15,16,256]{2,1,0:T(8,128)(2,1)S(1)}, u32[]{:S(2)}, u32[]{:S(2)}) collective-permute-start(bf16[15,16,256]{2,1,0:T(8,128)(2,1)S(1)} %get-tuple-element.16), channel_id=1, source_target_pairs={{0,15},{1,0},{2,1},{3,2},{4,3},{5,4},{6,5},{7,6},{8,7},{9,8},{10,9... | collective-permute-start | bytes 368648 | tf_op jit(solution)/shard_map/ppermute | solution.py:37
  28.6 23.9 %all-to-all-start = ((bf16[32,32,128]{2,1,0:T(8,128)(2,1)}), bf16[32,32,128]{2,1,0:T(8,128)(2,1)S(1)}, u32[]{:S(2)}, u32[]{:S(2)}) async-start(bf16[32,32,128]{2,1,0:T(8,128)(2,1)} %get-tuple-element.17), calls=%async_computation | async-start | bytes 524288 | tf_op jit(solution)/shard_map/all_to_all | solution.py:448
  39.1 13.4 %copy-start.3 = (bf16[1,1,8,128,128]{4,3,2,1,0:T(8,128)(2,1)S(1)}, bf16[1,1,8,128,128]{4,3,2,1,0:T(8,128)(2,1)}, u32[]{:S(2)}) copy-start(bf16[1,1,8,128,128]{4,3,2,1,0:T(8,128)(2,1)} %param.10) | copy-start | bytes 786436
  52.5 0.7 %copy-start.6 = (s32[1,1,16,8]{2,3,1,0:T(8,128)S(1)}, s32[1,1,16,8]{2,3,1,0:T(8,128)}, u32[]{:S(2)}) copy-start(s32[1,1,16,8]{2,3,1,0:T(8,128)} %param.13) | copy-start | bytes 1540
  52.5 0.7 %copy-start.5 = (s32[1,1,16,8]{2,3,1,0:T(8,128)S(1)}, s32[1,1,16,8]{2,3,1,0:T(8,128)}, u32[]{:S(2)}) copy-start(s32[1,1,16,8]{2,3,1,0:T(8,128)} %param.12) | copy-start | bytes 1540

commit v3 on v2

--- a/solution.py
+++ b/solution.py
@@ -167,14 +167,40 @@
         row(i, [q[v, i + 1] for v in range(NV)], [q[v, i - 1] for v in range(NV)])
 
 
-def ends_from(sides):
-    def ends_of(i):
-        return [(sides[0, v, pl.ds(i, 1), :], sides[1, v, pl.ds(i, 1), :]) for v in range(NV)]
-
-    return ends_of
-
-
-def first_step(ids, q, c, s, below, above, left, right, stepped, packed, sides, stage):
+def no_ends(i):
+    nothing = jnp.zeros((1, C3), F32)
+    return [(nothing, nothing)] * NV
+
+
+def inner_step(q, c, s, out):
+    section = lax.axis_index("sec")
+    nothing = [jnp.zeros((C2, C3), F32)] * NV
+
+    @pl.when(section == 0)
+    def _():
+        step_rows(False, q, c, None, nothing, nothing, no_ends, out)
+
+    @pl.when(section != 0)
+    def _():
+        step_rows(True, q, c, s, nothing, nothing, no_ends, out)
+
+
+def coupled(values, factor, k):
+    results = [factor * value for value in values]
+    results[0] += 0.125 * values[k + 1]
+    results[k + 1] += 0.125 * values[0]
+    return results
+
+
+def border_terms(acoustic, near, flow, factor, k, side):
+    sign = 1.0 - 2.0 * side
+    if acoustic:
+        return [sign * term for term in coupled(near, 0.125 * factor, k)]
+    weight = 0.25 * factor + (sign * 0.125) * flow
+    return [weight * value for value in near]
+
+
+def first_step(ids, inner, q, c, below, above, left, right, stepped, packed, sides):
     section = lax.axis_index("sec")
     slab = lax.axis_index("ax")
     slabs = packed.shape[0] // 2
@@ -182,40 +208,47 @@
         for v in range(NV):
             sides[side, v] = message[NEAR + v].astype(F32)
 
-    def run(acoustic):
-        step_rows(
-            acoustic,
-            q,
-            c,
-            s if acoustic else None,
-            fields_of(below, NEAR),
-            fields_of(above, NEAR),
-            ends_from(sides),
-            stepped,
-        )
+    def add_borders(acoustic):
+        for side, message in enumerate((below, above)):
+            i = side * (C1 - 1)
+            near = fields_of(message, NEAR)
+            terms = border_terms(acoustic, near, q[0, i], c[0, i], 0, side)
+            for v in range(NV):
+                stepped[v, i] += terms[v]
+        for i in range(C1):
+            for side in range(2):
+                j = side * (C2 - 1)
+                near = [sides[side, v, i : i + 1, :] for v in range(NV)]
+                flow = q[1, i, j : j + 1, :]
+                factor = c[1, i, j : j + 1, :]
+                terms = border_terms(acoustic, near, flow, factor, 1, side)
+                for v in range(NV):
+                    stepped[v, i, j : j + 1, :] += terms[v]
 
     @pl.when(section == 0)
     def _():
-        run(False)
-
-        @pl.loop(0, slabs)
-        def _(r):
-            packed[r] = jnp.zeros(packed.shape[1:], BF16)
-            for k in range(CAP):
-                block = ids[k, r]
-                chosen = jnp.maximum(block, 0)
-                i = chosen // (2 * C2)
-                j = (chosen // 2) % C2
-                for v in range(NV):
-                    line = stepped[v, i, pl.ds(j, 1), :]
-                    half = jnp.where(chosen % 2 == 0, line[:, :LINE], line[:, LINE:])
-                    stage[pl.ds(k * NV + v, 1), :] = jnp.where(block >= 0, half, 0.0)
-            packed[slabs + r] = stage[...].astype(BF16)
+        add_borders(False)
+
+        listed = ids[...]
+        columns = [listed[:, r : r + 1] for r in range(slabs)]
+        lanes = rows_of((CAP, C1 * C2), 1)
+        chosen = [jnp.where(lanes == (column >> 1), 1.0, 0.0) for column in columns]
+        chosen = jnp.concatenate(chosen, axis=0).astype(BF16)
+        picked = []
+        for v in range(NV):
+            cells = stepped[v].astype(BF16).reshape(C1 * C2, C3)
+            picked.append(jnp.dot(chosen, cells, preferred_element_type=F32))
+        for r in range(slabs):
+            odd = jnp.broadcast_to(columns[r] & 1, (CAP, LINE)) == 1
+            rows = []
+            for v in range(NV):
+                both = picked[v][r * CAP : (r + 1) * CAP]
+                rows.append(jnp.where(odd, both[:, LINE:], both[:, :LINE]))
+            packed[slabs + r] = jnp.concatenate(rows, axis=0).astype(BF16)
 
     @pl.when(section != 0)
     def _():
-        run(True)
-        packed[...] = jnp.zeros(packed.shape, BF16)
+        add_borders(True)
 
     def send_corners(peer, i):
         rows = []
@@ -233,6 +266,13 @@
     @pl.when(slab < slabs - 1)
     def _():
         send_corners(slab + 1, C1 - 1)
+
+
+def ends_from(sides):
+    def ends_of(i):
+        return [(sides[0, v, pl.ds(i, 1), :], sides[1, v, pl.ds(i, 1), :]) for v in range(NV)]
+
+    return ends_of
 
 
 def second_step(stepped, q, c, below, above, left, right, out, paths, rims):
@@ -315,14 +355,7 @@
         run(True)
 
 
-def coupled(values, factor, k):
-    results = [factor * value for value in values]
-    results[0] += 0.125 * values[k + 1]
-    results[k + 1] += 0.125 * values[0]
-    return results
-
-
-def add_source(targets, weights, received, blocks, base, paths, out, products, sums, total, done):
+def add_source(targets, weights, received, blocks, base, paths, out, total, done):
     section = lax.axis_index("sec")
     slab = lax.axis_index("ax")
     slabs = received.shape[0] // 2
@@ -351,14 +384,15 @@
                 terms[low, side] = [sign * (a + b) for a, b in zip(over_sector, over_slab)]
         return terms
 
-    def finish(acoustic):
+    def finish(acoustic, added):
         terms = corner_terms(acoustic)
         copies = []
         for v in range(NV):
             if acoustic:
                 for half in range(2):
                     lanes = slice(half * LINE, (half + 1) * LINE)
-                    total[v, :, :, lanes] = base[v, :, :, lanes] + 0.25 * sums[half, v]
+                    part = added[half][:, v * LINE : (v + 1) * LINE].reshape(C1, C2, LINE)
+                    total[v, :, :, lanes] = base[v, :, :, lanes] + part
             else:
                 total[v] = base[v]
             for (low, side), term in terms.items():
@@ -371,33 +405,44 @@
 
     @pl.when(section == 0)
     def _():
-        finish(False)
+        finish(False, None)
 
     @pl.when(section != 0)
     def _():
-        lines = received[0:slabs].reshape(slabs * CAP * NV, LINE)
+        kinds = weights[...]
+        masks = []
+        for a in range(slabs):
+            kind = jnp.broadcast_to(kinds[:, a : a + 1], (CAP, LINE))
+            masks.append(jnp.concatenate([kind] * NV, axis=0))
+        placed = []
         for w in range(NW):
-            products[w] = lax.dot_general(
-                lines, blocks[w], (((1,), (1,)), ((), ())), preferred_element_type=F32
-            )
-        sums[...] = jnp.zeros(sums.shape, F32)
-
-        @pl.loop(0, slabs)
-        def _(a):
-            for k in range(CAP):
-                target = targets[k, a]
-                w = weights[k, a]
-                i = target // (2 * C2)
-                j = (target // 2) % C2
-                half = target % 2
-                held = []
-                for v in range(NV):
-                    added = products[w, pl.ds(a * (CAP * NV) + k * NV + v, 1), :]
-                    held.append(sums[half, v, i, pl.ds(j, 1), :] + added)
-                for v in range(NV):
-                    sums[half, v, i, pl.ds(j, 1), :] = held[v]
-
-        finish(True)
+            parts = []
+            for a in range(slabs):
+                parts.append(jnp.where(masks[a] == w, 1.0, 0.0).astype(BF16) * received[a])
+            placed.append(jnp.concatenate(parts, axis=0))
+        placed = jnp.concatenate(placed, axis=1)
+        stacked = jnp.concatenate([blocks[w] for w in range(NW)], axis=1)
+        products = lax.dot_general(
+            placed, stacked, (((1,), (1,)), ((), ())), preferred_element_type=F32
+        )
+        lines = []
+        for v in range(NV):
+            rows = []
+            for a in range(slabs):
+                start = (a * NV + v) * CAP
+                rows.append(products[start : start + CAP])
+            lines.append(jnp.concatenate(rows, axis=0))
+        lines = jnp.concatenate(lines, axis=1)
+        high = lines.astype(BF16)
+        low = (lines - high.astype(F32)).astype(BF16)
+        lines = jnp.concatenate([high, low], axis=0)
+        wanted = jnp.concatenate([targets[...]] * 2, axis=1)
+        added = []
+        for half in range(2):
+            here = 2 * rows_of((C1 * C2, lines.shape[0]), 0) + half
+            chosen = jnp.where(here == wanted, 0.25, 0.0).astype(BF16)
+            added.append(jnp.dot(chosen, lines, preferred_element_type=F32))
+        finish(True, added)
 
 
 def shards(fields, coefficients, old_source, weight_blocks, send_ids, target_ids, weight_ids):
@@ -427,24 +472,24 @@
     left = shift(high_sector, "az", 1, True)
     right = shift(low_sector, "az", -1, True)
 
+    inner = pl.pallas_call(
+        inner_step,
+        in_specs=[VMEM] * 3,
+        out_specs=VMEM,
+        out_shape=field,
+        compiler_params=PARAMS,
+        name="inner_step",
+    )(current, factors, old_source)
     stepped, packed = pl.pallas_call(
         first_step,
-        in_specs=[SMEM] + [VMEM] * 7,
+        in_specs=[VMEM] * 8,
         out_specs=[VMEM] * 2,
         out_shape=[field, pltpu.HBM((peers, CAP * NV, LINE), BF16)],
-        scratch_shapes=[pltpu.VMEM((2, NV, C1, C3), F32), pltpu.VMEM((CAP * NV, LINE), F32)],
+        input_output_aliases={1: 0},
+        scratch_shapes=[pltpu.VMEM((2, NV, C1, C3), F32)],
         compiler_params=PARAMS,
         name="first_step",
-    )(
-        send_ids[0, 0].T,
-        current,
-        factors,
-        old_source,
-        below,
-        above,
-        left,
-        right,
-    )
+    )(send_ids[0, 0].T, inner, current, factors, below, above, left, right)
     received = lax.all_to_all(packed, ("sec", "ax"), split_axis=0, concat_axis=0, tiled=True)
     base, paths = pl.pallas_call(
         second_step,
@@ -460,19 +505,14 @@
     )(stepped, off_chip(current), off_chip(factors), below, above, left, right)
     advanced = pl.pallas_call(
         add_source,
-        in_specs=[SMEM] * 2 + [VMEM] * 4,
+        in_specs=[VMEM] * 6,
         out_specs=ANY,
         out_shape=jax.ShapeDtypeStruct((NV, C1, C2, C3), F32),
-        scratch_shapes=[
-            pltpu.VMEM((NW, peers // 2 * CAP * NV, LINE), F32),
-            pltpu.VMEM((2, NV, C1, C2, LINE), F32),
-            cells,
-            pltpu.SemaphoreType.DMA((NV,)),
-        ],
+        scratch_shapes=[cells, pltpu.SemaphoreType.DMA((NV,))],
         compiler_params=PARAMS,
         name="add_source",
     )(
-        target_ids[0, 0].T,
+        target_ids.reshape(1, -1),
         weight_ids[0, 0].T,
         received,
         weight_blocks[0, 0],

time: 55.2 us -> 51.8 us (0.938)
  Pallas kernels: 11.8 us -> 9.2 us
  waiting for transfers between devices: 11.8 us -> 9.96 us
  starting transfers between devices: 30.5 us -> 32 us
    pallas_call x2 -> x3, Pallas kernels: 6.3 us -> 3.76 us  [the longest x1 1.61 us: shards(): pl.pallas_call(inner_step, in_specs=[VMEM] * 3, out_specs=VMEM, out_shape...]
    ppermute x4, waiting for transfers between devices: 1.83 us -> 0.16 us  [shift(): return lax.ppermute(x, axis, pairs)]
    all_to_all x1, starting transfers between devices: 10.5 us -> 11.9 us  [shards(): lax.all_to_all(packed, ('sec', 'ax'), split_axis=0, concat_axis=0, tiled=...]
    unnamed x14 -> x15, local copies, waits for them, and re-layouts: 0.72 us -> 0.11 us
  transfers between devices with their start and end apart: 5 -> 5, of which waited for: 3 -> 2; matrix products, arithmetic and copies ran while one was open for 0% -> 0% of each run, Pallas kernels for 6% -> 10%
where the time goes in v3:
time: 51.8 us; the launch traced here: 51.5 us
  starting transfers between devices  32 us (62%)
  waiting for transfers between devices  9.96 us (19%)
  Pallas kernels  9.2 us (18%)
    ppermute x4, starting transfers between devices, shift(): return lax.ppermute(x, axis, pairs)  20 us
    all_to_all x1, starting transfers between devices, shards(): lax.all_to_all(packed, ('sec', 'ax'), split_axis=0, concat_axis=0, tiled=...  11.9 us
    all_to_all x1, waiting for transfers between devices, shards(): lax.all_to_all(packed, ('sec', 'ax'), split_axis=0, concat_axis=0, tiled=...  9.8 us
    pallas_call x1, Pallas kernels, shards(): pl.pallas_call(second_step, in_specs=[VMEM] * 7, out_specs=[VMEM] * 2, ou...  3.42 us
    pallas_call x1, Pallas kernels, shards(): pl.pallas_call(pack_halos, in_specs=[ANY] * 3, out_specs=[VMEM] * 4, out_...  2.02 us
    pallas_call x1, Pallas kernels, shards(): pl.pallas_call(inner_step, in_specs=[VMEM] * 3, out_specs=VMEM, out_shape...  1.61 us
    pallas_call x1, Pallas kernels, shards(): pl.pallas_call(first_step, in_specs=[VMEM] * 8, out_specs=[VMEM] * 2, out...  1.12 us
  transfers between devices with their start and end apart: 5, of which 2 were waited for; matrix products, arithmetic and copies ran while one was open for 0% of the time, Pallas kernels for 10%

profile of v3, /device:TPU:1, one launch (start us, length us, event | category | flops | bytes accessed | tf_op | source)
XLA Modules:
  0.0 51.5 jit_solution(16759324531107387876)
XLA Ops:
  0.0 0.0 copy-start
  0.0 0.0 copy-start.1
  0.0 0.0 copy-start.2
  0.0 2.0 %pack_halos.1 = (bf16[15,16,256]{2,1,0:T(8,128)(2,1)S(1)}, bf16[15,16,256]{2,1,0:T(8,128)(2,1)S(1)}, bf16[15,16,256]{2,1,0:T(8,128)(2,1)S(1)}, bf16[15,16,256]{2,1,0:T(8,128)(2,1)S(1)}) custom-call(f32[4,16,16,256]{3,2,1,0:T(8,128)} %bitcast.12, f32[3,16,16,256]{3,2,1,0:T(8,128)} %bitcast.16, f32[4,16,16,256]{3,2,1,0:T(8,128)} %s.3), custom_call_target="tpu_custom_call" | custom-call | tf_op jit(solution)/shard_map/pack_halos/pallas_call | solution.py:456
  2.0 4.6 %collective-permute-start = (bf16[15,16,256]{2,1,0:T(8,128)(2,1)S(1)}, bf16[15,16,256]{2,1,0:T(8,128)(2,1)S(1)}, u32[]{:S(2)}, u32[]{:S(2)}) collective-permute-start(bf16[15,16,256]{2,1,0:T(8,128)(2,1)S(1)} %get-tuple-element.13), channel_id=1, source_target_pairs={{0,16},{16,32},{32,48},{48,64},{64,80},{80,96},{96,112},{112,128},... | collective-permute-start | bytes 368648 | tf_op jit(solution)/shard_map/ppermute | solution.py:37
  6.6 5.5 %collective-permute-start.1 = (bf16[15,16,256]{2,1,0:T(8,128)(2,1)S(1)}, bf16[15,16,256]{2,1,0:T(8,128)(2,1)S(1)}, u32[]{:S(2)}, u32[]{:S(2)}) collective-permute-start(bf16[15,16,256]{2,1,0:T(8,128)(2,1)S(1)} %get-tuple-element.14), channel_id=1, source_target_pairs={{16,0},{32,16},{48,32},{64,48},{80,64},{96,80},{112,96},{128,112},... | collective-permute-start | bytes 368648 | tf_op jit(solution)/shard_map/ppermute | solution.py:37
  12.1 1.9 %collective-permute-start.2 = (bf16[15,16,256]{2,1,0:T(8,128)(2,1)S(1)}, bf16[15,16,256]{2,1,0:T(8,128)(2,1)S(1)}, u32[]{:S(2)}, u32[]{:S(2)}) collective-permute-start(bf16[15,16,256]{2,1,0:T(8,128)(2,1)S(1)} %get-tuple-element.15), channel_id=1, source_target_pairs={{0,1},{1,2},{2,3},{3,4},{4,5},{5,6},{6,7},{7,8},{8,9},{9,10},{10,1... | collective-permute-start | bytes 368648 | tf_op jit(solution)/shard_map/ppermute | solution.py:37
  14.1 8.0 %collective-permute-start.3 = (bf16[15,16,256]{2,1,0:T(8,128)(2,1)S(1)}, bf16[15,16,256]{2,1,0:T(8,128)(2,1)S(1)}, u32[]{:S(2)}, u32[]{:S(2)}) collective-permute-start(bf16[15,16,256]{2,1,0:T(8,128)(2,1)S(1)} %get-tuple-element.16), channel_id=1, source_target_pairs={{0,15},{1,0},{2,1},{3,2},{4,3},{5,4},{6,5},{7,6},{8,7},{9,8},{10,9... | collective-permute-start | bytes 368648 | tf_op jit(solution)/shard_map/ppermute | solution.py:37
  22.1 0.0 copy-done
  22.1 0.0 copy-done.1
  22.1 0.0 copy-done.2
  22.1 0.0 copy-start.4
  22.1 1.6 %inner_step.1.inner = f32[4,16,16,256]{3,2,1,0:T(8,128)S(1)} custom-call(f32[4,16,16,256]{3,2,1,0:T(8,128)S(1)} %bitcast.14, f32[3,16,16,256]{3,2,1,0:T(8,128)S(1)} %bitcast.18, f32[4,16,16,256]{3,2,1,0:T(8,128)S(1)} %copy-done.2), custom_call_target="tpu_custom_call" | custom-call | tf_op jit(solution)/shard_map/inner_step/pallas_call | solution.py:475
  23.8 0.0 collective-permute-done.below
  23.8 0.0 collective-permute-done.1.above
  23.8 0.0 collective-permute-done.2.left
  23.8 0.2 collective-permute-done.3.right
  24.0 0.0 copy-done.4
  24.0 1.1 %first_step.1 = (f32[4,16,16,256]{3,2,1,0:T(8,128)S(1)}, bf16[32,32,128]{2,1,0:T(8,128)(2,1)}) custom-call(s32[8,16]{1,0:T(8,128)S(1)} %bitcast.21, f32[4,16,16,256]{3,2,1,0:T(8,128)S(1)} %inner_step.1.inner, f32[4,16,16,256]{3,2,1,0:T(8,128)S(1)} %bitcast.15, f32[3,16,16,256]{3,2,1,0:T(8,128)S(1)} %bitcast.19, ...), custom_call_target="tpu_custom_call", output_to_operand_aliasing={{0}: (1, {})} | custom-call | tf_op jit(solution)/shard_map/first_step/pallas_call | solution.py:483
  25.1 0.0 copy-start.6
  25.1 11.9 %all-to-all-start = ((bf16[32,32,128]{2,1,0:T(8,128)(2,1)}), bf16[32,32,128]{2,1,0:T(8,128)(2,1)S(1)}, u32[]{:S(2)}, u32[]{:S(2)}) async-start(bf16[32,32,128]{2,1,0:T(8,128)(2,1)} %get-tuple-element.17), calls=%async_computation | async-start | bytes 524288 | tf_op jit(solution)/shard_map/all_to_all | solution.py:493
  37.0 0.0 copy-done.6
  37.0 0.1 copy.10
  37.1 0.1 reshape.3.targets
  37.2 0.0 copy-start.3
  37.2 3.4 %second_step.1 = (f32[4,16,16,256]{3,2,1,0:T(8,128)S(1)}, f32[2,2,8,256]{3,2,1,0:T(8,128)S(1)}) custom-call(f32[4,16,16,256]{3,2,1,0:T(8,128)S(1)} %get-tuple-element.18.stepped, f32[4,16,16,256]{3,2,1,0:T(8,128)} %bitcast.13, f32[3,16,16,256]{3,2,1,0:T(8,128)} %bitcast.17, bf16[15,16,256]{2,1,0:T(8,128)(2,1)S(1)} %collective-permute-done.below, ...), custom_call_target="tpu_custom_call" | custom-call | tf_op jit(solution)/shard_map/second_step/pallas_call | solution.py:494
  40.6 0.0 copy-start.5
  40.6 9.8 %all-to-all-done.received = bf16[32,32,128]{2,1,0:T(8,128)(2,1)S(1)} async-done(((bf16[32,32,128]{2,1,0:T(8,128)(2,1)}), bf16[32,32,128]{2,1,0:T(8,128)(2,1)S(1)}, u32[]{:S(2)}, u32[]{:S(2)}) %all-to-all-start) | async-done | bytes 262176 | tf_op jit(solution)/shard_map/all_to_all | solution.py:493
  50.4 0.0 copy-done.3
  50.4 0.0 copy-done.5
  50.4 1.0 %add_source.1 = f32[4,16,16,256]{3,2,1,0:T(8,128)} custom-call(s32[1,128]{1,0:T(1,128)S(1)} %reshape.3.targets, s32[8,16]{1,0:T(8,128)S(1)} %bitcast.22, bf16[32,32,128]{2,1,0:T(8,128)(2,1)S(1)} %all-to-all-done.received, bf16[8,128,128]{2,1,0:T(8,128)(2,1)S(1)} %bitcast.20, f32[4,16,16,256]{3,2,1,0:T(8,128)S(1)} %get-tuple-element.19.base, ...), custom_call_target="tpu_custom_call" | custom-call | tf_op jit(solution)/shard_map/add_source/pallas_call | solution.py:506
Async XLA Ops:
  0.0 22.1 %copy-start = (f32[1,4,16,16,256]{4,3,2,1,0:T(8,128)S(1)}, f32[1,4,16,16,256]{4,3,2,1,0:T(8,128)}, u32[]{:S(2)}) copy-start(f32[1,4,16,16,256]{4,3,2,1,0:T(8,128)} %param.7) | copy-start | bytes 3145732
  0.0 22.1 %copy-start.1 = (f32[1,3,16,16,256]{4,3,2,1,0:T(8,128)S(1)}, f32[1,3,16,16,256]{4,3,2,1,0:T(8,128)}, u32[]{:S(2)}) copy-start(f32[1,3,16,16,256]{4,3,2,1,0:T(8,128)} %param.8) | copy-start | bytes 2359300
  0.0 22.1 %copy-start.2 = (f32[4,16,16,256]{3,2,1,0:T(8,128)S(1)}, f32[4,16,16,256]{3,2,1,0:T(8,128)}, u32[]{:S(2)}) copy-start(f32[4,16,16,256]{3,2,1,0:T(8,128)} %s.3) | copy-start | bytes 3145732
  2.0 21.7 %collective-permute-start = (bf16[15,16,256]{2,1,0:T(8,128)(2,1)S(1)}, bf16[15,16,256]{2,1,0:T(8,128)(2,1)S(1)}, u32[]{:S(2)}, u32[]{:S(2)}) collective-permute-start(bf16[15,16,256]{2,1,0:T(8,128)(2,1)S(1)} %get-tuple-element.13), channel_id=1, source_target_pairs={{0,16},{16,32},{32,48},{48,64},{64,80},{80,96},{96,112},{112,128},... | collective-permute-start | bytes 368648 | tf_op jit(solution)/shard_map/ppermute | solution.py:37
  6.6 17.1 %collective-permute-start.1 = (bf16[15,16,256]{2,1,0:T(8,128)(2,1)S(1)}, bf16[15,16,256]{2,1,0:T(8,128)(2,1)S(1)}, u32[]{:S(2)}, u32[]{:S(2)}) collective-permute-start(bf16[15,16,256]{2,1,0:T(8,128)(2,1)S(1)} %get-tuple-element.14), channel_id=1, source_target_pairs={{16,0},{32,16},{48,32},{64,48},{80,64},{96,80},{112,96},{128,112},... | collective-permute-start | bytes 368648 | tf_op jit(solution)/shard_map/ppermute | solution.py:37
  12.1 11.7 %collective-permute-start.2 = (bf16[15,16,256]{2,1,0:T(8,128)(2,1)S(1)}, bf16[15,16,256]{2,1,0:T(8,128)(2,1)S(1)}, u32[]{:S(2)}, u32[]{:S(2)}) collective-permute-start(bf16[15,16,256]{2,1,0:T(8,128)(2,1)S(1)} %get-tuple-element.15), channel_id=1, source_target_pairs={{0,1},{1,2},{2,3},{3,4},{4,5},{5,6},{6,7},{7,8},{8,9},{9,10},{10,1... | collective-permute-start | bytes 368648 | tf_op jit(solution)/shard_map/ppermute | solution.py:37
  14.1 9.9 %collective-permute-start.3 = (bf16[15,16,256]{2,1,0:T(8,128)(2,1)S(1)}, bf16[15,16,256]{2,1,0:T(8,128)(2,1)S(1)}, u32[]{:S(2)}, u32[]{:S(2)}) collective-permute-start(bf16[15,16,256]{2,1,0:T(8,128)(2,1)S(1)} %get-tuple-element.16), channel_id=1, source_target_pairs={{0,15},{1,0},{2,1},{3,2},{4,3},{5,4},{6,5},{7,6},{8,7},{9,8},{10,9... | collective-permute-start | bytes 368648 | tf_op jit(solution)/shard_map/ppermute | solution.py:37
  22.1 1.8 %copy-start.4 = (s32[1,1,16,8]{2,3,1,0:T(8,128)S(1)}, s32[1,1,16,8]{2,3,1,0:T(8,128)}, u32[]{:S(2)}) copy-start(s32[1,1,16,8]{2,3,1,0:T(8,128)} %param.11) | copy-start | bytes 1540
  25.1 11.9 %copy-start.6 = (s32[1,1,16,8]{2,3,1,0:T(8,128)S(1)}, s32[1,1,16,8]{2,3,1,0:T(8,128)}, u32[]{:S(2)}) copy-start(s32[1,1,16,8]{2,3,1,0:T(8,128)} %param.12) | copy-start | bytes 1540
  25.1 25.4 %all-to-all-start = ((bf16[32,32,128]{2,1,0:T(8,128)(2,1)}), bf16[32,32,128]{2,1,0:T(8,128)(2,1)S(1)}, u32[]{:S(2)}, u32[]{:S(2)}) async-start(bf16[32,32,128]{2,1,0:T(8,128)(2,1)} %get-tuple-element.17), calls=%async_computation | async-start | bytes 524288 | tf_op jit(solution)/shard_map/all_to_all | solution.py:493
  37.2 13.3 %copy-start.3 = (bf16[1,1,8,128,128]{4,3,2,1,0:T(8,128)(2,1)S(1)}, bf16[1,1,8,128,128]{4,3,2,1,0:T(8,128)(2,1)}, u32[]{:S(2)}) copy-start(bf16[1,1,8,128,128]{4,3,2,1,0:T(8,128)(2,1)} %param.10) | copy-start | bytes 786436
  40.6 9.8 %copy-start.5 = (s32[1,1,16,8]{2,3,1,0:T(8,128)S(1)}, s32[1,1,16,8]{2,3,1,0:T(8,128)}, u32[]{:S(2)}) copy-start(s32[1,1,16,8]{2,3,1,0:T(8,128)} %param.13) | copy-start | bytes 1540

commit v4 on v3

--- a/solution.py
+++ b/solution.py
@@ -200,7 +200,7 @@
     return [weight * value for value in near]
 
 
-def first_step(ids, inner, q, c, below, above, left, right, stepped, packed, sides):
+def first_step(ids, inner, q, c, left, right, below, above, stepped, packed, sides):
     section = lax.axis_index("sec")
     slab = lax.axis_index("ax")
     slabs = packed.shape[0] // 2
@@ -275,7 +275,7 @@
     return ends_of
 
 
-def second_step(stepped, q, c, below, above, left, right, out, paths, rims):
+def second_step(stepped, q, c, left, right, below, above, out, paths, rims):
     section = lax.axis_index("sec")
     slab = lax.axis_index("ax")
     slabs = lax.axis_size("ax")
@@ -453,24 +453,19 @@
     field = jax.ShapeDtypeStruct((NV, C1, C2, C3), F32)
     cells = pltpu.VMEM((NV, C1, C2, C3), F32)
 
-    low_slab, high_slab, low_sector, high_sector = pl.pallas_call(
+    low_slab, high_slab, low_sector, high_sector, kept, kept_factors, kept_source = pl.pallas_call(
         pack_halos,
         in_specs=[ANY] * 3,
-        out_specs=[VMEM] * 4,
-        out_shape=[message] * 4,
-        scratch_shapes=[
-            cells,
-            pltpu.VMEM((3, C1, C2, C3), F32),
-            cells,
-            pltpu.SemaphoreType.DMA((2 * NV + 3,)),
-        ],
+        out_specs=[VMEM] * 7,
+        out_shape=[message] * 4 + [cells, pltpu.VMEM((3, C1, C2, C3), F32), cells],
+        scratch_shapes=[pltpu.SemaphoreType.DMA((2 * NV + 3,))],
         compiler_params=PARAMS,
         name="pack_halos",
     )(off_chip(current), off_chip(factors), off_chip(old_source))
+    left = shift(high_sector, "az", 1, True)
+    right = shift(low_sector, "az", -1, True)
     below = shift(high_slab, "ax", 1, False)
     above = shift(low_slab, "ax", -1, False)
-    left = shift(high_sector, "az", 1, True)
-    right = shift(low_sector, "az", -1, True)
 
     inner = pl.pallas_call(
         inner_step,
@@ -479,7 +474,7 @@
         out_shape=field,
         compiler_params=PARAMS,
         name="inner_step",
-    )(current, factors, old_source)
+    )(kept, kept_factors, kept_source)
     stepped, packed = pl.pallas_call(
         first_step,
         in_specs=[VMEM] * 8,
@@ -489,7 +484,7 @@
         scratch_shapes=[pltpu.VMEM((2, NV, C1, C3), F32)],
         compiler_params=PARAMS,
         name="first_step",
-    )(send_ids[0, 0].T, inner, current, factors, below, above, left, right)
+    )(send_ids[0, 0].T, inner, kept, kept_factors, left, right, below, above)
     received = lax.all_to_all(packed, ("sec", "ax"), split_axis=0, concat_axis=0, tiled=True)
     base, paths = pl.pallas_call(
         second_step,
@@ -502,7 +497,7 @@
         scratch_shapes=[pltpu.VMEM((4, NV, C1, C3), F32)],
         compiler_params=PARAMS,
         name="second_step",
-    )(stepped, off_chip(current), off_chip(factors), below, above, left, right)
+    )(stepped, off_chip(current), off_chip(factors), left, right, below, above)
     advanced = pl.pallas_call(
         add_source,
         in_specs=[VMEM] * 6,

time: 51.8 us -> 52 us (level)
  waiting for transfers between devices: 9.96 us -> 12.4 us
  starting transfers between devices: 32 us -> 29.9 us
    ppermute x4, waiting for transfers between devices: 0.16 us -> 2.61 us  [shift(): return lax.ppermute(x, axis, pairs)]
    all_to_all x1, starting transfers between devices: 11.9 us -> 9.63 us  [shards(): lax.all_to_all(packed, ('sec', 'ax'), split_axis=0, concat_axis=0, tiled=...]
where the time goes in v4:
time: 52 us; the launch traced here: 51.7 us
  starting transfers between devices  29.9 us (58%)
  waiting for transfers between devices  12.4 us (24%)
  Pallas kernels  9.05 us (17%)
    ppermute x4, starting transfers between devices, shift(): return lax.ppermute(x, axis, pairs)  20.3 us
    all_to_all x1, waiting for transfers between devices, shards(): lax.all_to_all(packed, ('sec', 'ax'), split_axis=0, concat_axis=0, tiled=...  9.8 us
    all_to_all x1, starting transfers between devices, shards(): lax.all_to_all(packed, ('sec', 'ax'), split_axis=0, concat_axis=0, tiled=...  9.63 us
    pallas_call x1, Pallas kernels, shards(): pl.pallas_call(second_step, in_specs=[VMEM] * 7, out_specs=[VMEM] * 2, ou...  3.42 us
    ppermute x4, waiting for transfers between devices, shift(): return lax.ppermute(x, axis, pairs)  2.61 us
    pallas_call x1, Pallas kernels, shards(): pl.pallas_call(pack_halos, in_specs=[ANY] * 3, out_specs=[VMEM] * 7, out_...  1.87 us
    pallas_call x1, Pallas kernels, shards(): pl.pallas_call(inner_step, in_specs=[VMEM] * 3, out_specs=VMEM, out_shape...  1.61 us
    pallas_call x1, Pallas kernels, shards(): pl.pallas_call(first_step, in_specs=[VMEM] * 8, out_specs=[VMEM] * 2, out...  1.12 us
  transfers between devices with their start and end apart: 5, of which 2 were waited for; matrix products, arithmetic and copies ran while one was open for 0% of the time, Pallas kernels for 10%

profile of v4, /device:TPU:1, one launch (start us, length us, event | category | flops | bytes accessed | tf_op | source)
XLA Modules:
  0.0 51.7 jit_solution(290965554322993636)
XLA Ops:
  0.0 1.9 %pack_halos.1 = (bf16[15,16,256]{2,1,0:T(8,128)(2,1)S(1)}, bf16[15,16,256]{2,1,0:T(8,128)(2,1)S(1)}, bf16[15,16,256]{2,1,0:T(8,128)(2,1)S(1)}, bf16[15,16,256]{2...) custom-call(f32[4,16,16,256]{3,2,1,0:T(8,128)} %bitcast.15, ...), custom_call_target="tpu_custom_call" | custom-call | tf_op jit(solution)/shard_map/pack_halos/pallas_call | solution.py:456
  1.9 4.8 %collective-permute-start = (bf16[15,16,256]{2,1,0:T(8,128)(2,1)S(1)}, bf16[15,16,256]{2,1,0:T(8,128)(2,1)S(1)}, u32[]{:S(2)}, u32[]{:S(2)}) collective-permute-start(bf16[15,16,256]{2,1,0:T(8,128)(2,1)S(1)} %get-tuple-element.19), channel_id=1, source_target_pairs={{0,1},{1,2},{2,3},{3,4},{4,5},{5,6},{6,7},{7,8},{8,9},{9,10},{10,1... | collective-permute-start | bytes 368648 | tf_op jit(solution)/shard_map/ppermute | solution.py:37
  6.7 9.5 %collective-permute-start.1 = (bf16[15,16,256]{2,1,0:T(8,128)(2,1)S(1)}, bf16[15,16,256]{2,1,0:T(8,128)(2,1)S(1)}, u32[]{:S(2)}, u32[]{:S(2)}) collective-permute-start(bf16[15,16,256]{2,1,0:T(8,128)(2,1)S(1)} %get-tuple-element.20), channel_id=1, source_target_pairs={{0,15},{1,0},{2,1},{3,2},{4,3},{5,4},{6,5},{7,6},{8,7},{9,8},{10,9... | collective-permute-start | bytes 368648 | tf_op jit(solution)/shard_map/ppermute | solution.py:37
  16.2 4.0 %collective-permute-start.2 = (bf16[15,16,256]{2,1,0:T(8,128)(2,1)S(1)}, bf16[15,16,256]{2,1,0:T(8,128)(2,1)S(1)}, u32[]{:S(2)}, u32[]{:S(2)}) collective-permute-start(bf16[15,16,256]{2,1,0:T(8,128)(2,1)S(1)} %get-tuple-element.21), channel_id=1, source_target_pairs={{0,16},{16,32},{32,48},{48,64},{64,80},{80,96},{96,112},{112,128},... | collective-permute-start | bytes 368648 | tf_op jit(solution)/shard_map/ppermute | solution.py:37
  20.3 1.9 %collective-permute-start.3 = (bf16[15,16,256]{2,1,0:T(8,128)(2,1)S(1)}, bf16[15,16,256]{2,1,0:T(8,128)(2,1)S(1)}, u32[]{:S(2)}, u32[]{:S(2)}) collective-permute-start(bf16[15,16,256]{2,1,0:T(8,128)(2,1)S(1)} %get-tuple-element.22), channel_id=1, source_target_pairs={{16,0},{32,16},{48,32},{64,48},{80,64},{96,80},{112,96},{128,112},... | collective-permute-start | bytes 368648 | tf_op jit(solution)/shard_map/ppermute | solution.py:37
  22.2 0.0 copy-start.1
  22.2 1.6 %inner_step.1.inner = f32[4,16,16,256]{3,2,1,0:T(8,128)S(1)} custom-call(f32[4,16,16,256]{3,2,1,0:T(8,128)S(1)} %get-tuple-element.16.q, f32[3,16,16,256]{3,2,1,0:T(8,128)S(1)} %get-tuple-element.17.c, f32[4,16,16,256]{3,2,1,0:T(8,128)S(1)} %get-tuple-element.18.s), custom_call_target="tpu_custom_call" | custom-call | tf_op jit(solution)/shard_map/inner_step/pallas_call | solution.py:470
  23.9 0.0 collective-permute-done.left
  23.9 0.0 collective-permute-done.1.right
  23.9 0.0 collective-permute-done.2.below
  23.9 2.6 %collective-permute-done.3.above = bf16[15,16,256]{2,1,0:T(8,128)(2,1)S(1)} collective-permute-done((bf16[15,16,256]{2,1,0:T(8,128)(2,1)S(1)}, bf16[15,16,256]{2,1,0:T(8,128)(2,1)S(1)}, u32[]{:S(2)}, u32[]{:S(2)}) %collective-permute-start.3) | collective-permute-done | bytes 122912 | tf_op jit(solution)/shard_map/ppermute | solution.py:37
  26.5 0.0 copy-done.1
  26.5 1.1 %first_step.1 = (f32[4,16,16,256]{3,2,1,0:T(8,128)S(1)}, bf16[32,32,128]{2,1,0:T(8,128)(2,1)}) custom-call(s32[8,16]{1,0:T(8,128)S(1)} %bitcast.13, f32[4,16,16,256]{3,2,1,0:T(8,128)S(1)} %inner_step.1.inner, f32[4,16,16,256]{3,2,1,0:T(8,128)S(1)} %get-tuple-element.16.q, ...), custom_call_target="tpu_custom_call", output_to_operand_aliasing={{0}: (1, {})} | custom-call | tf_op jit(solution)/shard_map/first_step/pallas_call | solution.py:478
  27.6 0.0 copy-start.3
  27.6 9.6 %all-to-all-start = ((bf16[32,32,128]{2,1,0:T(8,128)(2,1)}), bf16[32,32,128]{2,1,0:T(8,128)(2,1)S(1)}, u32[]{:S(2)}, u32[]{:S(2)}) async-start(bf16[32,32,128]{2,1,0:T(8,128)(2,1)} %get-tuple-element.23), calls=%async_computation | async-start | bytes 524288 | tf_op jit(solution)/shard_map/all_to_all | solution.py:488
  37.3 0.0 copy-done.3
  37.3 0.1 copy.10
  37.3 0.1 reshape.3.targets
  37.4 0.0 copy-start
  37.4 3.4 %second_step.1 = (f32[4,16,16,256]{3,2,1,0:T(8,128)S(1)}, f32[2,2,8,256]{3,2,1,0:T(8,128)S(1)}) custom-call(f32[4,16,16,256]{3,2,1,0:T(8,128)S(1)} %get-tuple-element.24.stepped, f32[4,16,16,256]{3,2,1,0:T(8,128)} %bitcast.16, f32[3,16,16,256]{3,2,1,0:T(8,128)} %bitcast.18, bf16[15,16,256]{2,1,0:T(8,128)(2,1)S(1)} %collective-permute-done.left, ...), custom_call_target="tpu_custom_call" | custom-call | tf_op jit(solution)/shard_map/second_step/pallas_call | solution.py:489
  40.9 0.0 copy-start.2
  40.9 9.8 %all-to-all-done.received = bf16[32,32,128]{2,1,0:T(8,128)(2,1)S(1)} async-done(((bf16[32,32,128]{2,1,0:T(8,128)(2,1)}), bf16[32,32,128]{2,1,0:T(8,128)(2,1)S(1)}, u32[]{:S(2)}, u32[]{:S(2)}) %all-to-all-start) | async-done | bytes 262176 | tf_op jit(solution)/shard_map/all_to_all | solution.py:488
  50.7 0.0 copy-done
  50.7 0.0 copy-done.2
  50.7 1.0 %add_source.1 = f32[4,16,16,256]{3,2,1,0:T(8,128)} custom-call(s32[1,128]{1,0:T(1,128)S(1)} %reshape.3.targets, s32[8,16]{1,0:T(8,128)S(1)} %bitcast.14, bf16[32,32,128]{2,1,0:T(8,128)(2,1)S(1)} %all-to-all-done.received, bf16[8,128,128]{2,1,0:T(8,128)(2,1)S(1)} %bitcast.12, f32[4,16,16,256]{3,2,1,0:T(8,128)S(1)} %get-tuple-element.25.base, ...), custom_call_target="tpu_custom_call" | custom-call | tf_op jit(solution)/shard_map/add_source/pallas_call | solution.py:501
Async XLA Ops:
  1.9 22.0 %collective-permute-start = (bf16[15,16,256]{2,1,0:T(8,128)(2,1)S(1)}, bf16[15,16,256]{2,1,0:T(8,128)(2,1)S(1)}, u32[]{:S(2)}, u32[]{:S(2)}) collective-permute-start(bf16[15,16,256]{2,1,0:T(8,128)(2,1)S(1)} %get-tuple-element.19), channel_id=1, source_target_pairs={{0,1},{1,2},{2,3},{3,4},{4,5},{5,6},{6,7},{7,8},{8,9},{9,10},{10,1... | collective-permute-start | bytes 368648 | tf_op jit(solution)/shard_map/ppermute | solution.py:37
  6.7 17.2 %collective-permute-start.1 = (bf16[15,16,256]{2,1,0:T(8,128)(2,1)S(1)}, bf16[15,16,256]{2,1,0:T(8,128)(2,1)S(1)}, u32[]{:S(2)}, u32[]{:S(2)}) collective-permute-start(bf16[15,16,256]{2,1,0:T(8,128)(2,1)S(1)} %get-tuple-element.20), channel_id=1, source_target_pairs={{0,15},{1,0},{2,1},{3,2},{4,3},{5,4},{6,5},{7,6},{8,7},{9,8},{10,9... | collective-permute-start | bytes 368648 | tf_op jit(solution)/shard_map/ppermute | solution.py:37
  16.2 7.6 %collective-permute-start.2 = (bf16[15,16,256]{2,1,0:T(8,128)(2,1)S(1)}, bf16[15,16,256]{2,1,0:T(8,128)(2,1)S(1)}, u32[]{:S(2)}, u32[]{:S(2)}) collective-permute-start(bf16[15,16,256]{2,1,0:T(8,128)(2,1)S(1)} %get-tuple-element.21), channel_id=1, source_target_pairs={{0,16},{16,32},{32,48},{48,64},{64,80},{80,96},{96,112},{112,128},... | collective-permute-start | bytes 368648 | tf_op jit(solution)/shard_map/ppermute | solution.py:37
  20.3 6.2 %collective-permute-start.3 = (bf16[15,16,256]{2,1,0:T(8,128)(2,1)S(1)}, bf16[15,16,256]{2,1,0:T(8,128)(2,1)S(1)}, u32[]{:S(2)}, u32[]{:S(2)}) collective-permute-start(bf16[15,16,256]{2,1,0:T(8,128)(2,1)S(1)} %get-tuple-element.22), channel_id=1, source_target_pairs={{16,0},{32,16},{48,32},{64,48},{80,64},{96,80},{112,96},{128,112},... | collective-permute-start | bytes 368648 | tf_op jit(solution)/shard_map/ppermute | solution.py:37
  22.2 4.3 %copy-start.1 = (s32[1,1,16,8]{2,3,1,0:T(8,128)S(1)}, s32[1,1,16,8]{2,3,1,0:T(8,128)}, u32[]{:S(2)}) copy-start(s32[1,1,16,8]{2,3,1,0:T(8,128)} %param.11) | copy-start | bytes 1540
  27.6 9.6 %copy-start.3 = (s32[1,1,16,8]{2,3,1,0:T(8,128)S(1)}, s32[1,1,16,8]{2,3,1,0:T(8,128)}, u32[]{:S(2)}) copy-start(s32[1,1,16,8]{2,3,1,0:T(8,128)} %param.12) | copy-start | bytes 1540
  27.6 23.1 %all-to-all-start = ((bf16[32,32,128]{2,1,0:T(8,128)(2,1)}), bf16[32,32,128]{2,1,0:T(8,128)(2,1)S(1)}, u32[]{:S(2)}, u32[]{:S(2)}) async-start(bf16[32,32,128]{2,1,0:T(8,128)(2,1)} %get-tuple-element.23), calls=%async_computation | async-start | bytes 524288 | tf_op jit(solution)/shard_map/all_to_all | solution.py:488
  37.4 13.3 %copy-start = (bf16[1,1,8,128,128]{4,3,2,1,0:T(8,128)(2,1)S(1)}, bf16[1,1,8,128,128]{4,3,2,1,0:T(8,128)(2,1)}, u32[]{:S(2)}) copy-start(bf16[1,1,8,128,128]{4,3,2,1,0:T(8,128)(2,1)} %param.10) | copy-start | bytes 786436
  40.9 9.8 %copy-start.2 = (s32[1,1,16,8]{2,3,1,0:T(8,128)S(1)}, s32[1,1,16,8]{2,3,1,0:T(8,128)}, u32[]{:S(2)}) copy-start(s32[1,1,16,8]{2,3,1,0:T(8,128)} %param.13) | copy-start | bytes 1540

commit v5 on v4

--- a/solution.py
+++ b/solution.py
@@ -31,10 +31,36 @@
     return pltpu.with_memory_space_constraint(x, pltpu.HBM)
 
 
-def shift(x, axis, by, periodic):
+def swap(x, axis, first, periodic):
     count = lax.axis_size(axis)
-    pairs = [(i, (i + by) % count) for i in range(count) if periodic or 0 <= i + by < count]
+    pairs = []
+    for i in range(first, count if periodic else count - 1, 2):
+        pairs += [(i, (i + 1) % count), ((i + 1) % count, i)]
     return lax.ppermute(x, axis, pairs)
+
+
+def is_early(sector, sectors):
+    return sector % (sectors // 2) == 0
+
+
+def swap_slabs(x, first, early):
+    sections, slabs, sectors = (lax.axis_size(axis) for axis in ("sec", "ax", "az"))
+    pairs = []
+    for section in range(sections):
+        for slab in range(first, slabs - 1, 2):
+            for sector in range(sectors):
+                if is_early(sector, sectors) == early:
+                    low = (section * slabs + slab) * sectors + sector
+                    pairs += [(low, low + sectors), (low + sectors, low)]
+    return lax.ppermute(x, ("sec", "ax", "az"), pairs)
+
+
+def joined(early, late):
+    return early.astype(F32) + late.astype(F32)
+
+
+def upper_first(axis):
+    return lax.axis_index(axis) % 2 == 0
 
 
 def rows_of(shape, axis):
@@ -116,7 +142,11 @@
     return ref[component, :, j, :]
 
 
-def pack_halos(q, c, s, low_slab, high_slab, low_sector, high_sector, cells, factors, source, done):
+def pack_halos(q, c, s, *rest):
+    *outs, cells, factors, source, done = rest
+    sector_first, sector_second, slab_first, slab_second = outs
+    sector_up = upper_first("az")
+    slab_up = upper_first("ax")
     parts = []
     for v in range(NV):
         parts.append((q.at[v], cells.at[v]))
@@ -127,23 +157,25 @@
     copies = [pltpu.make_async_copy(*part, done.at[n]) for n, part in enumerate(parts)]
     for copy in copies:
         copy.start()
+
+    def fill(ref, component, plane, depth):
+        high = jnp.where(slab_up, C1 - 1 - depth, depth)
+        slab_first[plane] = ref[component, high].astype(BF16)
+        slab_second[plane] = ref[component, C1 - 1 - high].astype(BF16)
+        low = column(ref, component, depth)
+        high = column(ref, component, C2 - 1 - depth)
+        sector_first[plane] = jnp.where(sector_up, high, low).astype(BF16)
+        sector_second[plane] = jnp.where(sector_up, low, high).astype(BF16)
+
     for n, copy in enumerate(copies):
         copy.wait()
         if n < NV:
-            ref, component, plane = cells, n, NEAR + n
+            fill(cells, n, NEAR + n, 0)
+            fill(cells, n, FAR + n, 1)
         elif n < NV + 3:
-            ref, component, plane = factors, n - NV, COEF + n - NV
+            fill(factors, n - NV, COEF + n - NV, 0)
         else:
-            ref, component, plane = source, n - NV - 3, SOURCE + n - NV - 3
-        low_slab[plane] = ref[component, 0].astype(BF16)
-        high_slab[plane] = ref[component, C1 - 1].astype(BF16)
-        low_sector[plane] = column(ref, component, 0).astype(BF16)
-        high_sector[plane] = column(ref, component, C2 - 1).astype(BF16)
-        if n < NV:
-            low_slab[FAR + n] = ref[component, 1].astype(BF16)
-            high_slab[FAR + n] = ref[component, C1 - 2].astype(BF16)
-            low_sector[FAR + n] = column(ref, component, 1).astype(BF16)
-            high_sector[FAR + n] = column(ref, component, C2 - 2).astype(BF16)
+            fill(source, n - NV - 3, SOURCE + n - NV - 3, 0)
 
 
 def fields_of(message, start, count=NV):
@@ -200,18 +232,25 @@
     return [weight * value for value in near]
 
 
-def first_step(ids, inner, q, c, left, right, below, above, stepped, packed, sides):
+def first_step(ids, inner, q, c, *rest):
+    *messages, stepped, packed, sides, faces = rest
     section = lax.axis_index("sec")
     slab = lax.axis_index("ax")
     slabs = packed.shape[0] // 2
-    for side, message in enumerate((left, right)):
-        for v in range(NV):
-            sides[side, v] = message[NEAR + v].astype(F32)
+    sector_first, early_first, early_second, sector_second, late_first, late_second = messages
+    sector_up = jnp.where(upper_first("az"), 1, 0)
+    slab_up = jnp.where(upper_first("ax"), 1, 0)
+    for v in range(NV):
+        plane = NEAR + v
+        sides[sector_up, v] = sector_first[plane].astype(F32)
+        sides[1 - sector_up, v] = sector_second[plane].astype(F32)
+        faces[slab_up, v] = joined(early_first[plane], late_first[plane])
+        faces[1 - slab_up, v] = joined(early_second[plane], late_second[plane])
 
     def add_borders(acoustic):
-        for side, message in enumerate((below, above)):
+        for side in range(2):
             i = side * (C1 - 1)
-            near = fields_of(message, NEAR)
+            near = [faces[side, v] for v in range(NV)]
             terms = border_terms(acoustic, near, q[0, i], c[0, i], 0, side)
             for v in range(NV):
                 stepped[v, i] += terms[v]
@@ -275,7 +314,16 @@
     return ends_of
 
 
-def second_step(stepped, q, c, left, right, below, above, out, paths, rims):
+def second_step(stepped, q, c, *rest):
+    *messages, out, paths, rims, halos = rest
+    sector_first, early_first, early_second, sector_second, late_first, late_second = messages
+    sector_up = jnp.where(upper_first("az"), 1, 0)
+    slab_up = jnp.where(upper_first("ax"), 1, 0)
+    halos[sector_up] = sector_first[...]
+    halos[1 - sector_up] = sector_second[...]
+    halos[2 + slab_up] = joined(early_first[...], late_first[...]).astype(BF16)
+    halos[3 - slab_up] = joined(early_second[...], late_second[...]).astype(BF16)
+    left, right, below, above = (halos.at[n] for n in range(4))
     section = lax.axis_index("sec")
     slab = lax.axis_index("ax")
     slabs = lax.axis_size("ax")
@@ -453,7 +501,7 @@
     field = jax.ShapeDtypeStruct((NV, C1, C2, C3), F32)
     cells = pltpu.VMEM((NV, C1, C2, C3), F32)
 
-    low_slab, high_slab, low_sector, high_sector, kept, kept_factors, kept_source = pl.pallas_call(
+    *sends, kept, kept_factors, kept_source = pl.pallas_call(
         pack_halos,
         in_specs=[ANY] * 3,
         out_specs=[VMEM] * 7,
@@ -462,11 +510,12 @@
         compiler_params=PARAMS,
         name="pack_halos",
     )(off_chip(current), off_chip(factors), off_chip(old_source))
-    left = shift(high_sector, "az", 1, True)
-    right = shift(low_sector, "az", -1, True)
-    below = shift(high_slab, "ax", 1, False)
-    above = shift(low_slab, "ax", -1, False)
-
+    sector_first = swap(sends[0], "az", 0, True)
+    early = [swap_slabs(sends[2 + n], n, True) for n in range(2)]
+    sector_second = swap(sends[1], "az", 1, True)
+    sector_first, *sends = lax.optimization_barrier((sector_first, *sends))
+    late = [swap_slabs(sends[2 + n], n, False) for n in range(2)]
+    messages = [sector_first, early[0], early[1], sector_second, late[0], late[1]]
     inner = pl.pallas_call(
         inner_step,
         in_specs=[VMEM] * 3,
@@ -477,27 +526,30 @@
     )(kept, kept_factors, kept_source)
     stepped, packed = pl.pallas_call(
         first_step,
-        in_specs=[VMEM] * 8,
+        in_specs=[VMEM] * 10,
         out_specs=[VMEM] * 2,
         out_shape=[field, pltpu.HBM((peers, CAP * NV, LINE), BF16)],
         input_output_aliases={1: 0},
-        scratch_shapes=[pltpu.VMEM((2, NV, C1, C3), F32)],
+        scratch_shapes=[pltpu.VMEM((2, NV, C1, C3), F32)] * 2,
         compiler_params=PARAMS,
         name="first_step",
-    )(send_ids[0, 0].T, inner, kept, kept_factors, left, right, below, above)
+    )(send_ids[0, 0].T, inner, kept, kept_factors, *messages)
     received = lax.all_to_all(packed, ("sec", "ax"), split_axis=0, concat_axis=0, tiled=True)
     base, paths = pl.pallas_call(
         second_step,
-        in_specs=[VMEM] * 7,
+        in_specs=[VMEM] * 9,
         out_specs=[VMEM] * 2,
         out_shape=[
             field,
             jax.ShapeDtypeStruct((2, 2, 8, C3), F32),
         ],
-        scratch_shapes=[pltpu.VMEM((4, NV, C1, C3), F32)],
+        scratch_shapes=[
+            pltpu.VMEM((4, NV, C1, C3), F32),
+            pltpu.VMEM((4, PLANES, C1, C3), BF16),
+        ],
         compiler_params=PARAMS,
         name="second_step",
-    )(stepped, off_chip(current), off_chip(factors), left, right, below, above)
+    )(stepped, off_chip(current), off_chip(factors), *messages)
     advanced = pl.pallas_call(
         add_source,
         in_specs=[VMEM] * 6,

time: 52 us -> 48.6 us (0.935)
  the two profiles are of different devices: /device:TPU:1 before, /device:TPU:192 now
where the time goes in v5:
time: 48.6 us; the launch traced here: 48.2 us
  starting transfers between devices  27.7 us (57%)
  waiting for transfers between devices  11 us (23%)
  Pallas kernels  9.16 us (19%)
    all_to_all x1, starting transfers between devices, shards(): lax.all_to_all(packed, ('sec', 'ax'), split_axis=0, concat_axis=0, tiled=...  14.9 us
    all_to_all x1, waiting for transfers between devices, shards(): lax.all_to_all(packed, ('sec', 'ax'), split_axis=0, concat_axis=0, tiled=...  11 us
    ppermute x2, starting transfers between devices, swap(): return lax.ppermute(x, axis, pairs)  8.87 us
    ppermute x4, starting transfers between devices, swap_slabs(): return lax.ppermute(x, ('sec', 'ax', 'az'), pairs)  3.93 us
    pallas_call x1, Pallas kernels, shards(): pl.pallas_call(second_step, in_specs=[VMEM] * 9, out_specs=[VMEM] * 2, ou...  3.5 us
    pallas_call x1, Pallas kernels, shards(): pl.pallas_call(pack_halos, in_specs=[ANY] * 3, out_specs=[VMEM] * 7, out_...  1.88 us
    pallas_call x1, Pallas kernels, shards(): pl.pallas_call(inner_step, in_specs=[VMEM] * 3, out_specs=VMEM, out_shape...  1.61 us
    pallas_call x1, Pallas kernels, shards(): pl.pallas_call(first_step, in_specs=[VMEM] * 10, out_specs=[VMEM] * 2, ou...  1.14 us
  transfers between devices with their start and end apart: 7, of which 1 were waited for; matrix products, arithmetic and copies ran while one was open for 0% of the time, Pallas kernels for 11%

profile of v5, /device:TPU:192, one launch (start us, length us, event | category | flops | bytes accessed | tf_op | source)
XLA Modules:
  0.0 48.2 jit_solution(5316074115006327771)
XLA Ops:
  0.0 1.9 %pack_halos.1 = (bf16[15,16,256]{2,1,0:T(8,128)(2,1)S(1)}, bf16[15,16,256]{2,1,0:T(8,128)(2,1)S(1)}, bf16[15,16,256]{2,1,0:T(8,128)(2,1)S(1)}, bf16[15,16,256]{2...) custom-call(f32[4,16,16,256]{3,2,1,0:T(8,128)} %bitcast.15, ...), custom_call_target="tpu_custom_call" | custom-call | tf_op jit(solution)/shard_map/pack_halos/pallas_call | solution.py:504
  1.9 1.9 %collective-permute-start = (bf16[15,16,256]{2,1,0:T(8,128)(2,1)S(1)}, bf16[15,16,256]{2,1,0:T(8,128)(2,1)S(1)}, u32[]{:S(2)}, u32[]{:S(2)}) collective-permute-start(bf16[15,16,256]{2,1,0:T(8,128)(2,1)S(1)} %get-tuple-element.22), channel_id=1, source_target_pairs={{0,1},{1,0},{2,3},{3,2},{4,5},{5,4},{6,7},{7,6},{8,9},{9,8},{10,11... | collective-permute-start | bytes 368648 | tf_op jit(solution)/shard_map/ppermute | solution.py:39
  3.8 0.7 %collective-permute-start.1 = (bf16[15,16,256]{2,1,0:T(8,128)(2,1)S(1)}, bf16[15,16,256]{2,1,0:T(8,128)(2,1)S(1)}, u32[]{:S(2)}, u32[]{:S(2)}) collective-permute-start(bf16[15,16,256]{2,1,0:T(8,128)(2,1)S(1)} %get-tuple-element.27), channel_id=1, source_target_pairs={{0,16},{16,0},{8,24},{24,8},{32,48},{48,32},{40,56},{56,40},{64,80... | collective-permute-start | bytes 368648 | tf_op jit(solution)/shard_map/ppermute | solution.py:55
  4.5 0.7 %collective-permute-start.2 = (bf16[15,16,256]{2,1,0:T(8,128)(2,1)S(1)}, bf16[15,16,256]{2,1,0:T(8,128)(2,1)S(1)}, u32[]{:S(2)}, u32[]{:S(2)}) collective-permute-start(bf16[15,16,256]{2,1,0:T(8,128)(2,1)S(1)} %get-tuple-element.28), channel_id=1, source_target_pairs={{16,32},{32,16},{24,40},{40,24},{48,64},{64,48},{56,72},{72,56},{8... | collective-permute-start | bytes 368648 | tf_op jit(solution)/shard_map/ppermute | solution.py:55
  5.2 7.0 %collective-permute-start.3 = (bf16[15,16,256]{2,1,0:T(8,128)(2,1)S(1)}, bf16[15,16,256]{2,1,0:T(8,128)(2,1)S(1)}, u32[]{:S(2)}, u32[]{:S(2)}) collective-permute-start(bf16[15,16,256]{2,1,0:T(8,128)(2,1)S(1)} %get-tuple-element.23), channel_id=1, source_target_pairs={{1,2},{2,1},{3,4},{4,3},{5,6},{6,5},{7,8},{8,7},{9,10},{10,9},{11,... | collective-permute-start | bytes 368648 | tf_op jit(solution)/shard_map/ppermute | solution.py:39
  12.1 0.0 collective-permute-done.rest_0_
  12.1 1.9 %collective-permute-start.4 = (bf16[15,16,256]{2,1,0:T(8,128)(2,1)S(1)}, bf16[15,16,256]{2,1,0:T(8,128)(2,1)S(1)}, u32[]{:S(2)}, u32[]{:S(2)}) collective-permute-start(bf16[15,16,256]{2,1,0:T(8,128)(2,1)S(1)} %get-tuple-element.27), channel_id=1, source_target_pairs={{1,17},{17,1},{2,18},{18,2},{3,19},{19,3},{4,20},{20,4},{5,21},{21... | collective-permute-start | bytes 368648 | tf_op jit(solution)/shard_map/ppermute | solution.py:55
  14.1 0.7 %collective-permute-start.5 = (bf16[15,16,256]{2,1,0:T(8,128)(2,1)S(1)}, bf16[15,16,256]{2,1,0:T(8,128)(2,1)S(1)}, u32[]{:S(2)}, u32[]{:S(2)}) collective-permute-start(bf16[15,16,256]{2,1,0:T(8,128)(2,1)S(1)} %get-tuple-element.28), channel_id=1, source_target_pairs={{17,33},{33,17},{18,34},{34,18},{19,35},{35,19},{20,36},{36,20},{2... | collective-permute-start | bytes 368648 | tf_op jit(solution)/shard_map/ppermute | solution.py:55
  14.7 0.0 copy-start.2
  14.8 1.6 %inner_step.1.inner = f32[4,16,16,256]{3,2,1,0:T(8,128)S(1)} custom-call(f32[4,16,16,256]{3,2,1,0:T(8,128)S(1)} %get-tuple-element.19.q, f32[3,16,16,256]{3,2,1,0:T(8,128)S(1)} %get-tuple-element.20.c, f32[4,16,16,256]{3,2,1,0:T(8,128)S(1)} %get-tuple-element.21.s), custom_call_target="tpu_custom_call" | custom-call | tf_op jit(solution)/shard_map/inner_step/pallas_call | solution.py:519
  16.4 0.0 collective-permute-done.1.rest_1_
  16.4 0.0 collective-permute-done.2.rest_2_
  16.4 0.0 collective-permute-done.3.rest_3_
  16.4 0.0 collective-permute-done.4.rest_4_
  16.4 0.0 collective-permute-done.5.rest_5_
  16.4 0.0 copy-done.2
  16.4 1.1 %first_step.1 = (f32[4,16,16,256]{3,2,1,0:T(8,128)S(1)}, bf16[32,32,128]{2,1,0:T(8,128)(2,1)}) custom-call(s32[8,16]{1,0:T(8,128)S(1)} %bitcast.14, f32[4,16,16,256]{3,2,1,0:T(8,128)S(1)} %inner_step.1.inner, f32[4,16,16,256]{3,2,1,0:T(8,128)S(1)} %get-tuple-element.19.q, ...), custom_call_target="tpu_custom_call", output_to_operand_aliasing={{0}: (1, {})} | custom-call | tf_op jit(solution)/shard_map/first_step/pallas_call | solution.py:527
  17.6 0.0 copy-start.3
  17.6 14.9 %all-to-all-start = ((bf16[32,32,128]{2,1,0:T(8,128)(2,1)}), bf16[32,32,128]{2,1,0:T(8,128)(2,1)S(1)}, u32[]{:S(2)}, u32[]{:S(2)}) async-start(bf16[32,32,128]{2,1,0:T(8,128)(2,1)} %get-tuple-element.29), calls=%async_computation | async-start | bytes 524288 | tf_op jit(solution)/shard_map/all_to_all | solution.py:537
  32.5 0.0 copy-done.3
  32.5 0.1 copy.10
  32.6 0.1 reshape.3.targets
  32.7 0.0 copy-start
  32.7 3.5 %second_step.1 = (f32[4,16,16,256]{3,2,1,0:T(8,128)S(1)}, f32[2,2,8,256]{3,2,1,0:T(8,128)S(1)}) custom-call(f32[4,16,16,256]{3,2,1,0:T(8,128)S(1)} %get-tuple-element.30.stepped, f32[4,16,16,256]{3,2,1,0:T(8,128)} %bitcast.16, f32[3,16,16,256]{3,2,1,0:T(8,128)} %bitcast.18, bf16[15,16,256]{2,1,0:T(8,128)(2,1)S(1)} %collective-permute-done.rest_0_, ...), custom_call_target="tpu_custom_call" | custom-call | tf_op jit(solution)/shard_map/second_step/pallas_call | solution.py:538
  36.2 0.0 copy-start.1
  36.2 11.0 %all-to-all-done.received = bf16[32,32,128]{2,1,0:T(8,128)(2,1)S(1)} async-done(((bf16[32,32,128]{2,1,0:T(8,128)(2,1)}), bf16[32,32,128]{2,1,0:T(8,128)(2,1)S(1)}, u32[]{:S(2)}, u32[]{:S(2)}) %all-to-all-start) | async-done | bytes 262176 | tf_op jit(solution)/shard_map/all_to_all | solution.py:537
  47.2 0.0 copy-done
  47.2 0.0 copy-done.1
  47.2 1.0 %add_source.1 = f32[4,16,16,256]{3,2,1,0:T(8,128)} custom-call(s32[1,128]{1,0:T(1,128)S(1)} %reshape.3.targets, s32[8,16]{1,0:T(8,128)S(1)} %bitcast.13, bf16[32,32,128]{2,1,0:T(8,128)(2,1)S(1)} %all-to-all-done.received, bf16[8,128,128]{2,1,0:T(8,128)(2,1)S(1)} %bitcast.12, f32[4,16,16,256]{3,2,1,0:T(8,128)S(1)} %get-tuple-element.31.base, ...), custom_call_target="tpu_custom_call" | custom-call | tf_op jit(solution)/shard_map/add_source/pallas_call | solution.py:553
Async XLA Ops:
  1.9 10.2 %collective-permute-start = (bf16[15,16,256]{2,1,0:T(8,128)(2,1)S(1)}, bf16[15,16,256]{2,1,0:T(8,128)(2,1)S(1)}, u32[]{:S(2)}, u32[]{:S(2)}) collective-permute-start(bf16[15,16,256]{2,1,0:T(8,128)(2,1)S(1)} %get-tuple-element.22), channel_id=1, source_target_pairs={{0,1},{1,0},{2,3},{3,2},{4,5},{5,4},{6,7},{7,6},{8,9},{9,8},{10,11... | collective-permute-start | bytes 368648 | tf_op jit(solution)/shard_map/ppermute | solution.py:39
  3.8 12.6 %collective-permute-start.1 = (bf16[15,16,256]{2,1,0:T(8,128)(2,1)S(1)}, bf16[15,16,256]{2,1,0:T(8,128)(2,1)S(1)}, u32[]{:S(2)}, u32[]{:S(2)}) collective-permute-start(bf16[15,16,256]{2,1,0:T(8,128)(2,1)S(1)} %get-tuple-element.27), channel_id=1, source_target_pairs={{0,16},{16,0},{8,24},{24,8},{32,48},{48,32},{40,56},{56,40},{64,80... | collective-permute-start | bytes 368648 | tf_op jit(solution)/shard_map/ppermute | solution.py:55
  4.5 11.9 %collective-permute-start.2 = (bf16[15,16,256]{2,1,0:T(8,128)(2,1)S(1)}, bf16[15,16,256]{2,1,0:T(8,128)(2,1)S(1)}, u32[]{:S(2)}, u32[]{:S(2)}) collective-permute-start(bf16[15,16,256]{2,1,0:T(8,128)(2,1)S(1)} %get-tuple-element.28), channel_id=1, source_target_pairs={{16,32},{32,16},{24,40},{40,24},{48,64},{64,48},{56,72},{72,56},{8... | collective-permute-start | bytes 368648 | tf_op jit(solution)/shard_map/ppermute | solution.py:55
  5.2 11.2 %collective-permute-start.3 = (bf16[15,16,256]{2,1,0:T(8,128)(2,1)S(1)}, bf16[15,16,256]{2,1,0:T(8,128)(2,1)S(1)}, u32[]{:S(2)}, u32[]{:S(2)}) collective-permute-start(bf16[15,16,256]{2,1,0:T(8,128)(2,1)S(1)} %get-tuple-element.23), channel_id=1, source_target_pairs={{1,2},{2,1},{3,4},{4,3},{5,6},{6,5},{7,8},{8,7},{9,10},{10,9},{11,... | collective-permute-start | bytes 368648 | tf_op jit(solution)/shard_map/ppermute | solution.py:39
  12.1 4.3 %collective-permute-start.4 = (bf16[15,16,256]{2,1,0:T(8,128)(2,1)S(1)}, bf16[15,16,256]{2,1,0:T(8,128)(2,1)S(1)}, u32[]{:S(2)}, u32[]{:S(2)}) collective-permute-start(bf16[15,16,256]{2,1,0:T(8,128)(2,1)S(1)} %get-tuple-element.27), channel_id=1, source_target_pairs={{1,17},{17,1},{2,18},{18,2},{3,19},{19,3},{4,20},{20,4},{5,21},{21... | collective-permute-start | bytes 368648 | tf_op jit(solution)/shard_map/ppermute | solution.py:55
  14.1 2.4 %collective-permute-start.5 = (bf16[15,16,256]{2,1,0:T(8,128)(2,1)S(1)}, bf16[15,16,256]{2,1,0:T(8,128)(2,1)S(1)}, u32[]{:S(2)}, u32[]{:S(2)}) collective-permute-start(bf16[15,16,256]{2,1,0:T(8,128)(2,1)S(1)} %get-tuple-element.28), channel_id=1, source_target_pairs={{17,33},{33,17},{18,34},{34,18},{19,35},{35,19},{20,36},{36,20},{2... | collective-permute-start | bytes 368648 | tf_op jit(solution)/shard_map/ppermute | solution.py:55
  14.7 1.7 %copy-start.2 = (s32[1,1,16,8]{2,3,1,0:T(8,128)S(1)}, s32[1,1,16,8]{2,3,1,0:T(8,128)}, u32[]{:S(2)}) copy-start(s32[1,1,16,8]{2,3,1,0:T(8,128)} %param.11) | copy-start | bytes 1540
  17.6 14.9 %copy-start.3 = (s32[1,1,16,8]{2,3,1,0:T(8,128)S(1)}, s32[1,1,16,8]{2,3,1,0:T(8,128)}, u32[]{:S(2)}) copy-start(s32[1,1,16,8]{2,3,1,0:T(8,128)} %param.12) | copy-start | bytes 1540
  17.6 29.6 %all-to-all-start = ((bf16[32,32,128]{2,1,0:T(8,128)(2,1)}), bf16[32,32,128]{2,1,0:T(8,128)(2,1)S(1)}, u32[]{:S(2)}, u32[]{:S(2)}) async-start(bf16[32,32,128]{2,1,0:T(8,128)(2,1)} %get-tuple-element.29), calls=%async_computation | async-start | bytes 524288 | tf_op jit(solution)/shard_map/all_to_all | solution.py:537
  32.7 14.5 %copy-start = (bf16[1,1,8,128,128]{4,3,2,1,0:T(8,128)(2,1)S(1)}, bf16[1,1,8,128,128]{4,3,2,1,0:T(8,128)(2,1)}, u32[]{:S(2)}) copy-start(bf16[1,1,8,128,128]{4,3,2,1,0:T(8,128)(2,1)} %param.10) | copy-start | bytes 786436
  36.2 11.0 %copy-start.1 = (s32[1,1,16,8]{2,3,1,0:T(8,128)S(1)}, s32[1,1,16,8]{2,3,1,0:T(8,128)}, u32[]{:S(2)}) copy-start(s32[1,1,16,8]{2,3,1,0:T(8,128)} %param.13) | copy-start | bytes 1540

commit v6 on v5

--- a/solution.py
+++ b/solution.py
@@ -237,7 +237,7 @@
     section = lax.axis_index("sec")
     slab = lax.axis_index("ax")
     slabs = packed.shape[0] // 2
-    sector_first, early_first, early_second, sector_second, late_first, late_second = messages
+    sector_first, early_second, early_first, sector_second, late_second, late_first = messages
     sector_up = jnp.where(upper_first("az"), 1, 0)
     slab_up = jnp.where(upper_first("ax"), 1, 0)
     for v in range(NV):
@@ -316,7 +316,7 @@
 
 def second_step(stepped, q, c, *rest):
     *messages, out, paths, rims, halos = rest
-    sector_first, early_first, early_second, sector_second, late_first, late_second = messages
+    sector_first, early_second, early_first, sector_second, late_second, late_first = messages
     sector_up = jnp.where(upper_first("az"), 1, 0)
     slab_up = jnp.where(upper_first("ax"), 1, 0)
     halos[sector_up] = sector_first[...]
@@ -511,11 +511,13 @@
         name="pack_halos",
     )(off_chip(current), off_chip(factors), off_chip(old_source))
     sector_first = swap(sends[0], "az", 0, True)
-    early = [swap_slabs(sends[2 + n], n, True) for n in range(2)]
+    early_second = swap_slabs(sends[3], 1, True)
+    early_first = swap_slabs(sends[2], 0, True)
     sector_second = swap(sends[1], "az", 1, True)
     sector_first, *sends = lax.optimization_barrier((sector_first, *sends))
-    late = [swap_slabs(sends[2 + n], n, False) for n in range(2)]
-    messages = [sector_first, early[0], early[1], sector_second, late[0], late[1]]
+    late_second = swap_slabs(sends[3], 1, False)
+    late_first = swap_slabs(sends[2], 0, False)
+    messages = [sector_first, early_second, early_first, sector_second, late_second, late_first]
     inner = pl.pallas_call(
         inner_step,
         in_specs=[VMEM] * 3,

time: 48.6 us -> 47.5 us (0.977)
  the two profiles are of different devices: /device:TPU:192 before, /device:TPU:1 now
where the time goes in v6:
time: 47.5 us; the launch traced here: 47.1 us
  starting transfers between devices  26.6 us (56%)
  waiting for transfers between devices  11.1 us (23%)
  Pallas kernels  9.16 us (19%)
    all_to_all x1, waiting for transfers between devices, shards(): lax.all_to_all(packed, ('sec', 'ax'), split_axis=0, concat_axis=0, tiled=...  9.72 us
    ppermute x2, starting transfers between devices, swap(): return lax.ppermute(x, axis, pairs)  9.4 us
    all_to_all x1, starting transfers between devices, shards(): lax.all_to_all(packed, ('sec', 'ax'), split_axis=0, concat_axis=0, tiled=...  9.28 us
    ppermute x4, starting transfers between devices, swap_slabs(): return lax.ppermute(x, ('sec', 'ax', 'az'), pairs)  7.88 us
    pallas_call x1, Pallas kernels, shards(): pl.pallas_call(second_step, in_specs=[VMEM] * 9, out_specs=[VMEM] * 2, ou...  3.5 us
    pallas_call x1, Pallas kernels, shards(): pl.pallas_call(pack_halos, in_specs=[ANY] * 3, out_specs=[VMEM] * 7, out_...  1.88 us
    pallas_call x1, Pallas kernels, shards(): pl.pallas_call(inner_step, in_specs=[VMEM] * 3, out_specs=VMEM, out_shape...  1.61 us
    ppermute x2, waiting for transfers between devices, swap(): return lax.ppermute(x, axis, pairs)  1.35 us
  transfers between devices with their start and end apart: 7, of which 2 were waited for; matrix products, arithmetic and copies ran while one was open for 0% of the time, Pallas kernels for 11%

profile of v6, /device:TPU:1, one launch (start us, length us, event | category | flops | bytes accessed | tf_op | source)
XLA Modules:
  0.0 47.1 jit_solution(2111772544507353724)
XLA Ops:
  0.0 1.9 %pack_halos.1 = (bf16[15,16,256]{2,1,0:T(8,128)(2,1)S(1)}, bf16[15,16,256]{2,1,0:T(8,128)(2,1)S(1)}, bf16[15,16,256]{2,1,0:T(8,128)(2,1)S(1)}, bf16[15,16,256]{2...) custom-call(f32[4,16,16,256]{3,2,1,0:T(8,128)} %bitcast.15, ...), custom_call_target="tpu_custom_call" | custom-call | tf_op jit(solution)/shard_map/pack_halos/pallas_call | solution.py:504
  1.9 4.8 %collective-permute-start = (bf16[15,16,256]{2,1,0:T(8,128)(2,1)S(1)}, bf16[15,16,256]{2,1,0:T(8,128)(2,1)S(1)}, u32[]{:S(2)}, u32[]{:S(2)}) collective-permute-start(bf16[15,16,256]{2,1,0:T(8,128)(2,1)S(1)} %get-tuple-element.22), channel_id=1, source_target_pairs={{0,1},{1,0},{2,3},{3,2},{4,5},{5,4},{6,7},{7,6},{8,9},{9,8},{10,11... | collective-permute-start | bytes 368648 | tf_op jit(solution)/shard_map/ppermute | solution.py:39
  6.7 4.0 %collective-permute-start.1 = (bf16[15,16,256]{2,1,0:T(8,128)(2,1)S(1)}, bf16[15,16,256]{2,1,0:T(8,128)(2,1)S(1)}, u32[]{:S(2)}, u32[]{:S(2)}) collective-permute-start(bf16[15,16,256]{2,1,0:T(8,128)(2,1)S(1)} %get-tuple-element.27), channel_id=1, source_target_pairs={{16,32},{32,16},{24,40},{40,24},{48,64},{64,48},{56,72},{72,56},{8... | collective-permute-start | bytes 368648 | tf_op jit(solution)/shard_map/ppermute | solution.py:55
  10.8 2.5 %collective-permute-start.2 = (bf16[15,16,256]{2,1,0:T(8,128)(2,1)S(1)}, bf16[15,16,256]{2,1,0:T(8,128)(2,1)S(1)}, u32[]{:S(2)}, u32[]{:S(2)}) collective-permute-start(bf16[15,16,256]{2,1,0:T(8,128)(2,1)S(1)} %get-tuple-element.28), channel_id=1, source_target_pairs={{0,16},{16,0},{8,24},{24,8},{32,48},{48,32},{40,56},{56,40},{64,80... | collective-permute-start | bytes 368648 | tf_op jit(solution)/shard_map/ppermute | solution.py:55
  13.3 4.6 %collective-permute-start.3 = (bf16[15,16,256]{2,1,0:T(8,128)(2,1)S(1)}, bf16[15,16,256]{2,1,0:T(8,128)(2,1)S(1)}, u32[]{:S(2)}, u32[]{:S(2)}) collective-permute-start(bf16[15,16,256]{2,1,0:T(8,128)(2,1)S(1)} %get-tuple-element.23), channel_id=1, source_target_pairs={{1,2},{2,1},{3,4},{4,3},{5,6},{6,5},{7,8},{8,7},{9,10},{10,9},{11,... | collective-permute-start | bytes 368648 | tf_op jit(solution)/shard_map/ppermute | solution.py:39
  17.9 0.0 collective-permute-done.rest_0_
  17.9 0.7 %collective-permute-start.4 = (bf16[15,16,256]{2,1,0:T(8,128)(2,1)S(1)}, bf16[15,16,256]{2,1,0:T(8,128)(2,1)S(1)}, u32[]{:S(2)}, u32[]{:S(2)}) collective-permute-start(bf16[15,16,256]{2,1,0:T(8,128)(2,1)S(1)} %get-tuple-element.27), channel_id=1, source_target_pairs={{17,33},{33,17},{18,34},{34,18},{19,35},{35,19},{20,36},{36,20},{2... | collective-permute-start | bytes 368648 | tf_op jit(solution)/shard_map/ppermute | solution.py:55
  18.6 0.7 %collective-permute-start.5 = (bf16[15,16,256]{2,1,0:T(8,128)(2,1)S(1)}, bf16[15,16,256]{2,1,0:T(8,128)(2,1)S(1)}, u32[]{:S(2)}, u32[]{:S(2)}) collective-permute-start(bf16[15,16,256]{2,1,0:T(8,128)(2,1)S(1)} %get-tuple-element.28), channel_id=1, source_target_pairs={{1,17},{17,1},{2,18},{18,2},{3,19},{19,3},{4,20},{20,4},{5,21},{21... | collective-permute-start | bytes 368648 | tf_op jit(solution)/shard_map/ppermute | solution.py:55
  19.2 0.0 copy-start.2
  19.2 1.6 %inner_step.1.inner = f32[4,16,16,256]{3,2,1,0:T(8,128)S(1)} custom-call(f32[4,16,16,256]{3,2,1,0:T(8,128)S(1)} %get-tuple-element.19.q, f32[3,16,16,256]{3,2,1,0:T(8,128)S(1)} %get-tuple-element.20.c, f32[4,16,16,256]{3,2,1,0:T(8,128)S(1)} %get-tuple-element.21.s), custom_call_target="tpu_custom_call" | custom-call | tf_op jit(solution)/shard_map/inner_step/pallas_call | solution.py:521
  20.9 0.0 collective-permute-done.1.rest_1_
  20.9 0.0 collective-permute-done.2.rest_2_
  20.9 1.4 %collective-permute-done.3.rest_3_ = bf16[15,16,256]{2,1,0:T(8,128)(2,1)S(1)} collective-permute-done((bf16[15,16,256]{2,1,0:T(8,128)(2,1)S(1)}, bf16[15,16,256]{2,1,0:T(8,128)(2,1)S(1)}, u32[]{:S(2)}, u32[]{:S(2)}) %collective-permute-start.3) | collective-permute-done | bytes 122912 | tf_op jit(solution)/shard_map/ppermute | solution.py:39
  22.2 0.0 collective-permute-done.4.rest_4_
  22.2 0.0 collective-permute-done.5.rest_5_
  22.2 0.0 copy-done.2
  22.2 1.1 %first_step.1 = (f32[4,16,16,256]{3,2,1,0:T(8,128)S(1)}, bf16[32,32,128]{2,1,0:T(8,128)(2,1)}) custom-call(s32[8,16]{1,0:T(8,128)S(1)} %bitcast.14, f32[4,16,16,256]{3,2,1,0:T(8,128)S(1)} %inner_step.1.inner, f32[4,16,16,256]{3,2,1,0:T(8,128)S(1)} %get-tuple-element.19.q, ...), custom_call_target="tpu_custom_call", output_to_operand_aliasing={{0}: (1, {})} | custom-call | tf_op jit(solution)/shard_map/first_step/pallas_call | solution.py:529
  23.4 0.0 copy-start.3
  23.4 9.3 %all-to-all-start = ((bf16[32,32,128]{2,1,0:T(8,128)(2,1)}), bf16[32,32,128]{2,1,0:T(8,128)(2,1)S(1)}, u32[]{:S(2)}, u32[]{:S(2)}) async-start(bf16[32,32,128]{2,1,0:T(8,128)(2,1)} %get-tuple-element.29), calls=%async_computation | async-start | bytes 524288 | tf_op jit(solution)/shard_map/all_to_all | solution.py:539
  32.7 0.0 copy-done.3
  32.7 0.1 copy.10
  32.8 0.1 reshape.3.targets
  32.9 0.0 copy-start
  32.9 3.5 %second_step.1 = (f32[4,16,16,256]{3,2,1,0:T(8,128)S(1)}, f32[2,2,8,256]{3,2,1,0:T(8,128)S(1)}) custom-call(f32[4,16,16,256]{3,2,1,0:T(8,128)S(1)} %get-tuple-element.30.stepped, f32[4,16,16,256]{3,2,1,0:T(8,128)} %bitcast.16, f32[3,16,16,256]{3,2,1,0:T(8,128)} %bitcast.18, bf16[15,16,256]{2,1,0:T(8,128)(2,1)S(1)} %collective-permute-done.rest_0_, ...), custom_call_target="tpu_custom_call" | custom-call | tf_op jit(solution)/shard_map/second_step/pallas_call | solution.py:540
  36.4 0.0 copy-start.1
  36.4 9.7 %all-to-all-done.received = bf16[32,32,128]{2,1,0:T(8,128)(2,1)S(1)} async-done(((bf16[32,32,128]{2,1,0:T(8,128)(2,1)}), bf16[32,32,128]{2,1,0:T(8,128)(2,1)S(1)}, u32[]{:S(2)}, u32[]{:S(2)}) %all-to-all-start) | async-done | bytes 262176 | tf_op jit(solution)/shard_map/all_to_all | solution.py:539
  46.1 0.0 copy-done
  46.1 0.0 copy-done.1
  46.1 1.0 %add_source.1 = f32[4,16,16,256]{3,2,1,0:T(8,128)} custom-call(s32[1,128]{1,0:T(1,128)S(1)} %reshape.3.targets, s32[8,16]{1,0:T(8,128)S(1)} %bitcast.13, bf16[32,32,128]{2,1,0:T(8,128)(2,1)S(1)} %all-to-all-done.received, bf16[8,128,128]{2,1,0:T(8,128)(2,1)S(1)} %bitcast.12, f32[4,16,16,256]{3,2,1,0:T(8,128)S(1)} %get-tuple-element.31.base, ...), custom_call_target="tpu_custom_call" | custom-call | tf_op jit(solution)/shard_map/add_source/pallas_call | solution.py:555
Async XLA Ops:
  1.9 16.0 %collective-permute-start = (bf16[15,16,256]{2,1,0:T(8,128)(2,1)S(1)}, bf16[15,16,256]{2,1,0:T(8,128)(2,1)S(1)}, u32[]{:S(2)}, u32[]{:S(2)}) collective-permute-start(bf16[15,16,256]{2,1,0:T(8,128)(2,1)S(1)} %get-tuple-element.22), channel_id=1, source_target_pairs={{0,1},{1,0},{2,3},{3,2},{4,5},{5,4},{6,7},{7,6},{8,9},{9,8},{10,11... | collective-permute-start | bytes 368648 | tf_op jit(solution)/shard_map/ppermute | solution.py:39
  6.7 14.1 %collective-permute-start.1 = (bf16[15,16,256]{2,1,0:T(8,128)(2,1)S(1)}, bf16[15,16,256]{2,1,0:T(8,128)(2,1)S(1)}, u32[]{:S(2)}, u32[]{:S(2)}) collective-permute-start(bf16[15,16,256]{2,1,0:T(8,128)(2,1)S(1)} %get-tuple-element.27), channel_id=1, source_target_pairs={{16,32},{32,16},{24,40},{40,24},{48,64},{64,48},{56,72},{72,56},{8... | collective-permute-start | bytes 368648 | tf_op jit(solution)/shard_map/ppermute | solution.py:55
  10.8 10.1 %collective-permute-start.2 = (bf16[15,16,256]{2,1,0:T(8,128)(2,1)S(1)}, bf16[15,16,256]{2,1,0:T(8,128)(2,1)S(1)}, u32[]{:S(2)}, u32[]{:S(2)}) collective-permute-start(bf16[15,16,256]{2,1,0:T(8,128)(2,1)S(1)} %get-tuple-element.28), channel_id=1, source_target_pairs={{0,16},{16,0},{8,24},{24,8},{32,48},{48,32},{40,56},{56,40},{64,80... | collective-permute-start | bytes 368648 | tf_op jit(solution)/shard_map/ppermute | solution.py:55
  13.3 8.9 %collective-permute-start.3 = (bf16[15,16,256]{2,1,0:T(8,128)(2,1)S(1)}, bf16[15,16,256]{2,1,0:T(8,128)(2,1)S(1)}, u32[]{:S(2)}, u32[]{:S(2)}) collective-permute-start(bf16[15,16,256]{2,1,0:T(8,128)(2,1)S(1)} %get-tuple-element.23), channel_id=1, source_target_pairs={{1,2},{2,1},{3,4},{4,3},{5,6},{6,5},{7,8},{8,7},{9,10},{10,9},{11,... | collective-permute-start | bytes 368648 | tf_op jit(solution)/shard_map/ppermute | solution.py:39
  17.9 4.4 %collective-permute-start.4 = (bf16[15,16,256]{2,1,0:T(8,128)(2,1)S(1)}, bf16[15,16,256]{2,1,0:T(8,128)(2,1)S(1)}, u32[]{:S(2)}, u32[]{:S(2)}) collective-permute-start(bf16[15,16,256]{2,1,0:T(8,128)(2,1)S(1)} %get-tuple-element.27), channel_id=1, source_target_pairs={{17,33},{33,17},{18,34},{34,18},{19,35},{35,19},{20,36},{36,20},{2... | collective-permute-start | bytes 368648 | tf_op jit(solution)/shard_map/ppermute | solution.py:55
  18.6 3.7 %collective-permute-start.5 = (bf16[15,16,256]{2,1,0:T(8,128)(2,1)S(1)}, bf16[15,16,256]{2,1,0:T(8,128)(2,1)S(1)}, u32[]{:S(2)}, u32[]{:S(2)}) collective-permute-start(bf16[15,16,256]{2,1,0:T(8,128)(2,1)S(1)} %get-tuple-element.28), channel_id=1, source_target_pairs={{1,17},{17,1},{2,18},{18,2},{3,19},{19,3},{4,20},{20,4},{5,21},{21... | collective-permute-start | bytes 368648 | tf_op jit(solution)/shard_map/ppermute | solution.py:55
  19.2 3.0 %copy-start.2 = (s32[1,1,16,8]{2,3,1,0:T(8,128)S(1)}, s32[1,1,16,8]{2,3,1,0:T(8,128)}, u32[]{:S(2)}) copy-start(s32[1,1,16,8]{2,3,1,0:T(8,128)} %param.11) | copy-start | bytes 1540
  23.4 9.3 %copy-start.3 = (s32[1,1,16,8]{2,3,1,0:T(8,128)S(1)}, s32[1,1,16,8]{2,3,1,0:T(8,128)}, u32[]{:S(2)}) copy-start(s32[1,1,16,8]{2,3,1,0:T(8,128)} %param.12) | copy-start | bytes 1540
  23.4 22.7 %all-to-all-start = ((bf16[32,32,128]{2,1,0:T(8,128)(2,1)}), bf16[32,32,128]{2,1,0:T(8,128)(2,1)S(1)}, u32[]{:S(2)}, u32[]{:S(2)}) async-start(bf16[32,32,128]{2,1,0:T(8,128)(2,1)} %get-tuple-element.29), calls=%async_computation | async-start | bytes 524288 | tf_op jit(solution)/shard_map/all_to_all | solution.py:539
  32.9 13.3 %copy-start = (bf16[1,1,8,128,128]{4,3,2,1,0:T(8,128)(2,1)S(1)}, bf16[1,1,8,128,128]{4,3,2,1,0:T(8,128)(2,1)}, u32[]{:S(2)}) copy-start(bf16[1,1,8,128,128]{4,3,2,1,0:T(8,128)(2,1)} %param.10) | copy-start | bytes 786436
  36.4 9.7 %copy-start.1 = (s32[1,1,16,8]{2,3,1,0:T(8,128)S(1)}, s32[1,1,16,8]{2,3,1,0:T(8,128)}, u32[]{:S(2)}) copy-start(s32[1,1,16,8]{2,3,1,0:T(8,128)} %param.13) | copy-start | bytes 1540

commit v7 on v6

--- a/solution.py
+++ b/solution.py
@@ -1,3 +1,5 @@
+import functools
+
 import jax
 import jax.numpy as jnp
 from jax import lax
@@ -16,10 +18,9 @@
 NW = 8
 
 NEAR = 0
-FAR = 4
+BEYOND = 4
 COEF = 8
-SOURCE = 11
-PLANES = 15
+PLANES = 11
 
 VMEM = pl.BlockSpec(memory_space=pltpu.VMEM)
 ANY = pl.BlockSpec(memory_space=pl.ANY)
@@ -31,16 +32,24 @@
     return pltpu.with_memory_space_constraint(x, pltpu.HBM)
 
 
-def swap(x, axis, first, periodic):
-    count = lax.axis_size(axis)
-    pairs = []
-    for i in range(first, count if periodic else count - 1, 2):
-        pairs += [(i, (i + 1) % count), ((i + 1) % count, i)]
-    return lax.ppermute(x, axis, pairs)
+def shift_sectors(x, pairs):
+    count = lax.axis_size("az")
+    half = count // 2
+    pairs = [
+        ((source + start) % count, (target + start) % count)
+        for start in (0, half)
+        for source, target in pairs
+    ]
+    return lax.ppermute(x, "az", pairs)
+
+
+def both_ways(firsts):
+    return [pair for i in firsts for pair in ((i, i + 1), (i + 1, i))]
 
 
 def is_early(sector, sectors):
-    return sector % (sectors // 2) == 0
+    place = sector % (sectors // 2)
+    return (place == 0) | (place == 1) | (place == 3)
 
 
 def swap_slabs(x, first, early):
@@ -49,7 +58,8 @@
     for section in range(sections):
         for slab in range(first, slabs - 1, 2):
             for sector in range(sectors):
-                if is_early(sector, sectors) == early:
+                ahead = sector % (sectors // 2) == 0 if first == 0 else is_early(sector, sectors)
+                if ahead == early:
                     low = (section * slabs + slab) * sectors + sector
                     pairs += [(low, low + sectors), (low + sectors, low)]
     return lax.ppermute(x, ("sec", "ax", "az"), pairs)
@@ -158,24 +168,59 @@
     for copy in copies:
         copy.start()
 
-    def fill(ref, component, plane, depth):
-        high = jnp.where(slab_up, C1 - 1 - depth, depth)
-        slab_first[plane] = ref[component, high].astype(BF16)
-        slab_second[plane] = ref[component, C1 - 1 - high].astype(BF16)
+    def slab(ref, component, depth, upper):
+        return ref[component, jnp.where(upper, C1 - 1 - depth, depth)]
+
+    def sector(ref, component, depth, upper):
         low = column(ref, component, depth)
-        high = column(ref, component, C2 - 1 - depth)
-        sector_first[plane] = jnp.where(sector_up, high, low).astype(BF16)
-        sector_second[plane] = jnp.where(sector_up, low, high).astype(BF16)
-
-    for n, copy in enumerate(copies):
+        return jnp.where(upper, column(ref, component, C2 - 1 - depth), low)
+
+    plans = []
+    for first, second, take, up, k in (
+        (sector_first, sector_second, sector, sector_up, 1),
+        (slab_first, slab_second, slab, slab_up, 0),
+    ):
+        plans.append((first, take, up, k))
+        plans.append((second, take, jnp.logical_not(up), k))
+
+    for copy in copies[:NV]:
         copy.wait()
-        if n < NV:
-            fill(cells, n, NEAR + n, 0)
-            fill(cells, n, FAR + n, 1)
-        elif n < NV + 3:
-            fill(factors, n - NV, COEF + n - NV, 0)
-        else:
-            fill(source, n - NV - 3, SOURCE + n - NV - 3, 0)
+    near = []
+    far = []
+    for out, take, upper, k in plans:
+        near.append([take(cells, v, 0, upper) for v in range(NV)])
+        far.append([take(cells, v, 1, upper) for v in range(NV)])
+        for v in range(NV):
+            out[NEAR + v] = near[-1][v].astype(BF16)
+    for copy in copies[NV : NV + 3]:
+        copy.wait()
+    factor = []
+    for out, take, upper, k in plans:
+        planes = [take(factors, n, 0, upper) for n in range(3)]
+        factor.append(planes[k])
+        for n in range(3):
+            out[COEF + n] = planes[n].astype(BF16)
+    for copy in copies[NV + 3 :]:
+        copy.wait()
+
+    def beyond(acoustic):
+        for n, (out, take, upper, k) in enumerate(plans):
+            sign = jnp.where(upper, 1.0, -1.0)
+            terms = border_terms(acoustic, far[n], near[n][k], factor[n], k, sign)
+            for v in range(NV):
+                if acoustic:
+                    terms[v] += 0.25 * take(source, v, 0, upper)
+                out[BEYOND + v] = terms[v].astype(BF16)
+
+    section = lax.axis_index("sec")
+
+    @pl.when(section == 0)
+    def _():
+        beyond(False)
+
+    @pl.when(section != 0)
+    def _():
+        beyond(True)
 
 
 def fields_of(message, start, count=NV):
@@ -204,15 +249,17 @@
     return [(nothing, nothing)] * NV
 
 
-def inner_step(q, c, s, out):
+def inner_step(early, q, c, s, *rest):
+    out = rest[-1]
     section = lax.axis_index("sec")
+    mine = is_early(lax.axis_index("az"), lax.axis_size("az")) == early
     nothing = [jnp.zeros((C2, C3), F32)] * NV
 
-    @pl.when(section == 0)
+    @pl.when(mine & (section == 0))
     def _():
         step_rows(False, q, c, None, nothing, nothing, no_ends, out)
 
-    @pl.when(section != 0)
+    @pl.when(mine & (section != 0))
     def _():
         step_rows(True, q, c, s, nothing, nothing, no_ends, out)
 
@@ -224,8 +271,7 @@
     return results
 
 
-def border_terms(acoustic, near, flow, factor, k, side):
-    sign = 1.0 - 2.0 * side
+def border_terms(acoustic, near, flow, factor, k, sign):
     if acoustic:
         return [sign * term for term in coupled(near, 0.125 * factor, k)]
     weight = 0.25 * factor + (sign * 0.125) * flow
@@ -237,13 +283,14 @@
     section = lax.axis_index("sec")
     slab = lax.axis_index("ax")
     slabs = packed.shape[0] // 2
-    sector_first, early_second, early_first, sector_second, late_second, late_first = messages
+    wrapped, sector_first, early_second, early_first = messages[:4]
+    sector_second, last_first, late_second, late_first = messages[4:]
     sector_up = jnp.where(upper_first("az"), 1, 0)
     slab_up = jnp.where(upper_first("ax"), 1, 0)
     for v in range(NV):
         plane = NEAR + v
-        sides[sector_up, v] = sector_first[plane].astype(F32)
-        sides[1 - sector_up, v] = sector_second[plane].astype(F32)
+        sides[sector_up, v] = joined(sector_first[plane], last_first[plane])
+        sides[1 - sector_up, v] = joined(wrapped[plane], sector_second[plane])
         faces[slab_up, v] = joined(early_first[plane], late_first[plane])
         faces[1 - slab_up, v] = joined(early_second[plane], late_second[plane])
 
@@ -251,7 +298,7 @@
         for side in range(2):
             i = side * (C1 - 1)
             near = [faces[side, v] for v in range(NV)]
-            terms = border_terms(acoustic, near, q[0, i], c[0, i], 0, side)
+            terms = border_terms(acoustic, near, q[0, i], c[0, i], 0, 1.0 - 2.0 * side)
             for v in range(NV):
                 stepped[v, i] += terms[v]
         for i in range(C1):
@@ -260,7 +307,7 @@
                 near = [sides[side, v, i : i + 1, :] for v in range(NV)]
                 flow = q[1, i, j : j + 1, :]
                 factor = c[1, i, j : j + 1, :]
-                terms = border_terms(acoustic, near, flow, factor, 1, side)
+                terms = border_terms(acoustic, near, flow, factor, 1, 1.0 - 2.0 * side)
                 for v in range(NV):
                     stepped[v, i, j : j + 1, :] += terms[v]
 
@@ -316,11 +363,12 @@
 
 def second_step(stepped, q, c, *rest):
     *messages, out, paths, rims, halos = rest
-    sector_first, early_second, early_first, sector_second, late_second, late_first = messages
+    wrapped, sector_first, early_second, early_first = messages[:4]
+    sector_second, last_first, late_second, late_first = messages[4:]
     sector_up = jnp.where(upper_first("az"), 1, 0)
     slab_up = jnp.where(upper_first("ax"), 1, 0)
-    halos[sector_up] = sector_first[...]
-    halos[1 - sector_up] = sector_second[...]
+    halos[sector_up] = joined(sector_first[...], last_first[...]).astype(BF16)
+    halos[1 - sector_up] = joined(wrapped[...], sector_second[...]).astype(BF16)
     halos[2 + slab_up] = joined(early_first[...], late_first[...]).astype(BF16)
     halos[3 - slab_up] = joined(early_second[...], late_second[...]).astype(BF16)
     left, right, below, above = (halos.at[n] for n in range(4))
@@ -334,11 +382,12 @@
 
         def rim(message, across, own, side):
             near = fields_of(message, NEAR)
-            far = fields_of(message, FAR)
-            upper, lower = (own, far) if side == 0 else (far, own)
-            source = fields_of(message, SOURCE) if acoustic else None
+            beyond = fields_of(message, BEYOND)
+            none = [jnp.zeros((C1, C3), F32)] * NV
+            upper, lower = (own, none) if side == 0 else (none, own)
             factors = fields_of(message, COEF, 3)
-            return plane_step(acoustic, near, upper, lower, ends, factors, across, source)
+            results = plane_step(acoustic, near, upper, lower, ends, factors, across, None)
+            return [results[v] + beyond[v] for v in range(NV)]
 
         for side, message in enumerate((left, right)):
             own = [column(q, v, side * (C2 - 1)) for v in range(NV)]
@@ -458,15 +507,16 @@
     @pl.when(section != 0)
     def _():
         kinds = weights[...]
-        masks = []
-        for a in range(slabs):
-            kind = jnp.broadcast_to(kinds[:, a : a + 1], (CAP, LINE))
-            masks.append(jnp.concatenate([kind] * NV, axis=0))
+        owners = [jnp.broadcast_to(kinds[:, a : a + 1], (CAP, LINE)) for a in range(slabs)]
+        given = [received[a] for a in range(slabs)]
         placed = []
         for w in range(NW):
             parts = []
             for a in range(slabs):
-                parts.append(jnp.where(masks[a] == w, 1.0, 0.0).astype(BF16) * received[a])
+                mask = jnp.where(owners[a] == w, 1.0, 0.0)
+                mask = jnp.concatenate([mask, mask], axis=0).astype(BF16)
+                for start in range(0, CAP * NV, 2 * CAP):
+                    parts.append(mask * given[a][start : start + 2 * CAP])
             placed.append(jnp.concatenate(parts, axis=0))
         placed = jnp.concatenate(placed, axis=1)
         stacked = jnp.concatenate([blocks[w] for w in range(NW)], axis=1)
@@ -510,25 +560,39 @@
         compiler_params=PARAMS,
         name="pack_halos",
     )(off_chip(current), off_chip(factors), off_chip(old_source))
-    sector_first = swap(sends[0], "az", 0, True)
+    last = lax.axis_size("az") // 2 - 1
+    wrapped = shift_sectors(sends[1], [(last, last + 1)])
+    sector_first = shift_sectors(sends[0], both_ways(range(0, last - 1, 2)))
     early_second = swap_slabs(sends[3], 1, True)
     early_first = swap_slabs(sends[2], 0, True)
-    sector_second = swap(sends[1], "az", 1, True)
-    sector_first, *sends = lax.optimization_barrier((sector_first, *sends))
-    late_second = swap_slabs(sends[3], 1, False)
-    late_first = swap_slabs(sends[2], 0, False)
-    messages = [sector_first, early_second, early_first, sector_second, late_second, late_first]
     inner = pl.pallas_call(
-        inner_step,
+        functools.partial(inner_step, True),
         in_specs=[VMEM] * 3,
         out_specs=VMEM,
         out_shape=field,
         compiler_params=PARAMS,
-        name="inner_step",
+        name="inner_step_early",
     )(kept, kept_factors, kept_source)
+    inner, sends[1] = lax.optimization_barrier((inner, sends[1]))
+    sector_second = shift_sectors(sends[1], both_ways(range(1, last - 1, 2)) + [(last + 1, last)])
+    sector_first, *sends = lax.optimization_barrier((sector_first, *sends))
+    last_first = shift_sectors(sends[0], both_ways([last - 1]))
+    late_second = swap_slabs(sends[3], 1, False)
+    late_first = swap_slabs(sends[2], 0, False)
+    messages = [wrapped, sector_first, early_second, early_first]
+    messages += [sector_second, last_first, late_second, late_first]
+    inner = pl.pallas_call(
+        functools.partial(inner_step, False),
+        in_specs=[VMEM] * 4,
+        out_specs=VMEM,
+        out_shape=field,
+        input_output_aliases={3: 0},
+        compiler_params=PARAMS,
+        name="inner_step_late",
+    )(kept, kept_factors, kept_source, inner)
     stepped, packed = pl.pallas_call(
         first_step,
-        in_specs=[VMEM] * 10,
+        in_specs=[VMEM] * 12,
         out_specs=[VMEM] * 2,
         out_shape=[field, pltpu.HBM((peers, CAP * NV, LINE), BF16)],
         input_output_aliases={1: 0},
@@ -539,7 +603,7 @@
     received = lax.all_to_all(packed, ("sec", "ax"), split_axis=0, concat_axis=0, tiled=True)
     base, paths = pl.pallas_call(
         second_step,
-        in_specs=[VMEM] * 9,
+        in_specs=[VMEM] * 11,
         out_specs=[VMEM] * 2,
         out_shape=[
             field,

time: 47.5 us -> 47 us (0.989)
  waiting for transfers between devices: 11.1 us -> 9.71 us
  local copies, waits for them, and re-layouts: 0.18 us -> 0.77 us
    ppermute x2 -> x4, waiting for transfers between devices: 1.35 us -> 0.01 us  [shift_sectors(): return lax.ppermute(x, 'az', pairs)]
    ppermute x2 -> x4, starting transfers between devices: 9.4 us -> 8.24 us  [shift_sectors(): return lax.ppermute(x, 'az', pairs)]
    all_to_all x1, starting transfers between devices: 9.28 us -> 10.4 us  [shards(): lax.all_to_all(packed, ('sec', 'ax'), split_axis=0, concat_axis=0, tiled=...]
    unnamed x9, local copies, waits for them, and re-layouts: 0.09 us -> 0.68 us
    pallas_call x3 -> x4, Pallas kernels: 6.26 us -> 6.33 us  [the longest x1 3.52 us: shards(): pl.pallas_call(second_step, in_specs=[VMEM] * 11, out_specs=[VMEM] * 2, o...]
  transfers between devices with their start and end apart: 7 -> 9, of which waited for: 2 -> 1; matrix products, arithmetic and copies ran while one was open for 0% -> 0% of each run, Pallas kernels for 11% -> 11%
where the time goes in v7:
time: 47 us; the launch traced here: 46.6 us
  starting transfers between devices  26.5 us (56%)
  waiting for transfers between devices  9.71 us (21%)
  Pallas kernels  9.39 us (20%)
  local copies, waits for them, and re-layouts  0.77 us (2%)
    all_to_all x1, starting transfers between devices, shards(): lax.all_to_all(packed, ('sec', 'ax'), split_axis=0, concat_axis=0, tiled=...  10.4 us
    all_to_all x1, waiting for transfers between devices, shards(): lax.all_to_all(packed, ('sec', 'ax'), split_axis=0, concat_axis=0, tiled=...  9.69 us
    ppermute x4, starting transfers between devices, shift_sectors(): return lax.ppermute(x, 'az', pairs)  8.24 us
    ppermute x4, starting transfers between devices, swap_slabs(): return lax.ppermute(x, ('sec', 'ax', 'az'), pairs)  7.88 us
    pallas_call x1, Pallas kernels, shards(): pl.pallas_call(second_step, in_specs=[VMEM] * 11, out_specs=[VMEM] * 2, o...  3.52 us
    pallas_call x1, Pallas kernels, shards(): pl.pallas_call(pack_halos, in_specs=[ANY] * 3, out_specs=[VMEM] * 7, out_...  2.04 us
    pallas_call x1, Pallas kernels, shards(): pl.pallas_call(functools.partial(inner_step, True), in_specs=[VMEM] * 3,...  1.62 us
    pallas_call x1, Pallas kernels, shards(): pl.pallas_call(first_step, in_specs=[VMEM] * 12, out_specs=[VMEM] * 2, ou...  1.15 us
  transfers between devices with their start and end apart: 9, of which 1 were waited for; matrix products, arithmetic and copies ran while one was open for 0% of the time, Pallas kernels for 11%

profile of v7, /device:TPU:1, one launch (start us, length us, event | category | flops | bytes accessed | tf_op | source)
XLA Modules:
  0.0 46.6 jit_solution(1782123304847670110)
XLA Ops:
  0.0 2.0 %pack_halos.1 = (bf16[11,16,256]{2,1,0:T(8,128)(2,1)S(1)}, bf16[11,16,256]{2,1,0:T(8,128)(2,1)S(1)}, bf16[11,16,256]{2,1,0:T(8,128)(2,1)S(1)}, bf16[11,16,256]{2...) custom-call(f32[4,16,16,256]{3,2,1,0:T(8,128)} %bitcast.15, ...), custom_call_target="tpu_custom_call" | custom-call | tf_op jit(solution)/shard_map/pack_halos/pallas_call | solution.py:554
  2.0 4.8 %collective-permute-start.1 = (bf16[11,16,256]{2,1,0:T(8,128)(2,1)S(1)}, bf16[11,16,256]{2,1,0:T(8,128)(2,1)S(1)}, u32[]{:S(2)}, u32[]{:S(2)}) collective-permute-start(bf16[11,16,256]{2,1,0:T(8,128)(2,1)S(1)} %get-tuple-element.32), channel_id=1, source_target_pairs={{0,1},{1,0},{2,3},{3,2},{4,5},{5,4},{8,9},{9,8},{10,11},{11,10},{1... | collective-permute-start | bytes 270344 | tf_op jit(solution)/shard_map/ppermute | solution.py:43
  6.9 1.3 %collective-permute-start = (bf16[11,16,256]{2,1,0:T(8,128)(2,1)S(1)}, bf16[11,16,256]{2,1,0:T(8,128)(2,1)S(1)}, u32[]{:S(2)}, u32[]{:S(2)}) collective-permute-start(bf16[11,16,256]{2,1,0:T(8,128)(2,1)S(1)} %get-tuple-element.28), channel_id=1, source_target_pairs={{7,8},{15,0},{23,24},{31,16},{39,40},{47,32},{55,56},{63,48},{71,7... | collective-permute-start | bytes 270344 | tf_op jit(solution)/shard_map/ppermute | solution.py:43
  8.2 4.0 %collective-permute-start.2 = (bf16[11,16,256]{2,1,0:T(8,128)(2,1)S(1)}, bf16[11,16,256]{2,1,0:T(8,128)(2,1)S(1)}, u32[]{:S(2)}, u32[]{:S(2)}) collective-permute-start(bf16[11,16,256]{2,1,0:T(8,128)(2,1)S(1)} %get-tuple-element.33), channel_id=1, source_target_pairs={{16,32},{32,16},{17,33},{33,17},{19,35},{35,19},{24,40},{40,24},{2... | collective-permute-start | bytes 270344 | tf_op jit(solution)/shard_map/ppermute | solution.py:65
  12.2 2.5 %collective-permute-start.3 = (bf16[11,16,256]{2,1,0:T(8,128)(2,1)S(1)}, bf16[11,16,256]{2,1,0:T(8,128)(2,1)S(1)}, u32[]{:S(2)}, u32[]{:S(2)}) collective-permute-start(bf16[11,16,256]{2,1,0:T(8,128)(2,1)S(1)} %get-tuple-element.34), channel_id=1, source_target_pairs={{0,16},{16,0},{8,24},{24,8},{32,48},{48,32},{40,56},{56,40},{64,80... | collective-permute-start | bytes 270344 | tf_op jit(solution)/shard_map/ppermute | solution.py:65
  14.7 1.6 %inner_step_early.1.rest_0_ = f32[4,16,16,256]{3,2,1,0:T(8,128)S(1)} custom-call(f32[4,16,16,256]{3,2,1,0:T(8,128)S(1)} %get-tuple-element.22.q, f32[3,16,16,256]{3,2,1,0:T(8,128)S(1)} %get-tuple-element.23.c, f32[4,16,16,256]{3,2,1,0:T(8,128)S(1)} %get-tuple-element.24.s), custom_call_target="tpu_custom_call" | custom-call | tf_op jit(solution)/shard_map/inner_step_early/pallas_call | solution.py:568
  16.4 1.5 %collective-permute-start.4 = (bf16[11,16,256]{2,1,0:T(8,128)(2,1)S(1)}, bf16[11,16,256]{2,1,0:T(8,128)(2,1)S(1)}, u32[]{:S(2)}, u32[]{:S(2)}) collective-permute-start(bf16[11,16,256]{2,1,0:T(8,128)(2,1)S(1)} %get-tuple-element.28), channel_id=1, source_target_pairs={{1,2},{2,1},{3,4},{4,3},{5,6},{6,5},{8,7},{9,10},{10,9},{11,12},{1... | collective-permute-start | bytes 270344 | tf_op jit(solution)/shard_map/ppermute | solution.py:43
  17.8 0.0 collective-permute-done.1.rest_1_
  17.8 0.7 %collective-permute-start.5 = (bf16[11,16,256]{2,1,0:T(8,128)(2,1)S(1)}, bf16[11,16,256]{2,1,0:T(8,128)(2,1)S(1)}, u32[]{:S(2)}, u32[]{:S(2)}) collective-permute-start(bf16[11,16,256]{2,1,0:T(8,128)(2,1)S(1)} %get-tuple-element.32), channel_id=1, source_target_pairs={{6,7},{7,6},{14,15},{15,14},{22,23},{23,22},{30,31},{31,30},{38,39... | collective-permute-start | bytes 270344 | tf_op jit(solution)/shard_map/ppermute | solution.py:43
  18.5 0.0 collective-permute-done.rest_0_
  18.5 0.7 %collective-permute-start.6 = (bf16[11,16,256]{2,1,0:T(8,128)(2,1)S(1)}, bf16[11,16,256]{2,1,0:T(8,128)(2,1)S(1)}, u32[]{:S(2)}, u32[]{:S(2)}) collective-permute-start(bf16[11,16,256]{2,1,0:T(8,128)(2,1)S(1)} %get-tuple-element.33), channel_id=1, source_target_pairs={{18,34},{34,18},{20,36},{36,20},{21,37},{37,21},{22,38},{38,22},{2... | collective-permute-start | bytes 270344 | tf_op jit(solution)/shard_map/ppermute | solution.py:65
  19.2 0.0 collective-permute-done.2.rest_2_
  19.2 0.7 %collective-permute-start.7 = (bf16[11,16,256]{2,1,0:T(8,128)(2,1)S(1)}, bf16[11,16,256]{2,1,0:T(8,128)(2,1)S(1)}, u32[]{:S(2)}, u32[]{:S(2)}) collective-permute-start(bf16[11,16,256]{2,1,0:T(8,128)(2,1)S(1)} %get-tuple-element.34), channel_id=1, source_target_pairs={{1,17},{17,1},{2,18},{18,2},{3,19},{19,3},{4,20},{20,4},{5,21},{21... | collective-permute-start | bytes 270344 | tf_op jit(solution)/shard_map/ppermute | solution.py:65
  19.9 0.0 copy-start.2
  19.9 0.0 collective-permute-done.3.rest_3_
  19.9 0.0 collective-permute-done.4.rest_4_
  20.0 0.0 collective-permute-done.5.rest_5_
  20.0 0.0 collective-permute-done.6.rest_6_
  20.0 0.0 collective-permute-done.7.rest_7_
  20.0 0.6 %copy-done.2 = s32[1,1,16,8]{2,3,1,0:T(8,128)S(1)} copy-done((s32[1,1,16,8]{2,3,1,0:T(8,128)S(1)}, s32[1,1,16,8]{2,3,1,0:T(8,128)}, u32[]{:S(2)}) %copy-start.2) | copy-done | bytes 536
  20.6 1.2 %first_step.1 = (f32[4,16,16,256]{3,2,1,0:T(8,128)S(1)}, bf16[32,32,128]{2,1,0:T(8,128)(2,1)}) custom-call(s32[8,16]{1,0:T(8,128)S(1)} %bitcast.14, f32[4,16,16,256]{3,2,1,0:T(8,128)S(1)} %inner_step_late.1.inner, f32[4,16,16,256]{3,2,1,0:T(8,128)S(1)} %get-tuple-element.22.q, ...), custom_call_target="tpu_custom_call", output_to_operand_aliasing={{0}: (1, {})} | custom-call | tf_op jit(solution)/shard_map/first_step/pallas_call | solution.py:593
  21.7 0.0 copy-start.3
  21.7 10.4 %all-to-all-start = ((bf16[32,32,128]{2,1,0:T(8,128)(2,1)}), bf16[32,32,128]{2,1,0:T(8,128)(2,1)S(1)}, u32[]{:S(2)}, u32[]{:S(2)}) async-start(bf16[32,32,128]{2,1,0:T(8,128)(2,1)} %get-tuple-element.35), calls=%async_computation | async-start | bytes 524288 | tf_op jit(solution)/shard_map/all_to_all | solution.py:603
  32.1 0.0 copy-done.3
  32.1 0.1 copy.11
  32.2 0.1 reshape.3.targets
  32.3 0.0 copy-start
  32.3 3.5 %second_step.1 = (f32[4,16,16,256]{3,2,1,0:T(8,128)S(1)}, f32[2,2,8,256]{3,2,1,0:T(8,128)S(1)}) custom-call(f32[4,16,16,256]{3,2,1,0:T(8,128)S(1)} %get-tuple-element.36.stepped, f32[4,16,16,256]{3,2,1,0:T(8,128)} %bitcast.16, f32[3,16,16,256]{3,2,1,0:T(8,128)} %bitcast.18, bf16[11,16,256]{2,1,0:T(8,128)(2,1)S(1)} %collective-permute-done.rest_0_, ...), custom_call_target="tpu_custom_call" | custom-call | tf_op jit(solution)/shard_map/second_step/pallas_call | solution.py:604
  35.8 0.0 copy-start.1
  35.8 9.7 %all-to-all-done.received = bf16[32,32,128]{2,1,0:T(8,128)(2,1)S(1)} async-done(((bf16[32,32,128]{2,1,0:T(8,128)(2,1)}), bf16[32,32,128]{2,1,0:T(8,128)(2,1)S(1)}, u32[]{:S(2)}, u32[]{:S(2)}) %all-to-all-start) | async-done | bytes 262176 | tf_op jit(solution)/shard_map/all_to_all | solution.py:603
  45.5 0.0 copy-done
  45.5 0.0 copy-done.1
  45.5 1.0 %add_source.1 = f32[4,16,16,256]{3,2,1,0:T(8,128)} custom-call(s32[1,128]{1,0:T(1,128)S(1)} %reshape.3.targets, s32[8,16]{1,0:T(8,128)S(1)} %bitcast.13, bf16[32,32,128]{2,1,0:T(8,128)(2,1)S(1)} %all-to-all-done.received, bf16[8,128,128]{2,1,0:T(8,128)(2,1)S(1)} %bitcast.12, f32[4,16,16,256]{3,2,1,0:T(8,128)S(1)} %get-tuple-element.37.base, ...), custom_call_target="tpu_custom_call" | custom-call | tf_op jit(solution)/shard_map/add_source/pallas_call | solution.py:619
  (1 shorter events, 0.0 us)
Async XLA Ops:
  2.0 15.8 %collective-permute-start.1 = (bf16[11,16,256]{2,1,0:T(8,128)(2,1)S(1)}, bf16[11,16,256]{2,1,0:T(8,128)(2,1)S(1)}, u32[]{:S(2)}, u32[]{:S(2)}) collective-permute-start(bf16[11,16,256]{2,1,0:T(8,128)(2,1)S(1)} %get-tuple-element.32), channel_id=1, source_target_pairs={{0,1},{1,0},{2,3},{3,2},{4,5},{5,4},{8,9},{9,8},{10,11},{11,10},{1... | collective-permute-start | bytes 270344 | tf_op jit(solution)/shard_map/ppermute | solution.py:43
  6.9 11.6 %collective-permute-start = (bf16[11,16,256]{2,1,0:T(8,128)(2,1)S(1)}, bf16[11,16,256]{2,1,0:T(8,128)(2,1)S(1)}, u32[]{:S(2)}, u32[]{:S(2)}) collective-permute-start(bf16[11,16,256]{2,1,0:T(8,128)(2,1)S(1)} %get-tuple-element.28), channel_id=1, source_target_pairs={{7,8},{15,0},{23,24},{31,16},{39,40},{47,32},{55,56},{63,48},{71,7... | collective-permute-start | bytes 270344 | tf_op jit(solution)/shard_map/ppermute | solution.py:43
  8.2 11.0 %collective-permute-start.2 = (bf16[11,16,256]{2,1,0:T(8,128)(2,1)S(1)}, bf16[11,16,256]{2,1,0:T(8,128)(2,1)S(1)}, u32[]{:S(2)}, u32[]{:S(2)}) collective-permute-start(bf16[11,16,256]{2,1,0:T(8,128)(2,1)S(1)} %get-tuple-element.33), channel_id=1, source_target_pairs={{16,32},{32,16},{17,33},{33,17},{19,35},{35,19},{24,40},{40,24},{2... | collective-permute-start | bytes 270344 | tf_op jit(solution)/shard_map/ppermute | solution.py:65
  12.2 7.7 %collective-permute-start.3 = (bf16[11,16,256]{2,1,0:T(8,128)(2,1)S(1)}, bf16[11,16,256]{2,1,0:T(8,128)(2,1)S(1)}, u32[]{:S(2)}, u32[]{:S(2)}) collective-permute-start(bf16[11,16,256]{2,1,0:T(8,128)(2,1)S(1)} %get-tuple-element.34), channel_id=1, source_target_pairs={{0,16},{16,0},{8,24},{24,8},{32,48},{48,32},{40,56},{56,40},{64,80... | collective-permute-start | bytes 270344 | tf_op jit(solution)/shard_map/ppermute | solution.py:65
  16.4 3.6 %collective-permute-start.4 = (bf16[11,16,256]{2,1,0:T(8,128)(2,1)S(1)}, bf16[11,16,256]{2,1,0:T(8,128)(2,1)S(1)}, u32[]{:S(2)}, u32[]{:S(2)}) collective-permute-start(bf16[11,16,256]{2,1,0:T(8,128)(2,1)S(1)} %get-tuple-element.28), channel_id=1, source_target_pairs={{1,2},{2,1},{3,4},{4,3},{5,6},{6,5},{8,7},{9,10},{10,9},{11,12},{1... | collective-permute-start | bytes 270344 | tf_op jit(solution)/shard_map/ppermute | solution.py:43
  17.8 2.1 %collective-permute-start.5 = (bf16[11,16,256]{2,1,0:T(8,128)(2,1)S(1)}, bf16[11,16,256]{2,1,0:T(8,128)(2,1)S(1)}, u32[]{:S(2)}, u32[]{:S(2)}) collective-permute-start(bf16[11,16,256]{2,1,0:T(8,128)(2,1)S(1)} %get-tuple-element.32), channel_id=1, source_target_pairs={{6,7},{7,6},{14,15},{15,14},{22,23},{23,22},{30,31},{31,30},{38,39... | collective-permute-start | bytes 270344 | tf_op jit(solution)/shard_map/ppermute | solution.py:43
  18.5 1.4 %collective-permute-start.6 = (bf16[11,16,256]{2,1,0:T(8,128)(2,1)S(1)}, bf16[11,16,256]{2,1,0:T(8,128)(2,1)S(1)}, u32[]{:S(2)}, u32[]{:S(2)}) collective-permute-start(bf16[11,16,256]{2,1,0:T(8,128)(2,1)S(1)} %get-tuple-element.33), channel_id=1, source_target_pairs={{18,34},{34,18},{20,36},{36,20},{21,37},{37,21},{22,38},{38,22},{2... | collective-permute-start | bytes 270344 | tf_op jit(solution)/shard_map/ppermute | solution.py:65
  19.2 0.8 %collective-permute-start.7 = (bf16[11,16,256]{2,1,0:T(8,128)(2,1)S(1)}, bf16[11,16,256]{2,1,0:T(8,128)(2,1)S(1)}, u32[]{:S(2)}, u32[]{:S(2)}) collective-permute-start(bf16[11,16,256]{2,1,0:T(8,128)(2,1)S(1)} %get-tuple-element.34), channel_id=1, source_target_pairs={{1,17},{17,1},{2,18},{18,2},{3,19},{19,3},{4,20},{20,4},{5,21},{21... | collective-permute-start | bytes 270344 | tf_op jit(solution)/shard_map/ppermute | solution.py:65
  19.9 0.7 %copy-start.2 = (s32[1,1,16,8]{2,3,1,0:T(8,128)S(1)}, s32[1,1,16,8]{2,3,1,0:T(8,128)}, u32[]{:S(2)}) copy-start(s32[1,1,16,8]{2,3,1,0:T(8,128)} %param.11) | copy-start | bytes 1540
  21.7 10.4 %copy-start.3 = (s32[1,1,16,8]{2,3,1,0:T(8,128)S(1)}, s32[1,1,16,8]{2,3,1,0:T(8,128)}, u32[]{:S(2)}) copy-start(s32[1,1,16,8]{2,3,1,0:T(8,128)} %param.12) | copy-start | bytes 1540
  21.7 23.8 %all-to-all-start = ((bf16[32,32,128]{2,1,0:T(8,128)(2,1)}), bf16[32,32,128]{2,1,0:T(8,128)(2,1)S(1)}, u32[]{:S(2)}, u32[]{:S(2)}) async-start(bf16[32,32,128]{2,1,0:T(8,128)(2,1)} %get-tuple-element.35), calls=%async_computation | async-start | bytes 524288 | tf_op jit(solution)/shard_map/all_to_all | solution.py:603
  32.3 13.3 %copy-start = (bf16[1,1,8,128,128]{4,3,2,1,0:T(8,128)(2,1)S(1)}, bf16[1,1,8,128,128]{4,3,2,1,0:T(8,128)(2,1)}, u32[]{:S(2)}) copy-start(bf16[1,1,8,128,128]{4,3,2,1,0:T(8,128)(2,1)} %param.10) | copy-start | bytes 786436
  35.8 9.7 %copy-start.1 = (s32[1,1,16,8]{2,3,1,0:T(8,128)S(1)}, s32[1,1,16,8]{2,3,1,0:T(8,128)}, u32[]{:S(2)}) copy-start(s32[1,1,16,8]{2,3,1,0:T(8,128)} %param.13) | copy-start | bytes 1540

commit v8 on v7

--- a/solution.py
+++ b/solution.py
@@ -152,8 +152,8 @@
     return ref[component, :, j, :]
 
 
-def pack_halos(q, c, s, *rest):
-    *outs, cells, factors, source, done = rest
+def pack_halos(q, c, s, ids, *rest):
+    *outs, cells, factors, source, listed, done, held = rest
     sector_first, sector_second, slab_first, slab_second = outs
     sector_up = upper_first("az")
     slab_up = upper_first("ax")
@@ -164,6 +164,7 @@
         parts.append((c.at[k], factors.at[k]))
     for v in range(NV):
         parts.append((s.at[v], source.at[v]))
+    parts.append((ids, listed))
     copies = [pltpu.make_async_copy(*part, done.at[n]) for n, part in enumerate(parts)]
     for copy in copies:
         copy.start()
@@ -200,27 +201,33 @@
         factor.append(planes[k])
         for n in range(3):
             out[COEF + n] = planes[n].astype(BF16)
+    def beyond(n, acoustic):
+        upper, k = plans[n][2:]
+        sign = jnp.where(upper, 1.0, -1.0)
+        return border_terms(acoustic, far[n], near[n][k], factor[n], k, sign)
+
+    section = lax.axis_index("sec")
+
+    @pl.when(section == 0)
+    def _():
+        for n, plan in enumerate(plans):
+            for v, term in enumerate(beyond(n, False)):
+                plan[0][BEYOND + v] = term.astype(BF16)
+
+    @pl.when(section != 0)
+    def _():
+        for n in range(len(plans)):
+            for v, term in enumerate(beyond(n, True)):
+                held[n, v] = term
+
     for copy in copies[NV + 3 :]:
         copy.wait()
 
-    def beyond(acoustic):
+    @pl.when(section != 0)
+    def _():
         for n, (out, take, upper, k) in enumerate(plans):
-            sign = jnp.where(upper, 1.0, -1.0)
-            terms = border_terms(acoustic, far[n], near[n][k], factor[n], k, sign)
             for v in range(NV):
-                if acoustic:
-                    terms[v] += 0.25 * take(source, v, 0, upper)
-                out[BEYOND + v] = terms[v].astype(BF16)
-
-    section = lax.axis_index("sec")
-
-    @pl.when(section == 0)
-    def _():
-        beyond(False)
-
-    @pl.when(section != 0)
-    def _():
-        beyond(True)
+                out[BEYOND + v] = (held[n, v] + 0.25 * take(source, v, 0, upper)).astype(BF16)
 
 
 def fields_of(message, start, count=NV):
@@ -551,15 +558,25 @@
     field = jax.ShapeDtypeStruct((NV, C1, C2, C3), F32)
     cells = pltpu.VMEM((NV, C1, C2, C3), F32)
 
-    *sends, kept, kept_factors, kept_source = pl.pallas_call(
+    *sends, kept, kept_factors, kept_source, listed = pl.pallas_call(
         pack_halos,
-        in_specs=[ANY] * 3,
-        out_specs=[VMEM] * 7,
-        out_shape=[message] * 4 + [cells, pltpu.VMEM((3, C1, C2, C3), F32), cells],
-        scratch_shapes=[pltpu.SemaphoreType.DMA((2 * NV + 3,))],
+        in_specs=[ANY] * 4,
+        out_specs=[VMEM] * 8,
+        out_shape=[message] * 4
+        + [cells, pltpu.VMEM((3, C1, C2, C3), F32), cells]
+        + [pltpu.VMEM((CAP, lax.axis_size("ax")), jnp.int32)],
+        scratch_shapes=[
+            pltpu.SemaphoreType.DMA((2 * NV + 4,)),
+            pltpu.VMEM((4, NV, C1, C3), F32),
+        ],
         compiler_params=PARAMS,
         name="pack_halos",
-    )(off_chip(current), off_chip(factors), off_chip(old_source))
+    )(
+        off_chip(current),
+        off_chip(factors),
+        off_chip(old_source),
+        off_chip(send_ids[0, 0].T),
+    )
     last = lax.axis_size("az") // 2 - 1
     wrapped = shift_sectors(sends[1], [(last, last + 1)])
     sector_first = shift_sectors(sends[0], both_ways(range(0, last - 1, 2)))
@@ -599,7 +616,7 @@
         scratch_shapes=[pltpu.VMEM((2, NV, C1, C3), F32)] * 2,
         compiler_params=PARAMS,
         name="first_step",
-    )(send_ids[0, 0].T, inner, kept, kept_factors, *messages)
+    )(listed, inner, kept, kept_factors, *messages)
     received = lax.all_to_all(packed, ("sec", "ax"), split_axis=0, concat_axis=0, tiled=True)
     base, paths = pl.pallas_call(
         second_step,

time: 47 us -> 46.6 us (level)
  local copies, waits for them, and re-layouts: 0.77 us -> 0.18 us
    unnamed x9 -> x7, local copies, waits for them, and re-layouts: 0.68 us -> 0.09 us
where the time goes in v8:
time: 46.6 us; the launch traced here: 45.8 us
  starting transfers between devices  26.4 us (57%)
  waiting for transfers between devices  9.71 us (21%)
  Pallas kernels  9.25 us (20%)
    all_to_all x1, starting transfers between devices, shards(): lax.all_to_all(packed, ('sec', 'ax'), split_axis=0, concat_axis=0, tiled=...  10.3 us
    all_to_all x1, waiting for transfers between devices, shards(): lax.all_to_all(packed, ('sec', 'ax'), split_axis=0, concat_axis=0, tiled=...  9.69 us
    ppermute x4, starting transfers between devices, shift_sectors(): return lax.ppermute(x, 'az', pairs)  8.24 us
    ppermute x4, starting transfers between devices, swap_slabs(): return lax.ppermute(x, ('sec', 'ax', 'az'), pairs)  7.88 us
    pallas_call x1, Pallas kernels, shards(): pl.pallas_call(second_step, in_specs=[VMEM] * 11, out_specs=[VMEM] * 2, o...  3.52 us
    pallas_call x1, Pallas kernels, shards(): pl.pallas_call(pack_halos, in_specs=[ANY] * 4, out_specs=[VMEM] * 8, out_...  1.9 us
    pallas_call x1, Pallas kernels, shards(): pl.pallas_call(functools.partial(inner_step, True), in_specs=[VMEM] * 3,...  1.62 us
    pallas_call x1, Pallas kernels, shards(): pl.pallas_call(first_step, in_specs=[VMEM] * 12, out_specs=[VMEM] * 2, ou...  1.16 us
  transfers between devices with their start and end apart: 9, of which 1 were waited for; matrix products, arithmetic and copies ran while one was open for 0% of the time, Pallas kernels for 11%

profile of v8, /device:TPU:1, one launch (start us, length us, event | category | flops | bytes accessed | tf_op | source)
XLA Modules:
  0.0 45.8 jit_solution(12585028206678888931)
XLA Ops:
  0.0 1.9 %pack_halos.1 = (bf16[11,16,256]{2,1,0:T(8,128)(2,1)S(1)}, bf16[11,16,256]{2,1,0:T(8,128)(2,1)S(1)}, bf16[11,16,256]{2,1,0:T(8,128)(2,1)S(1)}, bf16[11,16,256]{2...) custom-call(f32[4,16,16,256]{3,2,1,0:T(8,128)} %bitcast.14, ...), custom_call_target="tpu_custom_call" | custom-call | tf_op jit(solution)/shard_map/pack_halos/pallas_call | solution.py:561
  1.9 4.8 %collective-permute-start.1 = (bf16[11,16,256]{2,1,0:T(8,128)(2,1)S(1)}, bf16[11,16,256]{2,1,0:T(8,128)(2,1)S(1)}, u32[]{:S(2)}, u32[]{:S(2)}) collective-permute-start(bf16[11,16,256]{2,1,0:T(8,128)(2,1)S(1)} %get-tuple-element.34), channel_id=1, source_target_pairs={{0,1},{1,0},{2,3},{3,2},{4,5},{5,4},{8,9},{9,8},{10,11},{11,10},{1... | collective-permute-start | bytes 270344 | tf_op jit(solution)/shard_map/ppermute | solution.py:43
  6.7 1.3 %collective-permute-start = (bf16[11,16,256]{2,1,0:T(8,128)(2,1)S(1)}, bf16[11,16,256]{2,1,0:T(8,128)(2,1)S(1)}, u32[]{:S(2)}, u32[]{:S(2)}) collective-permute-start(bf16[11,16,256]{2,1,0:T(8,128)(2,1)S(1)} %get-tuple-element.30), channel_id=1, source_target_pairs={{7,8},{15,0},{23,24},{31,16},{39,40},{47,32},{55,56},{63,48},{71,7... | collective-permute-start | bytes 270344 | tf_op jit(solution)/shard_map/ppermute | solution.py:43
  8.0 4.0 %collective-permute-start.2 = (bf16[11,16,256]{2,1,0:T(8,128)(2,1)S(1)}, bf16[11,16,256]{2,1,0:T(8,128)(2,1)S(1)}, u32[]{:S(2)}, u32[]{:S(2)}) collective-permute-start(bf16[11,16,256]{2,1,0:T(8,128)(2,1)S(1)} %get-tuple-element.35), channel_id=1, source_target_pairs={{16,32},{32,16},{17,33},{33,17},{19,35},{35,19},{24,40},{40,24},{2... | collective-permute-start | bytes 270344 | tf_op jit(solution)/shard_map/ppermute | solution.py:65
  12.1 2.5 %collective-permute-start.3 = (bf16[11,16,256]{2,1,0:T(8,128)(2,1)S(1)}, bf16[11,16,256]{2,1,0:T(8,128)(2,1)S(1)}, u32[]{:S(2)}, u32[]{:S(2)}) collective-permute-start(bf16[11,16,256]{2,1,0:T(8,128)(2,1)S(1)} %get-tuple-element.36), channel_id=1, source_target_pairs={{0,16},{16,0},{8,24},{24,8},{32,48},{48,32},{40,56},{56,40},{64,80... | collective-permute-start | bytes 270344 | tf_op jit(solution)/shard_map/ppermute | solution.py:65
  14.6 1.6 %inner_step_early.1.rest_0_ = f32[4,16,16,256]{3,2,1,0:T(8,128)S(1)} custom-call(f32[4,16,16,256]{3,2,1,0:T(8,128)S(1)} %get-tuple-element.24.q, f32[3,16,16,256]{3,2,1,0:T(8,128)S(1)} %get-tuple-element.25.c, f32[4,16,16,256]{3,2,1,0:T(8,128)S(1)} %get-tuple-element.26.s), custom_call_target="tpu_custom_call" | custom-call | tf_op jit(solution)/shard_map/inner_step_early/pallas_call | solution.py:585
  16.2 1.5 %collective-permute-start.4 = (bf16[11,16,256]{2,1,0:T(8,128)(2,1)S(1)}, bf16[11,16,256]{2,1,0:T(8,128)(2,1)S(1)}, u32[]{:S(2)}, u32[]{:S(2)}) collective-permute-start(bf16[11,16,256]{2,1,0:T(8,128)(2,1)S(1)} %get-tuple-element.30), channel_id=1, source_target_pairs={{1,2},{2,1},{3,4},{4,3},{5,6},{6,5},{8,7},{9,10},{10,9},{11,12},{1... | collective-permute-start | bytes 270344 | tf_op jit(solution)/shard_map/ppermute | solution.py:43
  17.7 0.0 collective-permute-done.1.rest_1_
  17.7 0.7 %collective-permute-start.5 = (bf16[11,16,256]{2,1,0:T(8,128)(2,1)S(1)}, bf16[11,16,256]{2,1,0:T(8,128)(2,1)S(1)}, u32[]{:S(2)}, u32[]{:S(2)}) collective-permute-start(bf16[11,16,256]{2,1,0:T(8,128)(2,1)S(1)} %get-tuple-element.34), channel_id=1, source_target_pairs={{6,7},{7,6},{14,15},{15,14},{22,23},{23,22},{30,31},{31,30},{38,39... | collective-permute-start | bytes 270344 | tf_op jit(solution)/shard_map/ppermute | solution.py:43
  18.4 0.0 collective-permute-done.rest_0_
  18.4 0.7 %collective-permute-start.6 = (bf16[11,16,256]{2,1,0:T(8,128)(2,1)S(1)}, bf16[11,16,256]{2,1,0:T(8,128)(2,1)S(1)}, u32[]{:S(2)}, u32[]{:S(2)}) collective-permute-start(bf16[11,16,256]{2,1,0:T(8,128)(2,1)S(1)} %get-tuple-element.35), channel_id=1, source_target_pairs={{18,34},{34,18},{20,36},{36,20},{21,37},{37,21},{22,38},{38,22},{2... | collective-permute-start | bytes 270344 | tf_op jit(solution)/shard_map/ppermute | solution.py:65
  19.1 0.0 collective-permute-done.2.rest_2_
  19.1 0.7 %collective-permute-start.7 = (bf16[11,16,256]{2,1,0:T(8,128)(2,1)S(1)}, bf16[11,16,256]{2,1,0:T(8,128)(2,1)S(1)}, u32[]{:S(2)}, u32[]{:S(2)}) collective-permute-start(bf16[11,16,256]{2,1,0:T(8,128)(2,1)S(1)} %get-tuple-element.36), channel_id=1, source_target_pairs={{1,17},{17,1},{2,18},{18,2},{3,19},{19,3},{4,20},{20,4},{5,21},{21... | collective-permute-start | bytes 270344 | tf_op jit(solution)/shard_map/ppermute | solution.py:65
  19.8 0.0 collective-permute-done.3.rest_3_
  19.8 0.0 collective-permute-done.4.rest_4_
  19.8 0.0 collective-permute-done.5.rest_5_
  19.8 0.0 collective-permute-done.6.rest_6_
  19.8 0.0 collective-permute-done.7.rest_7_
  19.8 1.2 %first_step.1 = (f32[4,16,16,256]{3,2,1,0:T(8,128)S(1)}, bf16[32,32,128]{2,1,0:T(8,128)(2,1)}) custom-call(s32[8,16]{1,0:T(8,128)S(1)} %get-tuple-element.23.ids, f32[4,16,16,256]{3,2,1,0:T(8,128)S(1)} %inner_step_late.1.inner, f32[4,16,16,256]{3,2,1,0:T(8,128)S(1)} %get-tuple-element.24.q, ...), custom_call_target="tpu_custom_call", output_to_operand_aliasing={{0}: (1, {})} | custom-call | tf_op jit(solution)/shard_map/first_step/pallas_call | solution.py:610
  21.0 0.0 copy-start.2
  21.0 10.3 %all-to-all-start = ((bf16[32,32,128]{2,1,0:T(8,128)(2,1)}), bf16[32,32,128]{2,1,0:T(8,128)(2,1)S(1)}, u32[]{:S(2)}, u32[]{:S(2)}) async-start(bf16[32,32,128]{2,1,0:T(8,128)(2,1)} %get-tuple-element.37), calls=%async_computation | async-start | bytes 524288 | tf_op jit(solution)/shard_map/all_to_all | solution.py:620
  31.3 0.0 copy-done.2
  31.3 0.1 copy.11
  31.4 0.1 reshape.3.targets
  31.5 0.0 copy-start
  31.5 3.5 %second_step.1 = (f32[4,16,16,256]{3,2,1,0:T(8,128)S(1)}, f32[2,2,8,256]{3,2,1,0:T(8,128)S(1)}) custom-call(f32[4,16,16,256]{3,2,1,0:T(8,128)S(1)} %get-tuple-element.38.stepped, f32[4,16,16,256]{3,2,1,0:T(8,128)} %bitcast.15, f32[3,16,16,256]{3,2,1,0:T(8,128)} %bitcast.17, bf16[11,16,256]{2,1,0:T(8,128)(2,1)S(1)} %collective-permute-done.rest_0_, ...), custom_call_target="tpu_custom_call" | custom-call | tf_op jit(solution)/shard_map/second_step/pallas_call | solution.py:621
  35.0 0.0 copy-start.1
  35.1 9.7 %all-to-all-done.received = bf16[32,32,128]{2,1,0:T(8,128)(2,1)S(1)} async-done(((bf16[32,32,128]{2,1,0:T(8,128)(2,1)}), bf16[32,32,128]{2,1,0:T(8,128)(2,1)S(1)}, u32[]{:S(2)}, u32[]{:S(2)}) %all-to-all-start) | async-done | bytes 262176 | tf_op jit(solution)/shard_map/all_to_all | solution.py:620
  44.7 0.0 copy-done
  44.8 0.0 copy-done.1
  44.8 1.0 %add_source.1 = f32[4,16,16,256]{3,2,1,0:T(8,128)} custom-call(s32[1,128]{1,0:T(1,128)S(1)} %reshape.3.targets, s32[8,16]{1,0:T(8,128)S(1)} %bitcast.13, bf16[32,32,128]{2,1,0:T(8,128)(2,1)S(1)} %all-to-all-done.received, bf16[8,128,128]{2,1,0:T(8,128)(2,1)S(1)} %bitcast.12, f32[4,16,16,256]{3,2,1,0:T(8,128)S(1)} %get-tuple-element.39.base, ...), custom_call_target="tpu_custom_call" | custom-call | tf_op jit(solution)/shard_map/add_source/pallas_call | solution.py:636
  (1 shorter events, 0.0 us)
Async XLA Ops:
  1.9 15.8 %collective-permute-start.1 = (bf16[11,16,256]{2,1,0:T(8,128)(2,1)S(1)}, bf16[11,16,256]{2,1,0:T(8,128)(2,1)S(1)}, u32[]{:S(2)}, u32[]{:S(2)}) collective-permute-start(bf16[11,16,256]{2,1,0:T(8,128)(2,1)S(1)} %get-tuple-element.34), channel_id=1, source_target_pairs={{0,1},{1,0},{2,3},{3,2},{4,5},{5,4},{8,9},{9,8},{10,11},{11,10},{1... | collective-permute-start | bytes 270344 | tf_op jit(solution)/shard_map/ppermute | solution.py:43
  6.7 11.6 %collective-permute-start = (bf16[11,16,256]{2,1,0:T(8,128)(2,1)S(1)}, bf16[11,16,256]{2,1,0:T(8,128)(2,1)S(1)}, u32[]{:S(2)}, u32[]{:S(2)}) collective-permute-start(bf16[11,16,256]{2,1,0:T(8,128)(2,1)S(1)} %get-tuple-element.30), channel_id=1, source_target_pairs={{7,8},{15,0},{23,24},{31,16},{39,40},{47,32},{55,56},{63,48},{71,7... | collective-permute-start | bytes 270344 | tf_op jit(solution)/shard_map/ppermute | solution.py:43
  8.0 11.0 %collective-permute-start.2 = (bf16[11,16,256]{2,1,0:T(8,128)(2,1)S(1)}, bf16[11,16,256]{2,1,0:T(8,128)(2,1)S(1)}, u32[]{:S(2)}, u32[]{:S(2)}) collective-permute-start(bf16[11,16,256]{2,1,0:T(8,128)(2,1)S(1)} %get-tuple-element.35), channel_id=1, source_target_pairs={{16,32},{32,16},{17,33},{33,17},{19,35},{35,19},{24,40},{40,24},{2... | collective-permute-start | bytes 270344 | tf_op jit(solution)/shard_map/ppermute | solution.py:65
  12.1 7.7 %collective-permute-start.3 = (bf16[11,16,256]{2,1,0:T(8,128)(2,1)S(1)}, bf16[11,16,256]{2,1,0:T(8,128)(2,1)S(1)}, u32[]{:S(2)}, u32[]{:S(2)}) collective-permute-start(bf16[11,16,256]{2,1,0:T(8,128)(2,1)S(1)} %get-tuple-element.36), channel_id=1, source_target_pairs={{0,16},{16,0},{8,24},{24,8},{32,48},{48,32},{40,56},{56,40},{64,80... | collective-permute-start | bytes 270344 | tf_op jit(solution)/shard_map/ppermute | solution.py:65
  16.2 3.6 %collective-permute-start.4 = (bf16[11,16,256]{2,1,0:T(8,128)(2,1)S(1)}, bf16[11,16,256]{2,1,0:T(8,128)(2,1)S(1)}, u32[]{:S(2)}, u32[]{:S(2)}) collective-permute-start(bf16[11,16,256]{2,1,0:T(8,128)(2,1)S(1)} %get-tuple-element.30), channel_id=1, source_target_pairs={{1,2},{2,1},{3,4},{4,3},{5,6},{6,5},{8,7},{9,10},{10,9},{11,12},{1... | collective-permute-start | bytes 270344 | tf_op jit(solution)/shard_map/ppermute | solution.py:43
  17.7 2.1 %collective-permute-start.5 = (bf16[11,16,256]{2,1,0:T(8,128)(2,1)S(1)}, bf16[11,16,256]{2,1,0:T(8,128)(2,1)S(1)}, u32[]{:S(2)}, u32[]{:S(2)}) collective-permute-start(bf16[11,16,256]{2,1,0:T(8,128)(2,1)S(1)} %get-tuple-element.34), channel_id=1, source_target_pairs={{6,7},{7,6},{14,15},{15,14},{22,23},{23,22},{30,31},{31,30},{38,39... | collective-permute-start | bytes 270344 | tf_op jit(solution)/shard_map/ppermute | solution.py:43
  18.4 1.4 %collective-permute-start.6 = (bf16[11,16,256]{2,1,0:T(8,128)(2,1)S(1)}, bf16[11,16,256]{2,1,0:T(8,128)(2,1)S(1)}, u32[]{:S(2)}, u32[]{:S(2)}) collective-permute-start(bf16[11,16,256]{2,1,0:T(8,128)(2,1)S(1)} %get-tuple-element.35), channel_id=1, source_target_pairs={{18,34},{34,18},{20,36},{36,20},{21,37},{37,21},{22,38},{38,22},{2... | collective-permute-start | bytes 270344 | tf_op jit(solution)/shard_map/ppermute | solution.py:65
  19.1 0.8 %collective-permute-start.7 = (bf16[11,16,256]{2,1,0:T(8,128)(2,1)S(1)}, bf16[11,16,256]{2,1,0:T(8,128)(2,1)S(1)}, u32[]{:S(2)}, u32[]{:S(2)}) collective-permute-start(bf16[11,16,256]{2,1,0:T(8,128)(2,1)S(1)} %get-tuple-element.36), channel_id=1, source_target_pairs={{1,17},{17,1},{2,18},{18,2},{3,19},{19,3},{4,20},{20,4},{5,21},{21... | collective-permute-start | bytes 270344 | tf_op jit(solution)/shard_map/ppermute | solution.py:65
  21.0 10.3 %copy-start.2 = (s32[1,1,16,8]{2,3,1,0:T(8,128)S(1)}, s32[1,1,16,8]{2,3,1,0:T(8,128)}, u32[]{:S(2)}) copy-start(s32[1,1,16,8]{2,3,1,0:T(8,128)} %param.12) | copy-start | bytes 1540
  21.0 23.7 %all-to-all-start = ((bf16[32,32,128]{2,1,0:T(8,128)(2,1)}), bf16[32,32,128]{2,1,0:T(8,128)(2,1)S(1)}, u32[]{:S(2)}, u32[]{:S(2)}) async-start(bf16[32,32,128]{2,1,0:T(8,128)(2,1)} %get-tuple-element.37), calls=%async_computation | async-start | bytes 524288 | tf_op jit(solution)/shard_map/all_to_all | solution.py:620
  31.5 13.3 %copy-start = (bf16[1,1,8,128,128]{4,3,2,1,0:T(8,128)(2,1)S(1)}, bf16[1,1,8,128,128]{4,3,2,1,0:T(8,128)(2,1)}, u32[]{:S(2)}) copy-start(bf16[1,1,8,128,128]{4,3,2,1,0:T(8,128)(2,1)} %param.10) | copy-start | bytes 786436
  35.0 9.7 %copy-start.1 = (s32[1,1,16,8]{2,3,1,0:T(8,128)S(1)}, s32[1,1,16,8]{2,3,1,0:T(8,128)}, u32[]{:S(2)}) copy-start(s32[1,1,16,8]{2,3,1,0:T(8,128)} %param.13) | copy-start | bytes 1540
